TPU v7x, 32 devices: a whole 2x2x4 slice. The times are simulated.
32 devices in a mesh: sec: 2 (over x), lat: 16 (over z, y, core).
Axes of the slice: x: 2, y: 2, z: 4, core: 2. Of those that a mesh axis runs over, the one named last changes fastest.
Arguments:
- resid_in: bfloat16 [4, 128, 2048], P('sec', None, 'lat'), may hold values from -6 to 6
- mlp_out: bfloat16 [4, 128, 2048], P('sec', None, 'lat'), may hold values from -6 to 6
- enc_weight: bfloat16 [4, 2048, 1024], P('sec', None, 'lat'), may hold values from -0.125 to 0.125
- enc_bias: float32 [4, 1024], P('sec', 'lat'), may hold values from -3 to 3
- thresholds: int32 [4, 1024], P('sec', 'lat'), may hold values from 0 to 3
- same_dec: bfloat16 [4, 1024, 2048], P('sec', 'lat'), may hold values from -0.1875 to 0.1875
- next_dec: bfloat16 [2, 1024, 2048], P('sec', 'lat'), may hold values from -0.1875 to 0.1875
- cross_dec: bfloat16 [2, 2, 1024, 2048], P('sec', None, 'lat'), may hold values from -0.1875 to 0.1875
Outputs:
- mean_square: float32 [], replicated
- grad_enc: bfloat16 [4, 2048, 1024], P('sec', None, 'lat')
- grad_bias: float32 [4, 1024], P('sec', 'lat')
- grad_same: bfloat16 [4, 1024, 2048], P('sec', 'lat')
- grad_next: bfloat16 [2, 1024, 2048], P('sec', 'lat')
- grad_cross: bfloat16 [2, 2, 1024, 2048], P('sec', None, 'lat')
All inputs are finite; a program needn't handle non-finite values.
Results may differ from a plain program's by a relative error of at most 0.0059.
Values may be sent and summed in bfloat16 or wider, within the bound.
No kernel may reach another device: no remote copies, remote signals or barrier semaphores. Data moves between devices by JAX's collectives and lax.ppermute only.
A program may use at most 64 MiB of HBM per device.

v0:
```python
import jax
import jax.numpy as jnp
from jax import lax
from jax.sharding import PartitionSpec as P

D = 2048
TOKENS = 128


jump_width = 0.1


def shifted(value, axis, steps):
    count = lax.axis_size(axis)
    first, last = (max(0, -steps), min(count, count - steps))
    return lax.ppermute(value, axis, [(source, source + steps) for source in range(first, last)])


def back_dot(grad, weights):
    return lax.dot_general(
        grad, weights, (((1,), (1,)), ((), ())), preferred_element_type=jnp.float32
    )


def outer_dot(act, grad):
    return lax.dot_general(act, grad, (((0,), (0,)), ((), ())), preferred_element_type=jnp.float32)


def per_device(resid_in, mlp_out, enc_weight, enc_bias, thresholds, same_dec, next_dec, cross_dec):
    leading = lax.axis_index("sec") == 0
    inputs_full = lax.all_gather(resid_in, "lat", axis=2, tiled=True)
    pre_act = (
        jnp.einsum("ktd,kdc->ktc", inputs_full, enc_weight, preferred_element_type=jnp.float32)
        + enc_bias[:, None, :]
    )
    cut_level = 0.25 * thresholds.astype(jnp.float32)[:, None, :]
    gate_value = jax.nn.sigmoid((pre_act - cut_level) / jump_width)
    latent_act = (pre_act * gate_value).astype(jnp.bfloat16)
    rebuilt_first = jnp.dot(latent_act[0], same_dec[0], preferred_element_type=jnp.float32)
    rebuilt_second = jnp.dot(
        latent_act[1], same_dec[1], preferred_element_type=jnp.float32
    ) + jnp.dot(latent_act[0], next_dec[0], preferred_element_type=jnp.float32)
    far_weight = shifted(cross_dec, "sec", -1)
    source_act = jnp.where(leading, latent_act, jnp.zeros_like(latent_act))
    near_part = jnp.einsum(
        "ktc,kcd->td", source_act, cross_dec[0], preferred_element_type=jnp.float32
    )
    far_part = jnp.einsum(
        "ktc,kcd->td", source_act, far_weight[0], preferred_element_type=jnp.float32
    )
    partials = jnp.stack([rebuilt_first, rebuilt_second, near_part, far_part])
    summed = lax.psum_scatter(partials, "lat", scatter_dimension=2, tiled=True)
    crossing = shifted(summed[2:], "sec", 1)
    rebuilt = summed[:2] + crossing
    misfit = rebuilt - mlp_out.astype(jnp.float32)
    squared_total = lax.psum(jnp.sum(misfit * misfit), ("sec", "lat"))
    mean_square = squared_total / (4.0 * TOKENS * D)
    dy_rows = misfit.astype(jnp.bfloat16)
    extra_rows = shifted(dy_rows, "sec", -1)
    grad_full = lax.all_gather(
        jnp.concatenate([dy_rows, extra_rows], axis=0), "lat", axis=2, tiled=True
    )
    act_grad = jnp.stack(
        [
            back_dot(grad_full[0], same_dec[0]) + back_dot(grad_full[1], next_dec[0]),
            back_dot(grad_full[1], same_dec[1]),
        ]
    )
    cross_grad = jnp.einsum(
        "td,kcd->ktc", grad_full[2], cross_dec[0], preferred_element_type=jnp.float32
    )
    cross_grad = cross_grad + jnp.einsum(
        "td,kcd->ktc", grad_full[3], far_weight[0], preferred_element_type=jnp.float32
    )
    act_grad = act_grad + cross_grad
    gate_slope = gate_value + pre_act * gate_value * (1.0 - gate_value) / jump_width
    pre_grad = act_grad * gate_slope
    grad_bias = jnp.sum(pre_grad, axis=1)
    pre_rounded = pre_grad.astype(jnp.bfloat16)
    grad_enc = jnp.einsum(
        "ktd,ktc->kdc", inputs_full, pre_rounded, preferred_element_type=jnp.float32
    ).astype(jnp.bfloat16)
    grad_same = jnp.stack(
        [outer_dot(latent_act[0], grad_full[0]), outer_dot(latent_act[1], grad_full[1])]
    ).astype(jnp.bfloat16)
    grad_next = outer_dot(latent_act[0], grad_full[1])[None].astype(jnp.bfloat16)
    near_grad = jnp.einsum(
        "ktc,td->kcd", source_act, grad_full[2], preferred_element_type=jnp.float32
    ).astype(jnp.bfloat16)
    far_grad = jnp.einsum(
        "ktc,td->kcd", source_act, grad_full[3], preferred_element_type=jnp.float32
    ).astype(jnp.bfloat16)
    far_back = shifted(far_grad, "sec", 1)
    grad_cross = jnp.where(leading, near_grad, far_back)[None]
    return (mean_square, grad_enc, grad_bias, grad_same, grad_next, grad_cross)


def solution(mesh):
    in_specs = (
        P("sec", None, "lat"),
        P("sec", None, "lat"),
        P("sec", None, "lat"),
        P("sec", "lat"),
        P("sec", "lat"),
        P("sec", "lat", None),
        P("sec", "lat", None),
        P("sec", None, "lat", None),
    )
    out_specs = (
        P(),
        P("sec", None, "lat"),
        P("sec", "lat"),
        P("sec", "lat", None),
        P("sec", "lat", None),
        P("sec", None, "lat", None),
    )
    return jax.shard_map(
        per_device, mesh=mesh, in_specs=in_specs, out_specs=out_specs, check_vma=False
    )
```

profile of v0, /device:TPU:0, one launch (start us, length us, event | category | flops | bytes accessed | tf_op | source)
XLA Modules:
  0.0 208.9 jit_solution(15887882356919361757)
XLA Ops:
  8.0 1.3 collective-permute-start
  9.3 0.7 convert_multiply_fusion
  10.0 39.8 %all-gather.3.cloned.1.call-done = bf16[2,128,2048]{2,1,0:T(8,128)(2,1)} async-done(((bf16[2,128,128]{2,1,0:T(8,128)(2,1)}), bf16[2,128,2048]{2,1,0:T(8,128)(2,1)}) %all-gather.3.cloned.1.call-update) | async-done | bytes 1048592 | tf_op jit(solution)/shard_map/all_gather | solution.py:31
  49.7 1.7 fusion.30
  51.5 1.3 fusion.20
  54.5 2.2 %pad_maximum_fusion = f32[4,128,2048]{2,1,0:T(8,128)} fusion(f32[1,128,2048]{2,1,0:T(8,128)S(1)} %convolution_bitcast_fusion, f32[1,128,2048]{2,1,0:T(8,128)S(1)} %convolution_bitcast_fusion.1, f32[1,128,2048]{2,1,0:T(8,128)S(1)} %fusion, f32[1,128,2048]{2,1,0:T(8,128)S(1)} %convolution_bitcast_fusion.2), kind=kLoop, calls=%fused_computation | loop fusion | flops 3145728 | bytes 8388608 | tf_op jit(solution)/shard_map/stack | solution.py:51
  56.8 71.9 %reduce-scatter.2.cloned.1.call-done = f32[4,128,128]{2,1,0:T(8,128)} async-done(((f32[4,128,2048]{2,1,0:T(8,128)}), f32[4,128,128]{2,1,0:T(8,128)}) %reduce-scatter.2.cloned.1.call-update) | async-done | bytes 262160 | tf_op jit(solution)/shard_map/reduce_scatter | solution.py:52
  128.7 0.9 slice.55
  129.6 3.4 %collective-permute-start.1 = (f32[2,128,128]{2,1,0:T(8,128)S(1)}, f32[2,128,128]{2,1,0:T(8,128)S(1)}, u32[]{:S(2)}, u32[]{:S(2)}) collective-permute-start(f32[2,128,128]{2,1,0:T(8,128)S(1)} %slice.55), channel_id=1, source_target_pairs={{0,16},{1,17},{2,18},{3,19},{4,20},{5,21},{6,22},{7,23},{8,24},{9,... | collective-permute-start | bytes 393224 | tf_op jit(solution)/shard_map/ppermute | solution.py:16
  133.0 2.5 %collective-permute-done.1 = f32[2,128,128]{2,1,0:T(8,128)S(1)} collective-permute-done((f32[2,128,128]{2,1,0:T(8,128)S(1)}, f32[2,128,128]{2,1,0:T(8,128)S(1)}, u32[]{:S(2)}, u32[]{:S(2)}) %collective-permute-start.1) | collective-permute-done | bytes 131104 | tf_op jit(solution)/shard_map/ppermute | solution.py:16
  135.5 1.6 fusion.36
  137.1 1.3 collective-permute-start.2
  138.4 4.9 %collective-permute-done.2 = bf16[2,128,128]{2,1,0:T(8,128)(2,1)S(1)} collective-permute-done((bf16[2,128,128]{2,1,0:T(8,128)(2,1)S(1)}, bf16[2,128,128]{2,1,0:T(8,128)(2,1)S(1)}, u32[]{:S(2)}, u32[]{:S(2)}) %collective-permute-start.2) | collective-permute-done | bytes 65568 | tf_op jit(solution)/shard_map/ppermute | solution.py:16
  143.9 39.2 %psum.7 = f32[]{:T(128)} all-reduce(f32[]{:T(128)} %get-tuple-element.7), channel_id=1, replica_groups=mesh['sec'=2,'lat'=16] {'sec','lat'}, use_global_device_ids=true, to_apply=%region_2.3 | all-reduce | flops 1 | bytes 8 | tf_op jit(solution)/shard_map/psum | solution.py:56
  184.3 1.5 convolution_convert_fusion
  185.7 3.7 %collective-permute-start.3 = (bf16[2,64,2048]{2,1,0:T(8,128)(2,1)S(1)}, bf16[2,64,2048]{2,1,0:T(8,128)(2,1)S(1)}, u32[]{:S(2)}, u32[]{:S(2)}) collective-permute-start(bf16[2,64,2048]{2,1,0:T(8,128)(2,1)S(1)} %convolution_convert_fusion), channel_id=1, source_target_pairs={{0,16},{1,17},{2,18},{3,19},{4,20},{5,21},{6,22},{7,23},{8,24},{9,... | collective-permute-start | bytes 1572872 | tf_op jit(solution)/shard_map/ppermute | solution.py:16
  189.5 1.3 fusion.5
  190.8 1.3 fusion.4
  192.0 0.8 pad_maximum_fusion.1
  194.1 0.9 fusion.6
  195.0 1.0 fusion.41
  196.0 1.1 fusion.3
  197.1 3.0 %collective-permute-done.3 = bf16[2,64,2048]{2,1,0:T(8,128)(2,1)S(1)} collective-permute-done((bf16[2,64,2048]{2,1,0:T(8,128)(2,1)S(1)}, bf16[2,64,2048]{2,1,0:T(8,128)(2,1)S(1)}, u32[]{:S(2)}, u32[]{:S(2)}) %collective-permute-start.3) | collective-permute-done | bytes 524320 | tf_op jit(solution)/shard_map/ppermute | solution.py:16
  200.1 1.1 fusion.2
  (31 shorter events, 4.9 us)
Async XLA Ops:
  7.2 42.6 %copy-start = (bf16[2,2048,64]{1,2,0:T(8,128)(2,1)S(1)}, bf16[2,2048,64]{1,2,0:T(8,128)(2,1)}, u32[]{:S(2)}) copy-start(bf16[2,2048,64]{1,2,0:T(8,128)(2,1)} %param.10) | copy-start | bytes 1572868
  7.2 45.6 %copy-start.4 = (bf16[2,64,2048]{2,1,0:T(8,128)(2,1)S(1)}, bf16[2,64,2048]{2,1,0:T(8,128)(2,1)}, u32[]{:S(2)}) copy-start(bf16[2,64,2048]{2,1,0:T(8,128)(2,1)} %param.13) | copy-start | bytes 1572868
  7.2 42.5 %all-gather.3.cloned.1.call-start = ((), (), s32[]{:S(2)}) async-start(), calls=%async_computation.1 | async-start | bytes 1114112 | tf_op jit(solution)/shard_map/all_gather | solution.py:31
  7.9 120.8 %reduce-scatter.2.cloned.1.call-start = ((), (), s32[]{:S(2)}) async-start(), calls=%async_computation.2 | async-start | bytes 4456448 | tf_op jit(solution)/shard_map/reduce_scatter | solution.py:52
  8.0 46.1 %collective-permute-start = (bf16[1,2,64,2048]{3,2,1,0:T(8,128)(2,1)}, bf16[1,2,64,2048]{3,2,1,0:T(8,128)(2,1)S(1)}, u32[]{:S(2)}, u32[]{:S(2)}) collective-permute-start(bf16[1,2,64,2048]{3,2,1,0:T(8,128)(2,1)} %param.15), channel_id=1, source_target_pairs={{16,0},{17,1},{18,2},{19,3},{20,4},{21,5},{22,6},{23,7},{24,8},{25... | collective-permute-start | bytes 1572872 | tf_op jit(solution)/shard_map/ppermute | solution.py:16
  10.0 43.1 %copy-start.5 = (bf16[1,64,2048]{2,1,0:T(8,128)(2,1)S(1)}, bf16[1,64,2048]{2,1,0:T(8,128)(2,1)}, u32[]{:S(2)}) copy-start(bf16[1,64,2048]{2,1,0:T(8,128)(2,1)} %param.14) | copy-start | bytes 786436
  52.7 1.0 copy-start.2
  56.7 78.8 %copy-start.6 = (bf16[2,128,128]{2,1,0:T(8,128)(2,1)S(1)}, bf16[2,128,128]{2,1,0:T(8,128)(2,1)}, u32[]{:S(2)}) copy-start(bf16[2,128,128]{2,1,0:T(8,128)(2,1)} %param.9) | copy-start | bytes 196612
  56.7 127.5 %all-gather.5.cloned.1.call-start = ((), (), s32[]{:S(2)}) async-start(), calls=%async_computation.3 | async-start | bytes 2228224 | tf_op jit(solution)/shard_map/all_gather | solution.py:60
  129.6 5.9 %collective-permute-start.1 = (f32[2,128,128]{2,1,0:T(8,128)S(1)}, f32[2,128,128]{2,1,0:T(8,128)S(1)}, u32[]{:S(2)}, u32[]{:S(2)}) collective-permute-start(f32[2,128,128]{2,1,0:T(8,128)S(1)} %slice.55), channel_id=1, source_target_pairs={{0,16},{1,17},{2,18},{3,19},{4,20},{5,21},{6,22},{7,23},{8,24},{9,... | collective-permute-start | bytes 393224 | tf_op jit(solution)/shard_map/ppermute | solution.py:16
  137.1 6.1 %collective-permute-start.2 = (bf16[2,128,128]{2,1,0:T(8,128)(2,1)S(1)}, bf16[2,128,128]{2,1,0:T(8,128)(2,1)S(1)}, u32[]{:S(2)}, u32[]{:S(2)}) collective-permute-start(bf16[2,128,128]{2,1,0:T(8,128)(2,1)S(1)} %get-tuple-element.6), channel_id=1, source_target_pairs={{16,0},{17,1},{18,2},{19,3},{20,4},{21,5},{22,6},{23,7},{24,8},{25... | collective-permute-start | bytes 196616 | tf_op jit(solution)/shard_map/ppermute | solution.py:16
  184.3 8.6 %copy-start.1 = (bf16[4,128,2048]{2,1,0:T(8,128)(2,1)S(1)}, bf16[4,128,2048]{2,1,0:T(8,128)(2,1)}, u32[]{:S(2)}) copy-start(bf16[4,128,2048]{2,1,0:T(8,128)(2,1)} %all-gather.5.cloned.1.call-done) | copy-start | bytes 6291460
  185.7 14.4 %collective-permute-start.3 = (bf16[2,64,2048]{2,1,0:T(8,128)(2,1)S(1)}, bf16[2,64,2048]{2,1,0:T(8,128)(2,1)S(1)}, u32[]{:S(2)}, u32[]{:S(2)}) collective-permute-start(bf16[2,64,2048]{2,1,0:T(8,128)(2,1)S(1)} %convolution_convert_fusion), channel_id=1, source_target_pairs={{0,16},{1,17},{2,18},{3,19},{4,20},{5,21},{6,22},{7,23},{8,24},{9,... | collective-permute-start | bytes 1572872 | tf_op jit(solution)/shard_map/ppermute | solution.py:16
  193.5 2.5 %copy-start.3 = (bf16[2,128,2048]{2,1,0:T(8,128)(2,1)S(1)}, bf16[2,128,2048]{2,1,0:T(8,128)(2,1)}, u32[]{:S(2)}) copy-start(bf16[2,128,2048]{2,1,0:T(8,128)(2,1)} %all-gather.3.cloned.1.call-done) | copy-start | bytes 3145732
Sparse Core Ops, SparseCore 0:
  10.2 39.4 all-gather.2
  56.8 71.8 reduce-scatter.1
  144.0 40.1 all-gather.4
where the time goes:
time: 209 us
  waiting for transfers between devices  123 us (59%)
  blocking collectives  39.2 us (19%)
  between operations  15.7 us (8%)
  matrix products  13.5 us (6%)
  starting transfers between devices  9.81 us (5%)
  other arithmetic  5.98 us (3%)
    reduce_scatter x1, waiting for transfers between devices, per_device(): summed = lax.psum_scatter(partials, 'lat', scatter_dimension=2, tiled=True)  71.9 us
    all_gather x1, waiting for transfers between devices, per_device(): inputs_full = lax.all_gather(resid_in, 'lat', axis=2, tiled=True)  39.8 us
    psum x1, blocking collectives, per_device(): squared_total = lax.psum(jnp.sum(misfit * misfit), ('sec', 'lat'))  39.2 us
    ppermute x4, waiting for transfers between devices, shifted(): lax.ppermute(value, axis, [(source, source + steps) for source in range(f...  10.4 us
    ppermute x4, starting transfers between devices, shifted(): lax.ppermute(value, axis, [(source, source + steps) for source in range(f...  9.69 us
  transfers between devices with their start and end apart: 7, of which 6 were waited for; matrix products, arithmetic and copies ran while one was open for 6% of the time, Pallas kernels for 0%

commit v1 on v0

--- a/solution.py
+++ b/solution.py
@@ -1,13 +1,275 @@
+import functools
+
 import jax
 import jax.numpy as jnp
 from jax import lax
+from jax.experimental import pallas as pl
+from jax.experimental.pallas import tpu as pltpu
 from jax.sharding import PartitionSpec as P
 
-D = 2048
-TOKENS = 128
-
-
 jump_width = 0.1
+
+Z_STEP, Y_STEP, C_STEP = 4, 2, 1
+
+VMEM = pl.BlockSpec(memory_space=pltpu.VMEM)
+
+
+def dot_nt(a, b):
+    return lax.dot_general(a, b, (((1,), (1,)), ((), ())), preferred_element_type=jnp.float32)
+
+
+def dot_tn(a, b):
+    return lax.dot_general(a, b, (((0,), (0,)), ((), ())), preferred_element_type=jnp.float32)
+
+
+def dot_nn(a, b):
+    return lax.dot_general(a, b, (((1,), (0,)), ((), ())), preferred_element_type=jnp.float32)
+
+
+def place():
+    lat = lax.axis_index("lat")
+    return lat // Z_STEP, (lat // Y_STEP) % 2, lat % 2
+
+
+def lanes(start, size):
+    return pl.ds(pl.multiple_of(start, 128), size)
+
+
+def run(kernel, name, outs, *operands, cost=(0, 0)):
+    return pl.pallas_call(
+        kernel,
+        name=name,
+        out_shape=[jax.ShapeDtypeStruct(shape, dtype) for shape, dtype in outs],
+        in_specs=[VMEM] * len(operands),
+        out_specs=[VMEM] * len(outs),
+        compiler_params=pltpu.CompilerParams(vmem_limit_bytes=48 * 1024 * 1024),
+        cost_estimate=pl.CostEstimate(flops=cost[0], bytes_accessed=cost[1], transcendentals=0),
+    )(*operands)
+
+
+def to_lat(value, step):
+    return lax.ppermute(value, "lat", [(source, source ^ step) for source in range(lax.axis_size("lat"))])
+
+
+def to_both(value, sec_pairs, step):
+    count = lax.axis_size("lat")
+    pairs = [(a * count + lat, b * count + (lat ^ step)) for a, b in sec_pairs for lat in range(count)]
+    return lax.ppermute(value, ("sec", "lat"), pairs)
+
+
+DOWN, UP, SWAP = [(0, 1)], [(1, 0)], [(0, 1), (1, 0)]
+
+
+def pack_kernel(same, nxt, cross, own_s, own_x, far_s, far_x):
+    _, y, _ = place()
+    sources = [(same.at[1], 0), (nxt.at[0], 1), (same.at[0], 2)]
+    width = own_s.shape[1] // 4
+    for z in range(4):
+        to = slice(z * width, (z + 1) * width)
+        for half, (plain, crossed) in enumerate(((own_s, own_x), (far_s, far_x))):
+            cols = lanes(z * 2 * width + (y + half) % 2 * width, width)
+            for source, row in sources:
+                plain[row * 64 : row * 64 + 64, to] = source[:, cols]
+            for j in range(2):
+                crossed[j * 64 : j * 64 + 64, to] = cross[0, j, :, cols]
+
+
+def encode_kernel(*refs):
+    pieces, (weight, bias, cut, full, slope, act) = refs[:8], refs[8:]
+    z, y, c = place()
+    block = pieces[0].shape[-1]
+    for k in range(4):
+        for core in range(2):
+            for j in range(2):
+                home = (z ^ k) * Z_STEP + (y ^ j) * Y_STEP + (c ^ core)
+                for layer in range(2):
+                    full[layer, :, lanes(home * block, block)] = pieces[core * 4 + k][j, layer]
+    for layer in range(2):
+        pre = dot_nt(weight[layer], full[layer]) + bias[layer]
+        gate = jax.nn.sigmoid((pre - cut[layer]) / jump_width)
+        act[layer] = (pre * gate).astype(jnp.bfloat16)
+        slope[layer] = gate + pre * gate * (1.0 - gate) / jump_width
+
+
+def decode_kernel(act, act_y, act_x, act_d, own_s, own_x, peer_s, peer_x, near_x, diag_x, send, keep):
+    _, _, c = place()
+    rows = lambda ref: ref.reshape(128, 128)
+    first = dot_tn(jnp.concatenate([act[0], act_y[0]]), jnp.concatenate([own_s[128:192], peer_s[128:192]]))
+    first += dot_tn(rows(act_x[...]), near_x[...])
+    first += dot_tn(rows(act_d[...]), diag_x[...])
+    second = dot_tn(jnp.concatenate([act[1], act[0]]), own_s[0:128])
+    second += dot_tn(jnp.concatenate([act_y[1], act_y[0]]), peer_s[0:128])
+    second += dot_tn(rows(act_x[...]), own_x[...])
+    second += dot_tn(rows(act_d[...]), peer_x[...])
+    block = send.shape[-1]
+    for layer, total in enumerate((first, second)):
+        for z in range(4):
+            low = total[:, z * 2 * block : z * 2 * block + block]
+            high = total[:, z * 2 * block + block : (z + 1) * 2 * block]
+            keep[z, layer] = jnp.where(c == 0, low, high)
+            send[z, layer] = jnp.where(c == 0, high, low).astype(jnp.bfloat16)
+
+
+def fold_kernel(keep, got, mine, s1, s2, s3):
+    z, _, _ = place()
+    mine[...] = keep[z] + got[z].astype(jnp.float32)
+    for k, out in ((1, s1), (2, s2), (3, s3)):
+        out[...] = (keep[z ^ k] + got[z ^ k].astype(jnp.float32)).astype(jnp.bfloat16)
+
+
+def misfit_kernel(mine, g1, g2, g3, target, dy):
+    total = mine[...] + g1[...].astype(jnp.float32) + g2[...].astype(jnp.float32) + g3[...].astype(jnp.float32)
+    dy[...] = (total - target[...].astype(jnp.float32)).astype(jnp.bfloat16)
+
+
+def act_grad_kernel(mine, core, own_s, own_x, peer_s, peer_x, near_x, diag_x, half, grad_own, to_y, to_x, to_d):
+    z, _, c = place()
+    block = mine.shape[-1]
+    for k in range(4):
+        for layer in range(2):
+            half[layer, :, lanes(((z ^ k) * 2 + c) * block, block)] = mine[k, layer]
+            half[layer, :, lanes(((z ^ k) * 2 + 1 - c) * block, block)] = core[k, layer]
+    first, second = half[0], half[1]
+    a = dot_nt(own_s[0:128], second)
+    grad_own[0] = a[64:128] + dot_nt(own_s[128:192], first)
+    grad_own[1] = a[0:64]
+    a = dot_nt(peer_s[0:128], second)
+    to_y[0:64] = (a[64:128] + dot_nt(peer_s[128:192], first)).astype(jnp.bfloat16)
+    to_y[64:128] = a[0:64].astype(jnp.bfloat16)
+    to_x[0:128] = (dot_nt(own_x[...], second) + dot_nt(near_x[...], first)).astype(jnp.bfloat16)
+    to_d[0:128] = (dot_nt(peer_x[...], second) + dot_nt(diag_x[...], first)).astype(jnp.bfloat16)
+    wide = half[...].astype(jnp.float32)
+    squares = jnp.sum((wide * wide).reshape(-1, 8, wide.shape[-1]), axis=0)
+    part = sum(squares[:, n * 128 : n * 128 + 128] for n in range(squares.shape[1] // 128))
+    high = part.astype(jnp.bfloat16)
+    low = (part - high.astype(jnp.float32)).astype(jnp.bfloat16)
+    for out in (to_y, to_x, to_d):
+        out[128:144] = jnp.concatenate([high, low])
+    grad_own[2, 0:8] = part
+
+
+def encoder_grad_kernel(entries, grad_own, from_y, from_x, from_d, slope, full, mean_square, grad_enc, grad_bias):
+    leading = lax.axis_index("sec") == 0
+    wide = [ref[...].astype(jnp.float32) for ref in (from_y, from_x, from_d)]
+    squares = grad_own[2, 0:8] + sum(part[128:136] + part[136:144] for part in wide)
+    mean_square[...] = jnp.sum(squares, keepdims=True) / entries
+    for layer in range(2):
+        rows = slice(layer * 64, layer * 64 + 64)
+        across = wide[1][rows] + wide[2][rows]
+        total = grad_own[layer] + wide[0][rows] + jnp.where(leading, across, jnp.zeros_like(across))
+        pre_grad = total * slope[layer]
+        grad_bias[layer : layer + 1] = jnp.sum(pre_grad.T, axis=0, keepdims=True)
+        grad_enc[layer] = dot_nn(pre_grad.astype(jnp.bfloat16), full[layer]).astype(jnp.bfloat16)
+
+
+def decoder_grad_kernel(act, act_x, half, far, far_core, x_own, x_core, d_own, d_core, grad_same, grad_next, grad_cross, dy, dx):
+    z, y, c = place()
+    leading = lax.axis_index("sec") == 0
+    block = far.shape[-1]
+    for layer in range(2):
+        for n in range(4):
+            dy[layer, :, lanes((n * 2 + y) * 2 * block, 2 * block)] = half[layer, :, n * 2 * block : (n + 1) * 2 * block]
+        for k in range(4):
+            home = (z ^ k) * Z_STEP + (1 - y) * Y_STEP
+            dy[layer, :, lanes((home + c) * block, block)] = far[k, layer]
+            dy[layer, :, lanes((home + 1 - c) * block, block)] = far_core[k, layer]
+    both = jnp.concatenate([act[0], act[1]])
+    grad_same[0] = dot_nn(act[0], dy[0]).astype(jnp.bfloat16)
+    second = dot_nn(both, dy[1]).astype(jnp.bfloat16)
+    grad_next[0] = second[0:64]
+    grad_same[1] = second[64:128]
+
+    @pl.when(leading)
+    def _():
+        for k in range(4):
+            for row, own, core in ((y, x_own, x_core), (1 - y, d_own, d_core)):
+                home = (z ^ k) * Z_STEP + row * Y_STEP
+                dx[:, lanes((home + c) * block, block)] = own[k]
+                dx[:, lanes((home + 1 - c) * block, block)] = core[k]
+        grad_cross[0] = dot_nn(both, dx[...]).astype(jnp.bfloat16).reshape(2, 64, -1)
+
+    @pl.when(jnp.logical_not(leading))
+    def _():
+        grad_cross[0] = dot_nn(act_x[...].reshape(128, 128), dy[1]).astype(jnp.bfloat16).reshape(2, 64, -1)
+
+
+def staged(resid_in, mlp_out, enc_weight, enc_bias, thresholds, same_dec, next_dec, cross_dec):
+    bf16, f32 = jnp.bfloat16, jnp.float32
+    depth = same_dec.shape[-1]
+    block = resid_in.shape[-1]
+    entries = 2.0 * resid_in.size * lax.axis_size("lat")
+    tall = jnp.swapaxes(enc_weight, 1, 2)
+    bias = jnp.broadcast_to(enc_bias[:, :, None], (2, 64, 128))
+    cut = jnp.broadcast_to(0.25 * thresholds.astype(f32)[:, :, None], (2, 64, 128))
+
+    other = to_lat(resid_in, Y_STEP)
+    own_s, own_x, far_s, far_x = run(
+        pack_kernel, "pack",
+        [((192, depth // 2), bf16), ((128, depth // 2), bf16)] * 2,
+        same_dec, next_dec, cross_dec,
+    )
+    near = jnp.stack([resid_in, other])
+    line = [near] + [to_lat(near, k * Z_STEP) for k in (1, 2, 3)]
+    own_s, own_x, far_s, far_x, _ = lax.optimization_barrier((own_s, own_x, far_s, far_x, other))
+    peer_s = to_lat(far_s, Y_STEP)
+    near_x = to_both(own_x, DOWN, 0)
+    peer_x = to_both(far_x, [(1, 1)], Y_STEP)
+    diag_x = to_both(far_x, DOWN, Y_STEP)
+    pieces = line + [to_lat(piece, C_STEP) for piece in line]
+    full, slope, act = run(
+        encode_kernel, "encode",
+        [((2, 128, depth), bf16), ((2, 64, 128), f32), ((2, 64, 128), bf16)],
+        *pieces, tall, bias, cut,
+    )
+    act_y = to_lat(act, Y_STEP)
+    act_x = to_both(act, DOWN, 0)
+    act_d = to_both(act, DOWN, Y_STEP)
+    send, keep = run(
+        decode_kernel, "decode",
+        [((4, 2, 128, block), bf16), ((4, 2, 128, block), f32)],
+        act, act_y, act_x, act_d, own_s, own_x, peer_s, peer_x, near_x, diag_x,
+    )
+    got = to_lat(send, C_STEP)
+    mine, *parts = run(
+        fold_kernel, "fold",
+        [((2, 128, block), f32)] + [((2, 128, block), bf16)] * 3,
+        keep, got,
+    )
+    parts = [to_lat(part, k * Z_STEP) for k, part in zip((1, 2, 3), parts)]
+    (dy,) = run(misfit_kernel, "misfit", [((2, 128, block), bf16)], mine, *parts, mlp_out)
+    row = jnp.stack([dy] + [to_lat(dy, k * Z_STEP) for k in (1, 2, 3)])
+    row_core = to_lat(row, C_STEP)
+    far = to_lat(row, Y_STEP)
+    x_own = to_both(row[:, 0], UP, 0)
+    d_own = to_both(row[:, 0], UP, Y_STEP)
+    half, grad_own, to_y, to_x, to_d = run(
+        act_grad_kernel, "act_grad",
+        [((2, 128, depth // 2), bf16), ((3, 64, 128), f32)] + [((144, 128), bf16)] * 3,
+        row, row_core, own_s, own_x, peer_s, peer_x, near_x, diag_x,
+    )
+    from_y = to_lat(to_y, Y_STEP)
+    from_x = to_both(to_x, SWAP, 0)
+    from_d = to_both(to_d, SWAP, Y_STEP)
+    mean_square, grad_enc, grad_bias = run(
+        functools.partial(encoder_grad_kernel, entries), "encoder_grad",
+        [((1, 1), f32), ((2, 64, depth), bf16), ((2, 64), f32)],
+        grad_own, from_y, from_x, from_d, slope, full,
+    )
+    far_core = to_lat(far, C_STEP)
+    x_core = to_lat(x_own, C_STEP)
+    d_core = to_lat(d_own, C_STEP)
+    operands = (act, act_x, half, far, far_core, x_own, x_core, d_own, d_core)
+    outs = [((2, 64, depth), bf16), ((1, 64, depth), bf16), ((1, 2, 64, depth), bf16)]
+    grad_same, grad_next, grad_cross = pl.pallas_call(
+        decoder_grad_kernel,
+        name="decoder_grad",
+        out_shape=[jax.ShapeDtypeStruct(shape, dtype) for shape, dtype in outs],
+        in_specs=[VMEM] * len(operands),
+        out_specs=[VMEM] * len(outs),
+        scratch_shapes=[pltpu.VMEM((2, 128, depth), bf16), pltpu.VMEM((128, depth), bf16)],
+        compiler_params=pltpu.CompilerParams(vmem_limit_bytes=48 * 1024 * 1024),
+    )(*operands)
+    return (mean_square[0, 0], jnp.swapaxes(grad_enc, 1, 2), grad_bias, grad_same, grad_next, grad_cross)
 
 
 def shifted(value, axis, steps):
@@ -26,7 +288,7 @@
     return lax.dot_general(act, grad, (((0,), (0,)), ((), ())), preferred_element_type=jnp.float32)
 
 
-def per_device(resid_in, mlp_out, enc_weight, enc_bias, thresholds, same_dec, next_dec, cross_dec):
+def plain(resid_in, mlp_out, enc_weight, enc_bias, thresholds, same_dec, next_dec, cross_dec):
     leading = lax.axis_index("sec") == 0
     inputs_full = lax.all_gather(resid_in, "lat", axis=2, tiled=True)
     pre_act = (
@@ -54,7 +316,7 @@
     rebuilt = summed[:2] + crossing
     misfit = rebuilt - mlp_out.astype(jnp.float32)
     squared_total = lax.psum(jnp.sum(misfit * misfit), ("sec", "lat"))
-    mean_square = squared_total / (4.0 * TOKENS * D)
+    mean_square = squared_total / (2.0 * mlp_out.size * lax.axis_size("lat"))
     dy_rows = misfit.astype(jnp.bfloat16)
     extra_rows = shifted(dy_rows, "sec", -1)
     grad_full = lax.all_gather(
@@ -96,6 +358,7 @@
 
 
 def solution(mesh):
+    body = staged if mesh.shape["lat"] == 16 else plain
     in_specs = (
         P("sec", None, "lat"),
         P("sec", None, "lat"),
@@ -114,6 +377,4 @@
         P("sec", "lat", None),
         P("sec", None, "lat", None),
     )
-    return jax.shard_map(
-        per_device, mesh=mesh, in_specs=in_specs, out_specs=out_specs, check_vma=False
-    )
+    return jax.shard_map(body, mesh=mesh, in_specs=in_specs, out_specs=out_specs, check_vma=False)

time: 209 us -> 91.1 us (0.44)
  waiting for transfers between devices: 123 us -> 44.7 us
  blocking collectives: 39.2 us -> 0 us
  starting transfers between devices: 9.81 us -> 36.2 us
  between operations: 15.7 us -> 0.93 us
  matrix products: 13.5 us -> 0 us
  Pallas kernels: 0 us -> 5.75 us
  other arithmetic: 5.98 us -> 0.89 us
    reduce_scatter x1 -> x0, waiting for transfers between devices: 71.9 us -> none  [per_device(): summed = lax.psum_scatter(partials, 'lat', scatter_dimension=2, tiled=True)]
    all_gather x2 -> x0, waiting for transfers between devices: 40.3 us -> none  [the longest x1 39.8 us: per_device(): inputs_full = lax.all_gather(resid_in, 'lat', axis=2, tiled=True)]
    psum x1 -> x0, blocking collectives: 39.2 us -> none  [per_device(): squared_total = lax.psum(jnp.sum(misfit * misfit), ('sec', 'lat'))]
    ppermute x4 -> x32, waiting for transfers between devices: 10.4 us -> 44.7 us  [the longest x23 29.5 us: to_lat(): lax.ppermute(value, 'lat', [(source, source ^ step) for source in range(l...]
    ppermute x4 -> x32, starting transfers between devices: 9.69 us -> 36.2 us  [the longest x23 20.7 us: to_lat(): lax.ppermute(value, 'lat', [(source, source ^ step) for source in range(l...]
    dot_general x17 -> x0, matrix products: 13.5 us -> none  [the longest x3 3.44 us: outer_dot(): lax.dot_general(act, grad, (((0,), (0,)), ((), ())), preferred_element_ty...]
    pallas_call x0 -> x8, Pallas kernels: none -> 5.75 us  [the longest x7 3.73 us: run(): pl.pallas_call(kernel, name=name, out_shape=[jax.ShapeDtypeStruct(shape,...]
    another operation x2, other arithmetic: 3.07 us -> 0.89 us  [the longest x1 0.85 us: staged(): near = jnp.stack([resid_in, other])]
  transfers between devices with their start and end apart: 7 -> 32, of which waited for: 6 -> 18; matrix products, arithmetic and copies ran while one was open for 6% -> 0% of each run, Pallas kernels for 0% -> 3%
where the time goes in v1:
time: 91.1 us; the launch traced here: 90.8 us
  waiting for transfers between devices  44.7 us (49%)
  starting transfers between devices  36.2 us (40%)
  Pallas kernels  5.75 us (6%)
  local copies, waits for them, and re-layouts  2.33 us (3%)
  between operations  0.93 us (1%)
    ppermute x23, waiting for transfers between devices, to_lat(): lax.ppermute(value, 'lat', [(source, source ^ step) for source in range(l...  29.5 us
    ppermute x23, starting transfers between devices, to_lat(): lax.ppermute(value, 'lat', [(source, source ^ step) for source in range(l...  20.7 us
    ppermute x9, starting transfers between devices, to_both(): return lax.ppermute(value, ('sec', 'lat'), pairs)  15.5 us
    ppermute x9, waiting for transfers between devices, to_both(): return lax.ppermute(value, ('sec', 'lat'), pairs)  15.2 us
    pallas_call x7, Pallas kernels, run(): pl.pallas_call(kernel, name=name, out_shape=[jax.ShapeDtypeStruct(shape,...  3.73 us
    unnamed x14, local copies, waits for them, and re-layouts  2.1 us
    pallas_call x1, Pallas kernels, staged(): pl.pallas_call(decoder_grad_kernel, name='decoder_grad', out_shape=[jax.S...  2.03 us
  transfers between devices with their start and end apart: 32, of which 18 were waited for; matrix products, arithmetic and copies ran while one was open for 0% of the time, Pallas kernels for 3%

profile of v1, /device:TPU:0, one launch (start us, length us, event | category | flops | bytes accessed | tf_op | source)
XLA Modules:
  0.0 90.8 jit_solution(3073028099148346915)
XLA Ops:
  0.6 3.0 %collective-permute-start = (bf16[2,128,128]{2,1,0:T(8,128)(2,1)}, bf16[2,128,128]{2,1,0:T(8,128)(2,1)S(1)}, u32[]{:S(2)}, u32[]{:S(2)}) collective-permute-start(bf16[2,128,128]{2,1,0:T(8,128)(2,1)} %param.8), channel_id=1, source_target_pairs={{0,2},{1,3},{2,0},{3,1},{4,6},{5,7},{6,4},{7,5},{8,10},{9,11},{10,... | collective-permute-start | bytes 196616 | tf_op jit(solution)/shard_map/ppermute | solution.py:51
  3.7 2.5 %collective-permute-done = bf16[2,128,128]{2,1,0:T(8,128)(2,1)S(1)} collective-permute-done((bf16[2,128,128]{2,1,0:T(8,128)(2,1)}, bf16[2,128,128]{2,1,0:T(8,128)(2,1)S(1)}, u32[]{:S(2)}, u32[]{:S(2)}) %collective-permute-start) | collective-permute-done | bytes 65568 | tf_op jit(solution)/shard_map/ppermute | solution.py:51
  7.0 2.1 %collective-permute-start.1 = (bf16[2,2,128,128]{3,2,1,0:T(8,128)(2,1)S(1)}, bf16[2,2,128,128]{3,2,1,0:T(8,128)(2,1)S(1)}, u32[]{:S(2)}, u32[]{:S(2)}) collective-permute-start(bf16[2,2,128,128]{3,2,1,0:T(8,128)(2,1)S(1)} %pad_maximum_fusion.1.refs_0_), channel_id=1, source_target_pairs={{0,4},{1,5},{2,6},{3,7},{4,0},{5,1},{6,2},{7,3},{8,12},{9,13},{10,... | collective-permute-start | bytes 393224 | tf_op jit(solution)/shard_map/ppermute | solution.py:51
  9.1 2.6 %collective-permute-start.2 = (bf16[2,2,128,128]{3,2,1,0:T(8,128)(2,1)S(1)}, bf16[2,2,128,128]{3,2,1,0:T(8,128)(2,1)S(1)}, u32[]{:S(2)}, u32[]{:S(2)}) collective-permute-start(bf16[2,2,128,128]{3,2,1,0:T(8,128)(2,1)S(1)} %pad_maximum_fusion.1.refs_0_), channel_id=1, source_target_pairs={{0,8},{1,9},{2,10},{3,11},{4,12},{5,13},{6,14},{7,15},{8,0},{9,1},... | collective-permute-start | bytes 393224 | tf_op jit(solution)/shard_map/ppermute | solution.py:51
  14.6 1.7 %collective-permute-start.11 = (bf16[192,1024]{1,0:T(8,128)(2,1)S(1)}, bf16[192,1024]{1,0:T(8,128)(2,1)S(1)}, u32[]{:S(2)}, u32[]{:S(2)}) collective-permute-start(bf16[192,1024]{1,0:T(8,128)(2,1)S(1)} %get-tuple-element.41), channel_id=1, source_target_pairs={{0,2},{1,3},{2,0},{3,1},{4,6},{5,7},{6,4},{7,5},{8,10},{9,11},{10,... | collective-permute-start | bytes 1179656 | tf_op jit(solution)/shard_map/ppermute | solution.py:51
  16.3 4.6 %collective-permute-done.2.refs_2_ = bf16[2,2,128,128]{3,2,1,0:T(8,128)(2,1)S(1)} collective-permute-done((bf16[2,2,128,128]{3,2,1,0:T(8,128)(2,1)S(1)}, bf16[2,2,128,128]{3,2,1,0:T(8,128)(2,1)S(1)}, u32[]{:S(2)}, u32[]{:S(2)}) %collective-permute-start.2) | collective-permute-done | bytes 131104 | tf_op jit(solution)/shard_map/ppermute | solution.py:51
  20.9 3.4 %collective-permute-start.13 = (bf16[128,1024]{1,0:T(8,128)(2,1)S(1)}, bf16[128,1024]{1,0:T(8,128)(2,1)S(1)}, u32[]{:S(2)}, u32[]{:S(2)}) collective-permute-start(bf16[128,1024]{1,0:T(8,128)(2,1)S(1)} %get-tuple-element.40.own_x), channel_id=1, source_target_pairs={{0,16},{1,17},{2,18},{3,19},{4,20},{5,21},{6,22},{7,23},{8,24},{9,... | collective-permute-start | bytes 786440 | tf_op jit(solution)/shard_map/ppermute | solution.py:57
  25.0 4.0 %collective-permute-start.14 = (bf16[128,1024]{1,0:T(8,128)(2,1)S(1)}, bf16[128,1024]{1,0:T(8,128)(2,1)S(1)}, u32[]{:S(2)}, u32[]{:S(2)}) collective-permute-start(bf16[128,1024]{1,0:T(8,128)(2,1)S(1)} %get-tuple-element.42), channel_id=1, source_target_pairs={{0,18},{1,19},{2,16},{3,17},{4,22},{5,23},{6,20},{7,21},{8,26},{9,... | collective-permute-start | bytes 786440 | tf_op jit(solution)/shard_map/ppermute | solution.py:57
  31.4 1.3 %collective-permute-start.9 = (bf16[2,64,128]{2,1,0:T(8,128)(2,1)S(1)}, bf16[2,64,128]{2,1,0:T(8,128)(2,1)S(1)}, u32[]{:S(2)}, u32[]{:S(2)}) collective-permute-start(bf16[2,64,128]{2,1,0:T(8,128)(2,1)S(1)} %get-tuple-element.34.act), channel_id=1, source_target_pairs={{0,16},{1,17},{2,18},{3,19},{4,20},{5,21},{6,22},{7,23},{8,24},{9,... | collective-permute-start | bytes 98312 | tf_op jit(solution)/shard_map/ppermute | solution.py:57
  32.7 3.5 %collective-permute-start.10 = (bf16[2,64,128]{2,1,0:T(8,128)(2,1)S(1)}, bf16[2,64,128]{2,1,0:T(8,128)(2,1)S(1)}, u32[]{:S(2)}, u32[]{:S(2)}) collective-permute-start(bf16[2,64,128]{2,1,0:T(8,128)(2,1)S(1)} %get-tuple-element.34.act), channel_id=1, source_target_pairs={{0,18},{1,19},{2,16},{3,17},{4,22},{5,23},{6,20},{7,21},{8,26},{9,... | collective-permute-start | bytes 98312 | tf_op jit(solution)/shard_map/ppermute | solution.py:57
  37.8 2.4 %collective-permute-done.8.act_y = bf16[2,64,128]{2,1,0:T(8,128)(2,1)S(1)} collective-permute-done((bf16[2,64,128]{2,1,0:T(8,128)(2,1)S(1)}, bf16[2,64,128]{2,1,0:T(8,128)(2,1)S(1)}, u32[]{:S(2)}, u32[]{:S(2)}) %collective-permute-start.8) | collective-permute-done | bytes 32800 | tf_op jit(solution)/shard_map/ppermute | solution.py:51
  40.9 1.5 %collective-permute-done.15.got = bf16[4,2,128,128]{3,2,1,0:T(8,128)(2,1)S(1)} collective-permute-done((bf16[4,2,128,128]{3,2,1,0:T(8,128)(2,1)S(1)}, bf16[4,2,128,128]{3,2,1,0:T(8,128)(2,1)S(1)}, u32[]{:S(2)}, u32[]{:S(2)}) %collective-permute-start.15) | collective-permute-done | bytes 262176 | tf_op jit(solution)/shard_map/ppermute | solution.py:51
  43.4 2.3 %collective-permute-start.17 = (bf16[2,128,128]{2,1,0:T(8,128)(2,1)S(1)}, bf16[2,128,128]{2,1,0:T(8,128)(2,1)S(1)}, u32[]{:S(2)}, u32[]{:S(2)}) collective-permute-start(bf16[2,128,128]{2,1,0:T(8,128)(2,1)S(1)} %get-tuple-element.47), channel_id=1, source_target_pairs={{0,8},{1,9},{2,10},{3,11},{4,12},{5,13},{6,14},{7,15},{8,0},{9,1},... | collective-permute-start | bytes 196616 | tf_op jit(solution)/shard_map/ppermute | solution.py:51
  47.5 3.6 %collective-permute-done.17.g2 = bf16[2,128,128]{2,1,0:T(8,128)(2,1)S(1)} collective-permute-done((bf16[2,128,128]{2,1,0:T(8,128)(2,1)S(1)}, bf16[2,128,128]{2,1,0:T(8,128)(2,1)S(1)}, u32[]{:S(2)}, u32[]{:S(2)}) %collective-permute-start.17) | collective-permute-done | bytes 65568 | tf_op jit(solution)/shard_map/ppermute | solution.py:51
  53.2 1.4 %collective-permute-start.20 = (bf16[2,128,128]{2,1,0:T(8,128)(2,1)S(1)}, bf16[2,128,128]{2,1,0:T(8,128)(2,1)S(1)}, u32[]{:S(2)}, u32[]{:S(2)}) collective-permute-start(bf16[2,128,128]{2,1,0:T(8,128)(2,1)S(1)} %misfit.1), channel_id=1, source_target_pairs={{0,8},{1,9},{2,10},{3,11},{4,12},{5,13},{6,14},{7,15},{8,0},{9,1},... | collective-permute-start | bytes 196616 | tf_op jit(solution)/shard_map/ppermute | solution.py:51
  54.5 1.8 %collective-permute-start.21 = (bf16[2,128,128]{2,1,0:T(8,128)(2,1)S(1)}, bf16[2,128,128]{2,1,0:T(8,128)(2,1)S(1)}, u32[]{:S(2)}, u32[]{:S(2)}) collective-permute-start(bf16[2,128,128]{2,1,0:T(8,128)(2,1)S(1)} %misfit.1), channel_id=1, source_target_pairs={{0,12},{1,13},{2,14},{3,15},{4,8},{5,9},{6,10},{7,11},{8,4},{9,5},... | collective-permute-start | bytes 196616 | tf_op jit(solution)/shard_map/ppermute | solution.py:51
  56.3 2.9 %collective-permute-done.20 = bf16[2,128,128]{2,1,0:T(8,128)(2,1)S(1)} collective-permute-done((bf16[2,128,128]{2,1,0:T(8,128)(2,1)S(1)}, bf16[2,128,128]{2,1,0:T(8,128)(2,1)S(1)}, u32[]{:S(2)}, u32[]{:S(2)}) %collective-permute-start.20) | collective-permute-done | bytes 65568 | tf_op jit(solution)/shard_map/ppermute | solution.py:51
  59.2 1.4 %collective-permute-done.21 = bf16[2,128,128]{2,1,0:T(8,128)(2,1)S(1)} collective-permute-done((bf16[2,128,128]{2,1,0:T(8,128)(2,1)S(1)}, bf16[2,128,128]{2,1,0:T(8,128)(2,1)S(1)}, u32[]{:S(2)}, u32[]{:S(2)}) %collective-permute-start.21) | collective-permute-done | bytes 65568 | tf_op jit(solution)/shard_map/ppermute | solution.py:51
  62.9 4.2 %collective-permute-done.26 = bf16[4,2,128,128]{3,2,0,1:T(8,128)(2,1)S(1)} collective-permute-done((bf16[4,2,128,128]{3,2,0,1:T(8,128)(2,1)S(1)}, bf16[4,2,128,128]{3,2,0,1:T(8,128)(2,1)S(1)}, u32[]{:S(2)}, u32[]{:S(2)}) %collective-permute-start.26) | collective-permute-done | bytes 262176 | tf_op jit(solution)/shard_map/ppermute | solution.py:51
  68.4 3.6 %collective-permute-done.28.x_own = bf16[4,128,128]{2,1,0:T(8,128)(2,1)S(1)} collective-permute-done((bf16[4,128,128]{2,1,0:T(8,128)(2,1)S(1)}, bf16[4,128,128]{2,1,0:T(8,128)(2,1)S(1)}, u32[]{:S(2)}, u32[]{:S(2)}) %collective-permute-start.28) | collective-permute-done | bytes 131104 | tf_op jit(solution)/shard_map/ppermute | solution.py:57
  72.0 5.8 %collective-permute-done.30.d_own = bf16[4,128,128]{2,1,0:T(8,128)(2,1)S(1)} collective-permute-done((bf16[4,128,128]{2,1,0:T(8,128)(2,1)S(1)}, bf16[4,128,128]{2,1,0:T(8,128)(2,1)S(1)}, u32[]{:S(2)}, u32[]{:S(2)}) %collective-permute-start.30) | collective-permute-done | bytes 131104 | tf_op jit(solution)/shard_map/ppermute | solution.py:57
  78.9 3.8 %collective-permute-done.23.from_y = bf16[144,128]{1,0:T(8,128)(2,1)S(1)} collective-permute-done((bf16[144,128]{1,0:T(8,128)(2,1)S(1)}, bf16[144,128]{1,0:T(8,128)(2,1)S(1)}, u32[]{:S(2)}, u32[]{:S(2)}) %collective-permute-start.23) | collective-permute-done | bytes 36896 | tf_op jit(solution)/shard_map/ppermute | solution.py:51
  82.8 4.8 %collective-permute-done.25.from_d = bf16[144,128]{1,0:T(8,128)(2,1)S(1)} collective-permute-done((bf16[144,128]{1,0:T(8,128)(2,1)S(1)}, bf16[144,128]{1,0:T(8,128)(2,1)S(1)}, u32[]{:S(2)}, u32[]{:S(2)}) %collective-permute-start.25) | collective-permute-done | bytes 36896 | tf_op jit(solution)/shard_map/ppermute | solution.py:57
  88.7 2.0 %decoder_grad.1 = (bf16[2,64,2048]{2,1,0:T(8,128)(2,1)}, bf16[1,64,2048]{2,1,0:T(8,128)(2,1)}, bf16[1,2,64,2048]{3,2,1,0:T(8,128)(2,1)}) custom-call(bf16[2,64,128]{2,1,0:T(8,128)(2,1)S(1)} %get-tuple-element.34.act, bf16[2,64,128]{2,1,0:T(8,128)(2,1)S(1)} %collective-permute-done.9.act_x, bf16[2,128,1024]{2,1,0:T(8,128)(2,1)S(1)} %get-tuple-element.58.half, ...), custom_call_target="tpu_custom_call" | custom-call | tf_op jit(solution)/shard_map/decoder_grad/pallas_call | solution.py:263
  (72 shorter events, 19.7 us)
Async XLA Ops:
  0.6 5.5 %collective-permute-start = (bf16[2,128,128]{2,1,0:T(8,128)(2,1)}, bf16[2,128,128]{2,1,0:T(8,128)(2,1)S(1)}, u32[]{:S(2)}, u32[]{:S(2)}) collective-permute-start(bf16[2,128,128]{2,1,0:T(8,128)(2,1)} %param.8), channel_id=1, source_target_pairs={{0,2},{1,3},{2,0},{3,1},{4,6},{5,7},{6,4},{7,5},{8,10},{9,11},{10,... | collective-permute-start | bytes 196616 | tf_op jit(solution)/shard_map/ppermute | solution.py:51
  7.0 7.0 %collective-permute-start.1 = (bf16[2,2,128,128]{3,2,1,0:T(8,128)(2,1)S(1)}, bf16[2,2,128,128]{3,2,1,0:T(8,128)(2,1)S(1)}, u32[]{:S(2)}, u32[]{:S(2)}) collective-permute-start(bf16[2,2,128,128]{3,2,1,0:T(8,128)(2,1)S(1)} %pad_maximum_fusion.1.refs_0_), channel_id=1, source_target_pairs={{0,4},{1,5},{2,6},{3,7},{4,0},{5,1},{6,2},{7,3},{8,12},{9,13},{10,... | collective-permute-start | bytes 393224 | tf_op jit(solution)/shard_map/ppermute | solution.py:51
  9.1 11.8 %collective-permute-start.2 = (bf16[2,2,128,128]{3,2,1,0:T(8,128)(2,1)S(1)}, bf16[2,2,128,128]{3,2,1,0:T(8,128)(2,1)S(1)}, u32[]{:S(2)}, u32[]{:S(2)}) collective-permute-start(bf16[2,2,128,128]{3,2,1,0:T(8,128)(2,1)S(1)} %pad_maximum_fusion.1.refs_0_), channel_id=1, source_target_pairs={{0,8},{1,9},{2,10},{3,11},{4,12},{5,13},{6,14},{7,15},{8,0},{9,1},... | collective-permute-start | bytes 393224 | tf_op jit(solution)/shard_map/ppermute | solution.py:51
  11.7 9.2 %collective-permute-start.3 = (bf16[2,2,128,128]{3,2,1,0:T(8,128)(2,1)S(1)}, bf16[2,2,128,128]{3,2,1,0:T(8,128)(2,1)S(1)}, u32[]{:S(2)}, u32[]{:S(2)}) collective-permute-start(bf16[2,2,128,128]{3,2,1,0:T(8,128)(2,1)S(1)} %pad_maximum_fusion.1.refs_0_), channel_id=1, source_target_pairs={{0,12},{1,13},{2,14},{3,15},{4,8},{5,9},{6,10},{7,11},{8,4},{9,5},... | collective-permute-start | bytes 393224 | tf_op jit(solution)/shard_map/ppermute | solution.py:51
  11.7 12.6 %collective-permute-start.4 = (bf16[2,2,128,128]{3,2,1,0:T(8,128)(2,1)S(1)}, bf16[2,2,128,128]{3,2,1,0:T(8,128)(2,1)S(1)}, u32[]{:S(2)}, u32[]{:S(2)}) collective-permute-start(bf16[2,2,128,128]{3,2,1,0:T(8,128)(2,1)S(1)} %pad_maximum_fusion.1.refs_0_), channel_id=1, source_target_pairs={{0,1},{1,0},{2,3},{3,2},{4,5},{5,4},{6,7},{7,6},{8,9},{9,8},{10,11... | collective-permute-start | bytes 393224 | tf_op jit(solution)/shard_map/ppermute | solution.py:51
  14.0 11.0 %collective-permute-start.5 = (bf16[2,2,128,128]{3,2,1,0:T(8,128)(2,1)S(1)}, bf16[2,2,128,128]{3,2,1,0:T(8,128)(2,1)S(1)}, u32[]{:S(2)}, u32[]{:S(2)}) collective-permute-start(bf16[2,2,128,128]{3,2,1,0:T(8,128)(2,1)S(1)} %collective-permute-done.1.refs_1_), channel_id=1, source_target_pairs={{0,1},{1,0},{2,3},{3,2},{4,5},{5,4},{6,7},{7,6},{8,9},{9,8},{10,11... | collective-permute-start | bytes 393224 | tf_op jit(solution)/shard_map/ppermute | solution.py:51
  14.6 25.6 %collective-permute-start.11 = (bf16[192,1024]{1,0:T(8,128)(2,1)S(1)}, bf16[192,1024]{1,0:T(8,128)(2,1)S(1)}, u32[]{:S(2)}, u32[]{:S(2)}) collective-permute-start(bf16[192,1024]{1,0:T(8,128)(2,1)S(1)} %get-tuple-element.41), channel_id=1, source_target_pairs={{0,2},{1,3},{2,0},{3,1},{4,6},{5,7},{6,4},{7,5},{8,10},{9,11},{10,... | collective-permute-start | bytes 1179656 | tf_op jit(solution)/shard_map/ppermute | solution.py:51
  20.9 8.1 %collective-permute-start.6 = (bf16[2,2,128,128]{3,2,1,0:T(8,128)(2,1)S(1)}, bf16[2,2,128,128]{3,2,1,0:T(8,128)(2,1)S(1)}, u32[]{:S(2)}, u32[]{:S(2)}) collective-permute-start(bf16[2,2,128,128]{3,2,1,0:T(8,128)(2,1)S(1)} %collective-permute-done.2.refs_2_), channel_id=1, source_target_pairs={{0,1},{1,0},{2,3},{3,2},{4,5},{5,4},{6,7},{7,6},{8,9},{9,8},{10,11... | collective-permute-start | bytes 393224 | tf_op jit(solution)/shard_map/ppermute | solution.py:51
  20.9 11.8 %collective-permute-start.13 = (bf16[128,1024]{1,0:T(8,128)(2,1)S(1)}, bf16[128,1024]{1,0:T(8,128)(2,1)S(1)}, u32[]{:S(2)}, u32[]{:S(2)}) collective-permute-start(bf16[128,1024]{1,0:T(8,128)(2,1)S(1)} %get-tuple-element.40.own_x), channel_id=1, source_target_pairs={{0,16},{1,17},{2,18},{3,19},{4,20},{5,21},{6,22},{7,23},{8,24},{9,... | collective-permute-start | bytes 786440 | tf_op jit(solution)/shard_map/ppermute | solution.py:57
  24.3 11.9 %collective-permute-start.12 = (bf16[128,1024]{1,0:T(8,128)(2,1)S(1)}, bf16[128,1024]{1,0:T(8,128)(2,1)S(1)}, u32[]{:S(2)}, u32[]{:S(2)}) collective-permute-start(bf16[128,1024]{1,0:T(8,128)(2,1)S(1)} %get-tuple-element.42), channel_id=1, source_target_pairs={{16,18},{17,19},{18,16},{19,17},{20,22},{21,23},{22,20},{23,21},{2... | collective-permute-start | bytes 786440 | tf_op jit(solution)/shard_map/ppermute | solution.py:57
  25.0 11.8 %collective-permute-start.14 = (bf16[128,1024]{1,0:T(8,128)(2,1)S(1)}, bf16[128,1024]{1,0:T(8,128)(2,1)S(1)}, u32[]{:S(2)}, u32[]{:S(2)}) collective-permute-start(bf16[128,1024]{1,0:T(8,128)(2,1)S(1)} %get-tuple-element.42), channel_id=1, source_target_pairs={{0,18},{1,19},{2,16},{3,17},{4,22},{5,23},{6,20},{7,21},{8,26},{9,... | collective-permute-start | bytes 786440 | tf_op jit(solution)/shard_map/ppermute | solution.py:57
  31.4 5.8 %collective-permute-start.9 = (bf16[2,64,128]{2,1,0:T(8,128)(2,1)S(1)}, bf16[2,64,128]{2,1,0:T(8,128)(2,1)S(1)}, u32[]{:S(2)}, u32[]{:S(2)}) collective-permute-start(bf16[2,64,128]{2,1,0:T(8,128)(2,1)S(1)} %get-tuple-element.34.act), channel_id=1, source_target_pairs={{0,16},{1,17},{2,18},{3,19},{4,20},{5,21},{6,22},{7,23},{8,24},{9,... | collective-permute-start | bytes 98312 | tf_op jit(solution)/shard_map/ppermute | solution.py:57
  32.7 5.0 %collective-permute-start.10 = (bf16[2,64,128]{2,1,0:T(8,128)(2,1)S(1)}, bf16[2,64,128]{2,1,0:T(8,128)(2,1)S(1)}, u32[]{:S(2)}, u32[]{:S(2)}) collective-permute-start(bf16[2,64,128]{2,1,0:T(8,128)(2,1)S(1)} %get-tuple-element.34.act), channel_id=1, source_target_pairs={{0,18},{1,19},{2,16},{3,17},{4,22},{5,23},{6,20},{7,21},{8,26},{9,... | collective-permute-start | bytes 98312 | tf_op jit(solution)/shard_map/ppermute | solution.py:57
  43.4 7.7 %collective-permute-start.17 = (bf16[2,128,128]{2,1,0:T(8,128)(2,1)S(1)}, bf16[2,128,128]{2,1,0:T(8,128)(2,1)S(1)}, u32[]{:S(2)}, u32[]{:S(2)}) collective-permute-start(bf16[2,128,128]{2,1,0:T(8,128)(2,1)S(1)} %get-tuple-element.47), channel_id=1, source_target_pairs={{0,8},{1,9},{2,10},{3,11},{4,12},{5,13},{6,14},{7,15},{8,0},{9,1},... | collective-permute-start | bytes 196616 | tf_op jit(solution)/shard_map/ppermute | solution.py:51
  45.7 6.2 %collective-permute-start.18 = (bf16[2,128,128]{2,1,0:T(8,128)(2,1)S(1)}, bf16[2,128,128]{2,1,0:T(8,128)(2,1)S(1)}, u32[]{:S(2)}, u32[]{:S(2)}) collective-permute-start(bf16[2,128,128]{2,1,0:T(8,128)(2,1)S(1)} %get-tuple-element.48), channel_id=1, source_target_pairs={{0,12},{1,13},{2,14},{3,15},{4,8},{5,9},{6,10},{7,11},{8,4},{9,5},... | collective-permute-start | bytes 196616 | tf_op jit(solution)/shard_map/ppermute | solution.py:51
  53.2 6.1 %collective-permute-start.20 = (bf16[2,128,128]{2,1,0:T(8,128)(2,1)S(1)}, bf16[2,128,128]{2,1,0:T(8,128)(2,1)S(1)}, u32[]{:S(2)}, u32[]{:S(2)}) collective-permute-start(bf16[2,128,128]{2,1,0:T(8,128)(2,1)S(1)} %misfit.1), channel_id=1, source_target_pairs={{0,8},{1,9},{2,10},{3,11},{4,12},{5,13},{6,14},{7,15},{8,0},{9,1},... | collective-permute-start | bytes 196616 | tf_op jit(solution)/shard_map/ppermute | solution.py:51
  54.5 6.1 %collective-permute-start.21 = (bf16[2,128,128]{2,1,0:T(8,128)(2,1)S(1)}, bf16[2,128,128]{2,1,0:T(8,128)(2,1)S(1)}, u32[]{:S(2)}, u32[]{:S(2)}) collective-permute-start(bf16[2,128,128]{2,1,0:T(8,128)(2,1)S(1)} %misfit.1), channel_id=1, source_target_pairs={{0,12},{1,13},{2,14},{3,15},{4,8},{5,9},{6,10},{7,11},{8,4},{9,5},... | collective-permute-start | bytes 196616 | tf_op jit(solution)/shard_map/ppermute | solution.py:51
  60.7 6.4 %collective-permute-start.26 = (bf16[4,2,128,128]{3,2,0,1:T(8,128)(2,1)S(1)}, bf16[4,2,128,128]{3,2,0,1:T(8,128)(2,1)S(1)}, u32[]{:S(2)}, u32[]{:S(2)}) collective-permute-start(bf16[4,2,128,128]{3,2,0,1:T(8,128)(2,1)S(1)} %pad_maximum_fusion), channel_id=1, source_target_pairs={{0,2},{1,3},{2,0},{3,1},{4,6},{5,7},{6,4},{7,5},{8,10},{9,11},{10,... | collective-permute-start | bytes 786440 | tf_op jit(solution)/shard_map/ppermute | solution.py:51
  61.6 16.2 %collective-permute-start.22 = (bf16[4,2,128,128]{3,2,0,1:T(8,128)(2,1)S(1)}, bf16[4,2,128,128]{3,2,0,1:T(8,128)(2,1)S(1)}, u32[]{:S(2)}, u32[]{:S(2)}) collective-permute-start(bf16[4,2,128,128]{3,2,0,1:T(8,128)(2,1)S(1)} %pad_maximum_fusion), channel_id=1, source_target_pairs={{0,1},{1,0},{2,3},{3,2},{4,5},{5,4},{6,7},{7,6},{8,9},{9,8},{10,11... | collective-permute-start | bytes 786440 | tf_op jit(solution)/shard_map/ppermute | solution.py:51
  61.6 10.4 %collective-permute-start.28 = (bf16[4,128,128]{2,1,0:T(8,128)(2,1)S(1)}, bf16[4,128,128]{2,1,0:T(8,128)(2,1)S(1)}, u32[]{:S(2)}, u32[]{:S(2)}) collective-permute-start(bf16[4,128,128]{2,1,0:T(8,128)(2,1)S(1)} %slice_bitcast_fusion), channel_id=1, source_target_pairs={{16,0},{17,1},{18,2},{19,3},{20,4},{21,5},{22,6},{23,7},{24,8},{25... | collective-permute-start | bytes 393224 | tf_op jit(solution)/shard_map/ppermute | solution.py:57
  67.1 21.6 %collective-permute-start.27 = (bf16[4,2,128,128]{3,2,0,1:T(8,128)(2,1)S(1)}, bf16[4,2,128,128]{3,2,0,1:T(8,128)(2,1)S(1)}, u32[]{:S(2)}, u32[]{:S(2)}) collective-permute-start(bf16[4,2,128,128]{3,2,0,1:T(8,128)(2,1)S(1)} %collective-permute-done.26), channel_id=1, source_target_pairs={{0,1},{1,0},{2,3},{3,2},{4,5},{5,4},{6,7},{7,6},{8,9},{9,8},{10,11... | collective-permute-start | bytes 786440 | tf_op jit(solution)/shard_map/ppermute | solution.py:51
  67.1 10.6 %collective-permute-start.30 = (bf16[4,128,128]{2,1,0:T(8,128)(2,1)S(1)}, bf16[4,128,128]{2,1,0:T(8,128)(2,1)S(1)}, u32[]{:S(2)}, u32[]{:S(2)}) collective-permute-start(bf16[4,128,128]{2,1,0:T(8,128)(2,1)S(1)} %slice_bitcast_fusion), channel_id=1, source_target_pairs={{16,2},{17,3},{18,0},{19,1},{20,6},{21,7},{22,4},{23,5},{24,10},{2... | collective-permute-start | bytes 393224 | tf_op jit(solution)/shard_map/ppermute | solution.py:57
  72.0 16.8 %collective-permute-start.29 = (bf16[4,128,128]{2,1,0:T(8,128)(2,1)S(1)}, bf16[4,128,128]{2,1,0:T(8,128)(2,1)S(1)}, u32[]{:S(2)}, u32[]{:S(2)}) collective-permute-start(bf16[4,128,128]{2,1,0:T(8,128)(2,1)S(1)} %collective-permute-done.28.x_own), channel_id=1, source_target_pairs={{0,1},{1,0},{2,3},{3,2},{4,5},{5,4},{6,7},{7,6},{8,9},{9,8},{10,11... | collective-permute-start | bytes 393224 | tf_op jit(solution)/shard_map/ppermute | solution.py:51
  77.8 11.0 %collective-permute-start.31 = (bf16[4,128,128]{2,1,0:T(8,128)(2,1)S(1)}, bf16[4,128,128]{2,1,0:T(8,128)(2,1)S(1)}, u32[]{:S(2)}, u32[]{:S(2)}) collective-permute-start(bf16[4,128,128]{2,1,0:T(8,128)(2,1)S(1)} %collective-permute-done.30.d_own), channel_id=1, source_target_pairs={{0,1},{1,0},{2,3},{3,2},{4,5},{5,4},{6,7},{7,6},{8,9},{9,8},{10,11... | collective-permute-start | bytes 393224 | tf_op jit(solution)/shard_map/ppermute | solution.py:51
  (15 other events, 84.6 us)

commit v2 on v1

--- a/solution.py
+++ b/solution.py
@@ -72,6 +72,18 @@
                 plain[row * 64 : row * 64 + 64, to] = source[:, cols]
             for j in range(2):
                 crossed[j * 64 : j * 64 + 64, to] = cross[0, j, :, cols]
+
+
+def pair_kernel(own, other, pair):
+    pair[0] = own[...]
+    pair[1] = other[...]
+
+
+def row_kernel(own, *refs):
+    others, (row, lead) = refs[:3], refs[3:]
+    for k, part in enumerate((own, *others)):
+        row[k] = part[...]
+        lead[k] = part[0]
 
 
 def encode_kernel(*refs):
@@ -208,13 +220,13 @@
         [((192, depth // 2), bf16), ((128, depth // 2), bf16)] * 2,
         same_dec, next_dec, cross_dec,
     )
-    near = jnp.stack([resid_in, other])
+    far_s, far_x, lead_x, other = lax.optimization_barrier((far_s, far_x, own_x, other))
+    (near,) = run(pair_kernel, "pair", [((2, 2, 128, block), bf16)], resid_in, other)
     line = [near] + [to_lat(near, k * Z_STEP) for k in (1, 2, 3)]
-    own_s, own_x, far_s, far_x, _ = lax.optimization_barrier((own_s, own_x, far_s, far_x, other))
+    peer_x = to_lat(far_x, Y_STEP)
+    near_x = to_both(lead_x, SWAP, 0)
     peer_s = to_lat(far_s, Y_STEP)
-    near_x = to_both(own_x, DOWN, 0)
-    peer_x = to_both(far_x, [(1, 1)], Y_STEP)
-    diag_x = to_both(far_x, DOWN, Y_STEP)
+    diag_x = to_both(peer_x, SWAP, 0)
     pieces = line + [to_lat(piece, C_STEP) for piece in line]
     full, slope, act = run(
         encode_kernel, "encode",
@@ -237,11 +249,15 @@
     )
     parts = [to_lat(part, k * Z_STEP) for k, part in zip((1, 2, 3), parts)]
     (dy,) = run(misfit_kernel, "misfit", [((2, 128, block), bf16)], mine, *parts, mlp_out)
-    row = jnp.stack([dy] + [to_lat(dy, k * Z_STEP) for k in (1, 2, 3)])
+    row, lead = run(
+        row_kernel, "row",
+        [((4, 2, 128, block), bf16), ((4, 128, block), bf16)],
+        dy, *[to_lat(dy, k * Z_STEP) for k in (1, 2, 3)],
+    )
     row_core = to_lat(row, C_STEP)
     far = to_lat(row, Y_STEP)
-    x_own = to_both(row[:, 0], UP, 0)
-    d_own = to_both(row[:, 0], UP, Y_STEP)
+    x_own = to_both(lead, UP, 0)
+    d_own = to_both(lead, UP, Y_STEP)
     half, grad_own, to_y, to_x, to_d = run(
         act_grad_kernel, "act_grad",
         [((2, 128, depth // 2), bf16), ((3, 64, 128), f32)] + [((144, 128), bf16)] * 3,
@@ -255,6 +271,7 @@
         [((1, 1), f32), ((2, 64, depth), bf16), ((2, 64), f32)],
         grad_own, from_y, from_x, from_d, slope, full,
     )
+    far, x_own, d_own, _, _, _ = lax.optimization_barrier((far, x_own, d_own, from_y, from_x, from_d))
     far_core = to_lat(far, C_STEP)
     x_core = to_lat(x_own, C_STEP)
     d_core = to_lat(d_own, C_STEP)

time: 91.1 us -> 76.5 us (0.84)
  waiting for transfers between devices: 44.7 us -> 28.8 us
  starting transfers between devices: 36.2 us -> 37.6 us
    ppermute x23 -> x24, waiting for transfers between devices: 29.5 us -> 21.1 us  [to_lat(): lax.ppermute(value, 'lat', [(source, source ^ step) for source in range(l...]
    ppermute x9 -> x8, waiting for transfers between devices: 15.2 us -> 7.65 us  [to_both(): return lax.ppermute(value, ('sec', 'lat'), pairs)]
    ppermute x23 -> x24, starting transfers between devices: 20.7 us -> 22.7 us  [to_lat(): lax.ppermute(value, 'lat', [(source, source ^ step) for source in range(l...]
    unnamed x14 -> x16, local copies, waits for them, and re-layouts: 2.1 us -> 3.06 us
    ppermute x9 -> x8, starting transfers between devices: 15.5 us -> 14.9 us  [to_both(): return lax.ppermute(value, ('sec', 'lat'), pairs)]
    pallas_call x7 -> x9, Pallas kernels: 3.73 us -> 3.8 us  [run(): pl.pallas_call(kernel, name=name, out_shape=[jax.ShapeDtypeStruct(shape,...]
  transfers between devices with their start and end apart: 32 -> 32, of which waited for: 18 -> 16; matrix products, arithmetic and copies ran while one was open for 0% -> 0% of each run, Pallas kernels for 3% -> 4%
where the time goes in v2:
time: 76.5 us; the launch traced here: 76.2 us
  starting transfers between devices  37.6 us (49%)
  waiting for transfers between devices  28.8 us (38%)
  Pallas kernels  5.81 us (8%)
  local copies, waits for them, and re-layouts  3.2 us (4%)
  between operations  0.8 us (1%)
    ppermute x24, starting transfers between devices, to_lat(): lax.ppermute(value, 'lat', [(source, source ^ step) for source in range(l...  22.7 us
    ppermute x24, waiting for transfers between devices, to_lat(): lax.ppermute(value, 'lat', [(source, source ^ step) for source in range(l...  21.1 us
    ppermute x8, starting transfers between devices, to_both(): return lax.ppermute(value, ('sec', 'lat'), pairs)  14.9 us
    ppermute x8, waiting for transfers between devices, to_both(): return lax.ppermute(value, ('sec', 'lat'), pairs)  7.65 us
    pallas_call x9, Pallas kernels, run(): pl.pallas_call(kernel, name=name, out_shape=[jax.ShapeDtypeStruct(shape,...  3.8 us
    unnamed x16, local copies, waits for them, and re-layouts  3.06 us
    pallas_call x1, Pallas kernels, staged(): pl.pallas_call(decoder_grad_kernel, name='decoder_grad', out_shape=[jax.S...  2.01 us
  transfers between devices with their start and end apart: 32, of which 16 were waited for; matrix products, arithmetic and copies ran while one was open for 0% of the time, Pallas kernels for 4%

profile of v2, /device:TPU:0, one launch (start us, length us, event | category | flops | bytes accessed | tf_op | source)
XLA Modules:
  0.0 76.2 jit_solution(17619787732819471164)
XLA Ops:
  0.6 3.0 %collective-permute-start = (bf16[2,128,128]{2,1,0:T(8,128)(2,1)}, bf16[2,128,128]{2,1,0:T(8,128)(2,1)S(1)}, u32[]{:S(2)}, u32[]{:S(2)}) collective-permute-start(bf16[2,128,128]{2,1,0:T(8,128)(2,1)} %own.1), channel_id=1, source_target_pairs={{0,2},{1,3},{2,0},{3,1},{4,6},{5,7},{6,4},{7,5},{8,10},{9,11},{10,... | collective-permute-start | bytes 196616 | tf_op jit(solution)/shard_map/ppermute | solution.py:51
  8.2 1.6 %collective-permute-start.1 = (bf16[2,2,128,128]{3,2,1,0:T(8,128)(2,1)S(1)}, bf16[2,2,128,128]{3,2,1,0:T(8,128)(2,1)S(1)}, u32[]{:S(2)}, u32[]{:S(2)}) collective-permute-start(bf16[2,2,128,128]{3,2,1,0:T(8,128)(2,1)S(1)} %pair.1.refs_0_), channel_id=1, source_target_pairs={{0,4},{1,5},{2,6},{3,7},{4,0},{5,1},{6,2},{7,3},{8,12},{9,13},{10,... | collective-permute-start | bytes 393224 | tf_op jit(solution)/shard_map/ppermute | solution.py:51
  9.8 2.6 %collective-permute-start.2 = (bf16[2,2,128,128]{3,2,1,0:T(8,128)(2,1)S(1)}, bf16[2,2,128,128]{3,2,1,0:T(8,128)(2,1)S(1)}, u32[]{:S(2)}, u32[]{:S(2)}) collective-permute-start(bf16[2,2,128,128]{3,2,1,0:T(8,128)(2,1)S(1)} %pair.1.refs_0_), channel_id=1, source_target_pairs={{0,8},{1,9},{2,10},{3,11},{4,12},{5,13},{6,14},{7,15},{8,0},{9,1},... | collective-permute-start | bytes 393224 | tf_op jit(solution)/shard_map/ppermute | solution.py:51
  14.7 7.2 %collective-permute-done.2.refs_2_ = bf16[2,2,128,128]{3,2,1,0:T(8,128)(2,1)S(1)} collective-permute-done((bf16[2,2,128,128]{3,2,1,0:T(8,128)(2,1)S(1)}, bf16[2,2,128,128]{3,2,1,0:T(8,128)(2,1)S(1)}, u32[]{:S(2)}, u32[]{:S(2)}) %collective-permute-start.2) | collective-permute-done | bytes 131104 | tf_op jit(solution)/shard_map/ppermute | solution.py:51
  21.8 1.5 %collective-permute-start.13 = (bf16[128,1024]{1,0:T(8,128)(2,1)S(1)}, bf16[128,1024]{1,0:T(8,128)(2,1)S(1)}, u32[]{:S(2)}, u32[]{:S(2)}) collective-permute-start(bf16[128,1024]{1,0:T(8,128)(2,1)S(1)} %get-tuple-element.47.own_x), channel_id=1, source_target_pairs={{0,16},{1,17},{2,18},{3,19},{4,20},{5,21},{6,22},{7,23},{8,24},{9,... | collective-permute-start | bytes 786440 | tf_op jit(solution)/shard_map/ppermute | solution.py:57
  26.4 4.0 %collective-permute-start.10 = (bf16[2,64,128]{2,1,0:T(8,128)(2,1)S(1)}, bf16[2,64,128]{2,1,0:T(8,128)(2,1)S(1)}, u32[]{:S(2)}, u32[]{:S(2)}) collective-permute-start(bf16[2,64,128]{2,1,0:T(8,128)(2,1)S(1)} %get-tuple-element.43.act), channel_id=1, source_target_pairs={{0,18},{1,19},{2,16},{3,17},{4,22},{5,23},{6,20},{7,21},{8,26},{9,... | collective-permute-start | bytes 98312 | tf_op jit(solution)/shard_map/ppermute | solution.py:57
  31.3 3.0 %collective-permute-start.9 = (bf16[2,64,128]{2,1,0:T(8,128)(2,1)S(1)}, bf16[2,64,128]{2,1,0:T(8,128)(2,1)S(1)}, u32[]{:S(2)}, u32[]{:S(2)}) collective-permute-start(bf16[2,64,128]{2,1,0:T(8,128)(2,1)S(1)} %get-tuple-element.43.act), channel_id=1, source_target_pairs={{0,16},{1,17},{2,18},{3,19},{4,20},{5,21},{6,22},{7,23},{8,24},{9,... | collective-permute-start | bytes 98312 | tf_op jit(solution)/shard_map/ppermute | solution.py:57
  34.3 1.9 %collective-permute-done.10.act_d = bf16[2,64,128]{2,1,0:T(8,128)(2,1)S(1)} collective-permute-done((bf16[2,64,128]{2,1,0:T(8,128)(2,1)S(1)}, bf16[2,64,128]{2,1,0:T(8,128)(2,1)S(1)}, u32[]{:S(2)}, u32[]{:S(2)}) %collective-permute-start.10) | collective-permute-done | bytes 32800 | tf_op jit(solution)/shard_map/ppermute | solution.py:57
  37.4 1.5 %collective-permute-done.15.got = bf16[4,2,128,128]{3,2,1,0:T(8,128)(2,1)S(1)} collective-permute-done((bf16[4,2,128,128]{3,2,1,0:T(8,128)(2,1)S(1)}, bf16[4,2,128,128]{3,2,1,0:T(8,128)(2,1)S(1)}, u32[]{:S(2)}, u32[]{:S(2)}) %collective-permute-start.15) | collective-permute-done | bytes 262176 | tf_op jit(solution)/shard_map/ppermute | solution.py:51
  38.9 1.5 %collective-permute-start.16 = (bf16[2,128,128]{2,1,0:T(8,128)(2,1)S(1)}, bf16[2,128,128]{2,1,0:T(8,128)(2,1)S(1)}, u32[]{:S(2)}, u32[]{:S(2)}) collective-permute-start(bf16[2,128,128]{2,1,0:T(8,128)(2,1)S(1)} %get-tuple-element.51), channel_id=1, source_target_pairs={{0,4},{1,5},{2,6},{3,7},{4,0},{5,1},{6,2},{7,3},{8,12},{9,13},{10,... | collective-permute-start | bytes 196616 | tf_op jit(solution)/shard_map/ppermute | solution.py:51
  40.4 1.6 %collective-permute-start.17 = (bf16[2,128,128]{2,1,0:T(8,128)(2,1)S(1)}, bf16[2,128,128]{2,1,0:T(8,128)(2,1)S(1)}, u32[]{:S(2)}, u32[]{:S(2)}) collective-permute-start(bf16[2,128,128]{2,1,0:T(8,128)(2,1)S(1)} %get-tuple-element.52), channel_id=1, source_target_pairs={{0,8},{1,9},{2,10},{3,11},{4,12},{5,13},{6,14},{7,15},{8,0},{9,1},... | collective-permute-start | bytes 196616 | tf_op jit(solution)/shard_map/ppermute | solution.py:51
  42.0 1.3 %collective-permute-start.18 = (bf16[2,128,128]{2,1,0:T(8,128)(2,1)S(1)}, bf16[2,128,128]{2,1,0:T(8,128)(2,1)S(1)}, u32[]{:S(2)}, u32[]{:S(2)}) collective-permute-start(bf16[2,128,128]{2,1,0:T(8,128)(2,1)S(1)} %get-tuple-element.53), channel_id=1, source_target_pairs={{0,12},{1,13},{2,14},{3,15},{4,8},{5,9},{6,10},{7,11},{8,4},{9,5},... | collective-permute-start | bytes 196616 | tf_op jit(solution)/shard_map/ppermute | solution.py:51
  43.4 5.3 %collective-permute-done.17.g2 = bf16[2,128,128]{2,1,0:T(8,128)(2,1)S(1)} collective-permute-done((bf16[2,128,128]{2,1,0:T(8,128)(2,1)S(1)}, bf16[2,128,128]{2,1,0:T(8,128)(2,1)S(1)}, u32[]{:S(2)}, u32[]{:S(2)}) %collective-permute-start.17) | collective-permute-done | bytes 65568 | tf_op jit(solution)/shard_map/ppermute | solution.py:51
  48.7 1.4 %collective-permute-start.19 = (bf16[2,128,128]{2,1,0:T(8,128)(2,1)S(1)}, bf16[2,128,128]{2,1,0:T(8,128)(2,1)S(1)}, u32[]{:S(2)}, u32[]{:S(2)}) collective-permute-start(bf16[2,128,128]{2,1,0:T(8,128)(2,1)S(1)} %misfit.1.own), channel_id=1, source_target_pairs={{0,4},{1,5},{2,6},{3,7},{4,0},{5,1},{6,2},{7,3},{8,12},{9,13},{10,... | collective-permute-start | bytes 196616 | tf_op jit(solution)/shard_map/ppermute | solution.py:51
  50.1 1.4 %collective-permute-start.20 = (bf16[2,128,128]{2,1,0:T(8,128)(2,1)S(1)}, bf16[2,128,128]{2,1,0:T(8,128)(2,1)S(1)}, u32[]{:S(2)}, u32[]{:S(2)}) collective-permute-start(bf16[2,128,128]{2,1,0:T(8,128)(2,1)S(1)} %misfit.1.own), channel_id=1, source_target_pairs={{0,8},{1,9},{2,10},{3,11},{4,12},{5,13},{6,14},{7,15},{8,0},{9,1},... | collective-permute-start | bytes 196616 | tf_op jit(solution)/shard_map/ppermute | solution.py:51
  51.5 1.6 %collective-permute-start.21 = (bf16[2,128,128]{2,1,0:T(8,128)(2,1)S(1)}, bf16[2,128,128]{2,1,0:T(8,128)(2,1)S(1)}, u32[]{:S(2)}, u32[]{:S(2)}) collective-permute-start(bf16[2,128,128]{2,1,0:T(8,128)(2,1)S(1)} %misfit.1.own), channel_id=1, source_target_pairs={{0,12},{1,13},{2,14},{3,15},{4,8},{5,9},{6,10},{7,11},{8,4},{9,5},... | collective-permute-start | bytes 196616 | tf_op jit(solution)/shard_map/ppermute | solution.py:51
  53.8 4.0 %collective-permute-done.20.refs_1_ = bf16[2,128,128]{2,1,0:T(8,128)(2,1)S(1)} collective-permute-done((bf16[2,128,128]{2,1,0:T(8,128)(2,1)S(1)}, bf16[2,128,128]{2,1,0:T(8,128)(2,1)S(1)}, u32[]{:S(2)}, u32[]{:S(2)}) %collective-permute-start.20) | collective-permute-done | bytes 65568 | tf_op jit(solution)/shard_map/ppermute | solution.py:51
  57.9 1.3 %collective-permute-start.26 = (bf16[4,2,128,128]{3,2,1,0:T(8,128)(2,1)S(1)}, bf16[4,2,128,128]{3,2,1,0:T(8,128)(2,1)S(1)}, u32[]{:S(2)}, u32[]{:S(2)}) collective-permute-start(bf16[4,2,128,128]{3,2,1,0:T(8,128)(2,1)S(1)} %get-tuple-element.54.mine), channel_id=1, source_target_pairs={{0,2},{1,3},{2,0},{3,1},{4,6},{5,7},{6,4},{7,5},{8,10},{9,11},{10,... | collective-permute-start | bytes 786440 | tf_op jit(solution)/shard_map/ppermute | solution.py:51
  59.2 1.3 %collective-permute-start.27 = (bf16[4,128,128]{2,1,0:T(8,128)(2,1)S(1)}, bf16[4,128,128]{2,1,0:T(8,128)(2,1)S(1)}, u32[]{:S(2)}, u32[]{:S(2)}) collective-permute-start(bf16[4,128,128]{2,1,0:T(8,128)(2,1)S(1)} %get-tuple-element.65), channel_id=1, source_target_pairs={{16,0},{17,1},{18,2},{19,3},{20,4},{21,5},{22,6},{23,7},{24,8},{25... | collective-permute-start | bytes 393224 | tf_op jit(solution)/shard_map/ppermute | solution.py:57
  60.5 1.3 %collective-permute-start.28 = (bf16[4,128,128]{2,1,0:T(8,128)(2,1)S(1)}, bf16[4,128,128]{2,1,0:T(8,128)(2,1)S(1)}, u32[]{:S(2)}, u32[]{:S(2)}) collective-permute-start(bf16[4,128,128]{2,1,0:T(8,128)(2,1)S(1)} %get-tuple-element.65), channel_id=1, source_target_pairs={{16,2},{17,3},{18,0},{19,1},{20,6},{21,7},{22,4},{23,5},{24,10},{2... | collective-permute-start | bytes 393224 | tf_op jit(solution)/shard_map/ppermute | solution.py:57
  63.6 3.3 %collective-permute-start.24 = (bf16[144,128]{1,0:T(8,128)(2,1)S(1)}, bf16[144,128]{1,0:T(8,128)(2,1)S(1)}, u32[]{:S(2)}, u32[]{:S(2)}) collective-permute-start(bf16[144,128]{1,0:T(8,128)(2,1)S(1)} %get-tuple-element.57), channel_id=1, source_target_pairs={{0,16},{1,17},{2,18},{3,19},{4,20},{5,21},{6,22},{7,23},{8,24},{9,... | collective-permute-start | bytes 110600 | tf_op jit(solution)/shard_map/ppermute | solution.py:57
  67.4 3.1 %collective-permute-done.28.d_own = bf16[4,128,128]{2,1,0:T(8,128)(2,1)S(1)} collective-permute-done((bf16[4,128,128]{2,1,0:T(8,128)(2,1)S(1)}, bf16[4,128,128]{2,1,0:T(8,128)(2,1)S(1)}, u32[]{:S(2)}, u32[]{:S(2)}) %collective-permute-start.28) | collective-permute-done | bytes 131104 | tf_op jit(solution)/shard_map/ppermute | solution.py:57
  70.7 1.6 %collective-permute-done.25.from_d = bf16[144,128]{1,0:T(8,128)(2,1)S(1)} collective-permute-done((bf16[144,128]{1,0:T(8,128)(2,1)S(1)}, bf16[144,128]{1,0:T(8,128)(2,1)S(1)}, u32[]{:S(2)}, u32[]{:S(2)}) %collective-permute-start.25) | collective-permute-done | bytes 36896 | tf_op jit(solution)/shard_map/ppermute | solution.py:57
  74.2 2.0 %decoder_grad.1 = (bf16[2,64,2048]{2,1,0:T(8,128)(2,1)}, bf16[1,64,2048]{2,1,0:T(8,128)(2,1)}, bf16[1,2,64,2048]{3,2,1,0:T(8,128)(2,1)}) custom-call(bf16[2,64,128]{2,1,0:T(8,128)(2,1)S(1)} %get-tuple-element.43.act, bf16[2,64,128]{2,1,0:T(8,128)(2,1)S(1)} %collective-permute-done.9.act_x, bf16[2,128,1024]{2,1,0:T(8,128)(2,1)S(1)} %get-tuple-element.64.half, ...), custom_call_target="tpu_custom_call" | custom-call | tf_op jit(solution)/shard_map/decoder_grad/pallas_call | solution.py:280
  (69 shorter events, 16.9 us)
Async XLA Ops:
  0.6 6.3 %collective-permute-start = (bf16[2,128,128]{2,1,0:T(8,128)(2,1)}, bf16[2,128,128]{2,1,0:T(8,128)(2,1)S(1)}, u32[]{:S(2)}, u32[]{:S(2)}) collective-permute-start(bf16[2,128,128]{2,1,0:T(8,128)(2,1)} %own.1), channel_id=1, source_target_pairs={{0,2},{1,3},{2,0},{3,1},{4,6},{5,7},{6,4},{7,5},{8,10},{9,11},{10,... | collective-permute-start | bytes 196616 | tf_op jit(solution)/shard_map/ppermute | solution.py:51
  6.9 16.4 %collective-permute-start.12 = (bf16[128,1024]{1,0:T(8,128)(2,1)S(1)}, bf16[128,1024]{1,0:T(8,128)(2,1)S(1)}, u32[]{:S(2)}, u32[]{:S(2)}) collective-permute-start(bf16[128,1024]{1,0:T(8,128)(2,1)S(1)} %get-tuple-element.46), channel_id=1, source_target_pairs={{0,2},{1,3},{2,0},{3,1},{4,6},{5,7},{6,4},{7,5},{8,10},{9,11},{10,... | collective-permute-start | bytes 786440 | tf_op jit(solution)/shard_map/ppermute | solution.py:51
  8.2 6.5 %collective-permute-start.1 = (bf16[2,2,128,128]{3,2,1,0:T(8,128)(2,1)S(1)}, bf16[2,2,128,128]{3,2,1,0:T(8,128)(2,1)S(1)}, u32[]{:S(2)}, u32[]{:S(2)}) collective-permute-start(bf16[2,2,128,128]{3,2,1,0:T(8,128)(2,1)S(1)} %pair.1.refs_0_), channel_id=1, source_target_pairs={{0,4},{1,5},{2,6},{3,7},{4,0},{5,1},{6,2},{7,3},{8,12},{9,13},{10,... | collective-permute-start | bytes 393224 | tf_op jit(solution)/shard_map/ppermute | solution.py:51
  9.8 12.0 %collective-permute-start.2 = (bf16[2,2,128,128]{3,2,1,0:T(8,128)(2,1)S(1)}, bf16[2,2,128,128]{3,2,1,0:T(8,128)(2,1)S(1)}, u32[]{:S(2)}, u32[]{:S(2)}) collective-permute-start(bf16[2,2,128,128]{3,2,1,0:T(8,128)(2,1)S(1)} %pair.1.refs_0_), channel_id=1, source_target_pairs={{0,8},{1,9},{2,10},{3,11},{4,12},{5,13},{6,14},{7,15},{8,0},{9,1},... | collective-permute-start | bytes 393224 | tf_op jit(solution)/shard_map/ppermute | solution.py:51
  12.4 9.5 %collective-permute-start.3 = (bf16[2,2,128,128]{3,2,1,0:T(8,128)(2,1)S(1)}, bf16[2,2,128,128]{3,2,1,0:T(8,128)(2,1)S(1)}, u32[]{:S(2)}, u32[]{:S(2)}) collective-permute-start(bf16[2,2,128,128]{3,2,1,0:T(8,128)(2,1)S(1)} %pair.1.refs_0_), channel_id=1, source_target_pairs={{0,12},{1,13},{2,14},{3,15},{4,8},{5,9},{6,10},{7,11},{8,4},{9,5},... | collective-permute-start | bytes 393224 | tf_op jit(solution)/shard_map/ppermute | solution.py:51
  12.6 24.0 %collective-permute-start.11 = (bf16[192,1024]{1,0:T(8,128)(2,1)S(1)}, bf16[192,1024]{1,0:T(8,128)(2,1)S(1)}, u32[]{:S(2)}, u32[]{:S(2)}) collective-permute-start(bf16[192,1024]{1,0:T(8,128)(2,1)S(1)} %get-tuple-element.45), channel_id=1, source_target_pairs={{0,2},{1,3},{2,0},{3,1},{4,6},{5,7},{6,4},{7,5},{8,10},{9,11},{10,... | collective-permute-start | bytes 1179656 | tf_op jit(solution)/shard_map/ppermute | solution.py:51
  14.7 9.2 %collective-permute-start.4 = (bf16[2,2,128,128]{3,2,1,0:T(8,128)(2,1)S(1)}, bf16[2,2,128,128]{3,2,1,0:T(8,128)(2,1)S(1)}, u32[]{:S(2)}, u32[]{:S(2)}) collective-permute-start(bf16[2,2,128,128]{3,2,1,0:T(8,128)(2,1)S(1)} %pair.1.refs_0_), channel_id=1, source_target_pairs={{0,1},{1,0},{2,3},{3,2},{4,5},{5,4},{6,7},{7,6},{8,9},{9,8},{10,11... | collective-permute-start | bytes 393224 | tf_op jit(solution)/shard_map/ppermute | solution.py:51
  21.8 9.5 %collective-permute-start.13 = (bf16[128,1024]{1,0:T(8,128)(2,1)S(1)}, bf16[128,1024]{1,0:T(8,128)(2,1)S(1)}, u32[]{:S(2)}, u32[]{:S(2)}) collective-permute-start(bf16[128,1024]{1,0:T(8,128)(2,1)S(1)} %get-tuple-element.47.own_x), channel_id=1, source_target_pairs={{0,16},{1,17},{2,18},{3,19},{4,20},{5,21},{6,22},{7,23},{8,24},{9,... | collective-permute-start | bytes 786440 | tf_op jit(solution)/shard_map/ppermute | solution.py:57
  23.3 13.3 %collective-permute-start.14 = (bf16[128,1024]{1,0:T(8,128)(2,1)S(1)}, bf16[128,1024]{1,0:T(8,128)(2,1)S(1)}, u32[]{:S(2)}, u32[]{:S(2)}) collective-permute-start(bf16[128,1024]{1,0:T(8,128)(2,1)S(1)} %collective-permute-done.12.peer_x), channel_id=1, source_target_pairs={{0,16},{1,17},{2,18},{3,19},{4,20},{5,21},{6,22},{7,23},{8,24},{9,... | collective-permute-start | bytes 786440 | tf_op jit(solution)/shard_map/ppermute | solution.py:57
  26.4 9.9 %collective-permute-start.10 = (bf16[2,64,128]{2,1,0:T(8,128)(2,1)S(1)}, bf16[2,64,128]{2,1,0:T(8,128)(2,1)S(1)}, u32[]{:S(2)}, u32[]{:S(2)}) collective-permute-start(bf16[2,64,128]{2,1,0:T(8,128)(2,1)S(1)} %get-tuple-element.43.act), channel_id=1, source_target_pairs={{0,18},{1,19},{2,16},{3,17},{4,22},{5,23},{6,20},{7,21},{8,26},{9,... | collective-permute-start | bytes 98312 | tf_op jit(solution)/shard_map/ppermute | solution.py:57
  30.4 5.8 %collective-permute-start.8 = (bf16[2,64,128]{2,1,0:T(8,128)(2,1)S(1)}, bf16[2,64,128]{2,1,0:T(8,128)(2,1)S(1)}, u32[]{:S(2)}, u32[]{:S(2)}) collective-permute-start(bf16[2,64,128]{2,1,0:T(8,128)(2,1)S(1)} %get-tuple-element.43.act), channel_id=1, source_target_pairs={{0,2},{1,3},{2,0},{3,1},{4,6},{5,7},{6,4},{7,5},{8,10},{9,11},{10,... | collective-permute-start | bytes 98312 | tf_op jit(solution)/shard_map/ppermute | solution.py:51
  31.3 5.3 %collective-permute-start.9 = (bf16[2,64,128]{2,1,0:T(8,128)(2,1)S(1)}, bf16[2,64,128]{2,1,0:T(8,128)(2,1)S(1)}, u32[]{:S(2)}, u32[]{:S(2)}) collective-permute-start(bf16[2,64,128]{2,1,0:T(8,128)(2,1)S(1)} %get-tuple-element.43.act), channel_id=1, source_target_pairs={{0,16},{1,17},{2,18},{3,19},{4,20},{5,21},{6,22},{7,23},{8,24},{9,... | collective-permute-start | bytes 98312 | tf_op jit(solution)/shard_map/ppermute | solution.py:57
  38.9 4.5 %collective-permute-start.16 = (bf16[2,128,128]{2,1,0:T(8,128)(2,1)S(1)}, bf16[2,128,128]{2,1,0:T(8,128)(2,1)S(1)}, u32[]{:S(2)}, u32[]{:S(2)}) collective-permute-start(bf16[2,128,128]{2,1,0:T(8,128)(2,1)S(1)} %get-tuple-element.51), channel_id=1, source_target_pairs={{0,4},{1,5},{2,6},{3,7},{4,0},{5,1},{6,2},{7,3},{8,12},{9,13},{10,... | collective-permute-start | bytes 196616 | tf_op jit(solution)/shard_map/ppermute | solution.py:51
  40.4 8.2 %collective-permute-start.17 = (bf16[2,128,128]{2,1,0:T(8,128)(2,1)S(1)}, bf16[2,128,128]{2,1,0:T(8,128)(2,1)S(1)}, u32[]{:S(2)}, u32[]{:S(2)}) collective-permute-start(bf16[2,128,128]{2,1,0:T(8,128)(2,1)S(1)} %get-tuple-element.52), channel_id=1, source_target_pairs={{0,8},{1,9},{2,10},{3,11},{4,12},{5,13},{6,14},{7,15},{8,0},{9,1},... | collective-permute-start | bytes 196616 | tf_op jit(solution)/shard_map/ppermute | solution.py:51
  42.0 6.6 %collective-permute-start.18 = (bf16[2,128,128]{2,1,0:T(8,128)(2,1)S(1)}, bf16[2,128,128]{2,1,0:T(8,128)(2,1)S(1)}, u32[]{:S(2)}, u32[]{:S(2)}) collective-permute-start(bf16[2,128,128]{2,1,0:T(8,128)(2,1)S(1)} %get-tuple-element.53), channel_id=1, source_target_pairs={{0,12},{1,13},{2,14},{3,15},{4,8},{5,9},{6,10},{7,11},{8,4},{9,5},... | collective-permute-start | bytes 196616 | tf_op jit(solution)/shard_map/ppermute | solution.py:51
  48.7 5.0 %collective-permute-start.19 = (bf16[2,128,128]{2,1,0:T(8,128)(2,1)S(1)}, bf16[2,128,128]{2,1,0:T(8,128)(2,1)S(1)}, u32[]{:S(2)}, u32[]{:S(2)}) collective-permute-start(bf16[2,128,128]{2,1,0:T(8,128)(2,1)S(1)} %misfit.1.own), channel_id=1, source_target_pairs={{0,4},{1,5},{2,6},{3,7},{4,0},{5,1},{6,2},{7,3},{8,12},{9,13},{10,... | collective-permute-start | bytes 196616 | tf_op jit(solution)/shard_map/ppermute | solution.py:51
  50.1 7.7 %collective-permute-start.20 = (bf16[2,128,128]{2,1,0:T(8,128)(2,1)S(1)}, bf16[2,128,128]{2,1,0:T(8,128)(2,1)S(1)}, u32[]{:S(2)}, u32[]{:S(2)}) collective-permute-start(bf16[2,128,128]{2,1,0:T(8,128)(2,1)S(1)} %misfit.1.own), channel_id=1, source_target_pairs={{0,8},{1,9},{2,10},{3,11},{4,12},{5,13},{6,14},{7,15},{8,0},{9,1},... | collective-permute-start | bytes 196616 | tf_op jit(solution)/shard_map/ppermute | solution.py:51
  51.5 6.3 %collective-permute-start.21 = (bf16[2,128,128]{2,1,0:T(8,128)(2,1)S(1)}, bf16[2,128,128]{2,1,0:T(8,128)(2,1)S(1)}, u32[]{:S(2)}, u32[]{:S(2)}) collective-permute-start(bf16[2,128,128]{2,1,0:T(8,128)(2,1)S(1)} %misfit.1.own), channel_id=1, source_target_pairs={{0,12},{1,13},{2,14},{3,15},{4,8},{5,9},{6,10},{7,11},{8,4},{9,5},... | collective-permute-start | bytes 196616 | tf_op jit(solution)/shard_map/ppermute | solution.py:51
  57.9 12.6 %collective-permute-start.26 = (bf16[4,2,128,128]{3,2,1,0:T(8,128)(2,1)S(1)}, bf16[4,2,128,128]{3,2,1,0:T(8,128)(2,1)S(1)}, u32[]{:S(2)}, u32[]{:S(2)}) collective-permute-start(bf16[4,2,128,128]{3,2,1,0:T(8,128)(2,1)S(1)} %get-tuple-element.54.mine), channel_id=1, source_target_pairs={{0,2},{1,3},{2,0},{3,1},{4,6},{5,7},{6,4},{7,5},{8,10},{9,11},{10,... | collective-permute-start | bytes 786440 | tf_op jit(solution)/shard_map/ppermute | solution.py:51
  59.2 8.2 %collective-permute-start.27 = (bf16[4,128,128]{2,1,0:T(8,128)(2,1)S(1)}, bf16[4,128,128]{2,1,0:T(8,128)(2,1)S(1)}, u32[]{:S(2)}, u32[]{:S(2)}) collective-permute-start(bf16[4,128,128]{2,1,0:T(8,128)(2,1)S(1)} %get-tuple-element.65), channel_id=1, source_target_pairs={{16,0},{17,1},{18,2},{19,3},{20,4},{21,5},{22,6},{23,7},{24,8},{25... | collective-permute-start | bytes 393224 | tf_op jit(solution)/shard_map/ppermute | solution.py:57
  60.5 10.1 %collective-permute-start.28 = (bf16[4,128,128]{2,1,0:T(8,128)(2,1)S(1)}, bf16[4,128,128]{2,1,0:T(8,128)(2,1)S(1)}, u32[]{:S(2)}, u32[]{:S(2)}) collective-permute-start(bf16[4,128,128]{2,1,0:T(8,128)(2,1)S(1)} %get-tuple-element.65), channel_id=1, source_target_pairs={{16,2},{17,3},{18,0},{19,1},{20,6},{21,7},{22,4},{23,5},{24,10},{2... | collective-permute-start | bytes 393224 | tf_op jit(solution)/shard_map/ppermute | solution.py:57
  62.7 7.9 %collective-permute-start.23 = (bf16[144,128]{1,0:T(8,128)(2,1)S(1)}, bf16[144,128]{1,0:T(8,128)(2,1)S(1)}, u32[]{:S(2)}, u32[]{:S(2)}) collective-permute-start(bf16[144,128]{1,0:T(8,128)(2,1)S(1)} %get-tuple-element.56), channel_id=1, source_target_pairs={{0,2},{1,3},{2,0},{3,1},{4,6},{5,7},{6,4},{7,5},{8,10},{9,11},{10,... | collective-permute-start | bytes 110600 | tf_op jit(solution)/shard_map/ppermute | solution.py:51
  63.6 7.1 %collective-permute-start.24 = (bf16[144,128]{1,0:T(8,128)(2,1)S(1)}, bf16[144,128]{1,0:T(8,128)(2,1)S(1)}, u32[]{:S(2)}, u32[]{:S(2)}) collective-permute-start(bf16[144,128]{1,0:T(8,128)(2,1)S(1)} %get-tuple-element.57), channel_id=1, source_target_pairs={{0,16},{1,17},{2,18},{3,19},{4,20},{5,21},{6,22},{7,23},{8,24},{9,... | collective-permute-start | bytes 110600 | tf_op jit(solution)/shard_map/ppermute | solution.py:57
  67.4 4.9 %collective-permute-start.25 = (bf16[144,128]{1,0:T(8,128)(2,1)S(1)}, bf16[144,128]{1,0:T(8,128)(2,1)S(1)}, u32[]{:S(2)}, u32[]{:S(2)}) collective-permute-start(bf16[144,128]{1,0:T(8,128)(2,1)S(1)} %get-tuple-element.58), channel_id=1, source_target_pairs={{0,18},{1,19},{2,16},{3,17},{4,22},{5,23},{6,20},{7,21},{8,26},{9,... | collective-permute-start | bytes 110600 | tf_op jit(solution)/shard_map/ppermute | solution.py:57
  (16 other events, 67.2 us)

commit v3 on v2

--- a/solution.py
+++ b/solution.py
@@ -57,21 +57,37 @@
     return lax.ppermute(value, ("sec", "lat"), pairs)
 
 
-DOWN, UP, SWAP = [(0, 1)], [(1, 0)], [(0, 1), (1, 0)]
-
-
-def pack_kernel(same, nxt, cross, own_s, own_x, far_s, far_x):
+SWAP = [(0, 1), (1, 0)]
+
+
+def pack_kernel(same, nxt, cross, own_s, own_x, far_s, far_x, same_v, nxt_v, cross_v, sems):
     _, y, _ = place()
-    sources = [(same.at[1], 0), (nxt.at[0], 1), (same.at[0], 2)]
-    width = own_s.shape[1] // 4
-    for z in range(4):
-        to = slice(z * width, (z + 1) * width)
-        for half, (plain, crossed) in enumerate(((own_s, own_x), (far_s, far_x))):
-            cols = lanes(z * 2 * width + (y + half) % 2 * width, width)
-            for source, row in sources:
-                plain[row * 64 : row * 64 + 64, to] = source[:, cols]
-            for j in range(2):
-                crossed[j * 64 : j * 64 + 64, to] = cross[0, j, :, cols]
+    width = own_s.shape[-1] // 4
+    copies = [
+        pltpu.make_async_copy(source, target, sems.at[n])
+        for n, (source, target) in enumerate(((cross.at[0], cross_v), (same, same_v), (nxt.at[0], nxt_v)))
+    ]
+    for copy in copies:
+        copy.start()
+
+    def move(source, plain, row, crossed):
+        for z in range(4):
+            to = slice(z * width, (z + 1) * width)
+            for half, out in enumerate((plain, crossed)):
+                out[row, :, to] = source[:, lanes(z * 2 * width + (y + half) % 2 * width, width)]
+
+    copies[0].wait()
+    for j in range(2):
+        move(cross_v.at[j], own_x, j, far_x)
+    copies[1].wait()
+    for layer in range(2):
+        move(same_v.at[layer], own_s, layer, far_s)
+    copies[2].wait()
+    move(nxt_v, own_s, 2, far_s)
+
+
+def stacked(ref, first, last):
+    return ref[first:last].reshape((last - first) * ref.shape[1], ref.shape[2])
 
 
 def pair_kernel(own, other, pair):
@@ -87,15 +103,22 @@
 
 
 def encode_kernel(*refs):
-    pieces, (weight, bias, cut, full, slope, act) = refs[:8], refs[8:]
+    pieces, (weight, bias, cut, full, slope, act) = refs[:10], refs[10:]
     z, y, c = place()
     block = pieces[0].shape[-1]
-    for k in range(4):
-        for core in range(2):
+
+    def put(k, j, core, layer, value):
+        home = (z ^ k) * Z_STEP + (y ^ j) * Y_STEP + (c ^ core)
+        full[layer, :, lanes(home * block, block)] = value
+
+    for core in range(2):
+        mine, line1, line3, line2, line2_y = pieces[core * 5 : core * 5 + 5]
+        for layer in range(2):
             for j in range(2):
-                home = (z ^ k) * Z_STEP + (y ^ j) * Y_STEP + (c ^ core)
-                for layer in range(2):
-                    full[layer, :, lanes(home * block, block)] = pieces[core * 4 + k][j, layer]
+                for k, pair in ((0, mine), (1, line1), (3, line3)):
+                    put(k, j, core, layer, pair[j, layer])
+            put(2, 0, core, layer, line2[layer])
+            put(2, 1, core, layer, line2_y[layer])
     for layer in range(2):
         pre = dot_nt(weight[layer], full[layer]) + bias[layer]
         gate = jax.nn.sigmoid((pre - cut[layer]) / jump_width)
@@ -105,14 +128,17 @@
 
 def decode_kernel(act, act_y, act_x, act_d, own_s, own_x, peer_s, peer_x, near_x, diag_x, send, keep):
     _, _, c = place()
-    rows = lambda ref: ref.reshape(128, 128)
-    first = dot_tn(jnp.concatenate([act[0], act_y[0]]), jnp.concatenate([own_s[128:192], peer_s[128:192]]))
-    first += dot_tn(rows(act_x[...]), near_x[...])
-    first += dot_tn(rows(act_d[...]), diag_x[...])
-    second = dot_tn(jnp.concatenate([act[1], act[0]]), own_s[0:128])
-    second += dot_tn(jnp.concatenate([act_y[1], act_y[0]]), peer_s[0:128])
-    second += dot_tn(rows(act_x[...]), own_x[...])
-    second += dot_tn(rows(act_d[...]), peer_x[...])
+    leading = lax.axis_index("sec") == 0
+    across, diagonal = (
+        jnp.where(leading, jnp.zeros((128, 128), jnp.bfloat16), stacked(ref, 0, 2)) for ref in (act_x, act_d)
+    )
+    first = dot_tn(jnp.concatenate([act[0], act_y[0]]), jnp.concatenate([own_s[0], peer_s[0]]))
+    first += dot_tn(across, stacked(near_x, 0, 2))
+    first += dot_tn(diagonal, stacked(diag_x, 0, 2))
+    second = dot_tn(jnp.concatenate([act[1], act[0]]), stacked(own_s, 1, 3))
+    second += dot_tn(jnp.concatenate([act_y[1], act_y[0]]), stacked(peer_s, 1, 3))
+    second += dot_tn(across, stacked(own_x, 0, 2))
+    second += dot_tn(diagonal, stacked(peer_x, 0, 2))
     block = send.shape[-1]
     for layer, total in enumerate((first, second)):
         for z in range(4):
@@ -142,14 +168,14 @@
             half[layer, :, lanes(((z ^ k) * 2 + c) * block, block)] = mine[k, layer]
             half[layer, :, lanes(((z ^ k) * 2 + 1 - c) * block, block)] = core[k, layer]
     first, second = half[0], half[1]
-    a = dot_nt(own_s[0:128], second)
-    grad_own[0] = a[64:128] + dot_nt(own_s[128:192], first)
+    a = dot_nt(stacked(own_s, 1, 3), second)
+    grad_own[0] = a[64:128] + dot_nt(own_s[0], first)
     grad_own[1] = a[0:64]
-    a = dot_nt(peer_s[0:128], second)
-    to_y[0:64] = (a[64:128] + dot_nt(peer_s[128:192], first)).astype(jnp.bfloat16)
+    a = dot_nt(stacked(peer_s, 1, 3), second)
+    to_y[0:64] = (a[64:128] + dot_nt(peer_s[0], first)).astype(jnp.bfloat16)
     to_y[64:128] = a[0:64].astype(jnp.bfloat16)
-    to_x[0:128] = (dot_nt(own_x[...], second) + dot_nt(near_x[...], first)).astype(jnp.bfloat16)
-    to_d[0:128] = (dot_nt(peer_x[...], second) + dot_nt(diag_x[...], first)).astype(jnp.bfloat16)
+    to_x[0:128] = (dot_nt(stacked(own_x, 0, 2), second) + dot_nt(stacked(near_x, 0, 2), first)).astype(jnp.bfloat16)
+    to_d[0:128] = (dot_nt(stacked(peer_x, 0, 2), second) + dot_nt(stacked(diag_x, 0, 2), first)).astype(jnp.bfloat16)
     wide = half[...].astype(jnp.float32)
     squares = jnp.sum((wide * wide).reshape(-1, 8, wide.shape[-1]), axis=0)
     part = sum(squares[:, n * 128 : n * 128 + 128] for n in range(squares.shape[1] // 128))
@@ -215,27 +241,42 @@
     cut = jnp.broadcast_to(0.25 * thresholds.astype(f32)[:, :, None], (2, 64, 128))
 
     other = to_lat(resid_in, Y_STEP)
-    own_s, own_x, far_s, far_x = run(
-        pack_kernel, "pack",
-        [((192, depth // 2), bf16), ((128, depth // 2), bf16)] * 2,
-        same_dec, next_dec, cross_dec,
-    )
-    far_s, far_x, lead_x, other = lax.optimization_barrier((far_s, far_x, own_x, other))
+    line2 = to_lat(resid_in, 2 * Z_STEP)
+    shapes = [((3, 64, depth // 2), bf16), ((2, 64, depth // 2), bf16)] * 2
+    own_s, own_x, far_s, far_x = pl.pallas_call(
+        pack_kernel,
+        name="pack",
+        out_shape=[jax.ShapeDtypeStruct(shape, dtype) for shape, dtype in shapes],
+        in_specs=[pl.BlockSpec(memory_space=pl.ANY)] * 3,
+        out_specs=[VMEM] * 4,
+        scratch_shapes=[
+            pltpu.VMEM((2, 64, depth), bf16),
+            pltpu.VMEM((64, depth), bf16),
+            pltpu.VMEM((2, 64, depth), bf16),
+            pltpu.SemaphoreType.DMA((3,)),
+        ],
+    )(same_dec, next_dec, cross_dec)
     (near,) = run(pair_kernel, "pair", [((2, 2, 128, block), bf16)], resid_in, other)
-    line = [near] + [to_lat(near, k * Z_STEP) for k in (1, 2, 3)]
+    line1, line3 = (to_lat(near, k * Z_STEP) for k in (1, 3))
+    line2, far_x, _ = lax.optimization_barrier((line2, far_x, near))
+    line2_y = to_lat(line2, Y_STEP)
     peer_x = to_lat(far_x, Y_STEP)
+    lead_x, _ = lax.optimization_barrier((own_x, other))
     near_x = to_both(lead_x, SWAP, 0)
+    far_s, _, _ = lax.optimization_barrier((far_s, other, line2))
     peer_s = to_lat(far_s, Y_STEP)
     diag_x = to_both(peer_x, SWAP, 0)
-    pieces = line + [to_lat(piece, C_STEP) for piece in line]
+    line1, line3, near_x = lax.optimization_barrier((line1, line3, near_x))
+    pieces = [near, line1, line3, line2, line2_y]
+    pieces += [to_lat(piece, C_STEP) for piece in pieces]
     full, slope, act = run(
         encode_kernel, "encode",
         [((2, 128, depth), bf16), ((2, 64, 128), f32), ((2, 64, 128), bf16)],
         *pieces, tall, bias, cut,
     )
     act_y = to_lat(act, Y_STEP)
-    act_x = to_both(act, DOWN, 0)
-    act_d = to_both(act, DOWN, Y_STEP)
+    act_x = to_both(act, SWAP, 0)
+    act_d = to_both(act, SWAP, Y_STEP)
     send, keep = run(
         decode_kernel, "decode",
         [((4, 2, 128, block), bf16), ((4, 2, 128, block), f32)],
@@ -256,8 +297,8 @@
     )
     row_core = to_lat(row, C_STEP)
     far = to_lat(row, Y_STEP)
-    x_own = to_both(lead, UP, 0)
-    d_own = to_both(lead, UP, Y_STEP)
+    x_own = to_both(lead, SWAP, 0)
+    d_own = to_both(lead, SWAP, Y_STEP)
     half, grad_own, to_y, to_x, to_d = run(
         act_grad_kernel, "act_grad",
         [((2, 128, depth // 2), bf16), ((3, 64, 128), f32)] + [((144, 128), bf16)] * 3,

time: 76.5 us -> 70.1 us (0.916)
  local copies, waits for them, and re-layouts: 3.2 us -> 0.18 us
  starting transfers between devices: 37.6 us -> 34.7 us
  waiting for transfers between devices: 28.8 us -> 26.2 us
  Pallas kernels: 5.81 us -> 8.06 us
    ppermute x8, starting transfers between devices: 14.9 us -> 8.41 us  [to_both(): return lax.ppermute(value, ('sec', 'lat'), pairs)]
    ppermute x24 -> x26, starting transfers between devices: 22.7 us -> 26.2 us  [to_lat(): lax.ppermute(value, 'lat', [(source, source ^ step) for source in range(l...]
    unnamed x16 -> x14, local copies, waits for them, and re-layouts: 3.06 us -> 0.04 us
    pallas_call x0 -> x1, Pallas kernels: none -> 2.44 us  [staged(): pl.pallas_call(pack_kernel, name='pack', out_shape=[jax.ShapeDtypeStruct(...]
    ppermute x8, waiting for transfers between devices: 7.65 us -> 5.93 us  [to_both(): return lax.ppermute(value, ('sec', 'lat'), pairs)]
    ppermute x24 -> x26, waiting for transfers between devices: 21.1 us -> 20.3 us  [to_lat(): lax.ppermute(value, 'lat', [(source, source ^ step) for source in range(l...]
    pallas_call x9 -> x8, Pallas kernels: 3.8 us -> 3.61 us  [run(): pl.pallas_call(kernel, name=name, out_shape=[jax.ShapeDtypeStruct(shape,...]
  transfers between devices with their start and end apart: 32 -> 34, of which waited for: 16 -> 19; matrix products, arithmetic and copies ran while one was open for 0% -> 0% of each run, Pallas kernels for 4% -> 7%
where the time goes in v3:
time: 70.1 us; the launch traced here: 69.9 us
  starting transfers between devices  34.7 us (50%)
  waiting for transfers between devices  26.2 us (37%)
  Pallas kernels  8.06 us (11%)
  between operations  0.8 us (1%)
    ppermute x26, starting transfers between devices, to_lat(): lax.ppermute(value, 'lat', [(source, source ^ step) for source in range(l...  26.2 us
    ppermute x26, waiting for transfers between devices, to_lat(): lax.ppermute(value, 'lat', [(source, source ^ step) for source in range(l...  20.3 us
    ppermute x8, starting transfers between devices, to_both(): return lax.ppermute(value, ('sec', 'lat'), pairs)  8.41 us
    ppermute x8, waiting for transfers between devices, to_both(): return lax.ppermute(value, ('sec', 'lat'), pairs)  5.93 us
    pallas_call x8, Pallas kernels, run(): pl.pallas_call(kernel, name=name, out_shape=[jax.ShapeDtypeStruct(shape,...  3.61 us
    pallas_call x1, Pallas kernels, staged(): pl.pallas_call(pack_kernel, name='pack', out_shape=[jax.ShapeDtypeStruct(...  2.44 us
    pallas_call x1, Pallas kernels, staged(): pl.pallas_call(decoder_grad_kernel, name='decoder_grad', out_shape=[jax.S...  2.01 us
  transfers between devices with their start and end apart: 34, of which 19 were waited for; matrix products, arithmetic and copies ran while one was open for 0% of the time, Pallas kernels for 7%

profile of v3, /device:TPU:0, one launch (start us, length us, event | category | flops | bytes accessed | tf_op | source)
XLA Modules:
  0.0 69.9 jit_solution(7547015163309648511)
XLA Ops:
  0.6 3.0 %collective-permute-start = (bf16[2,128,128]{2,1,0:T(8,128)(2,1)}, bf16[2,128,128]{2,1,0:T(8,128)(2,1)S(1)}, u32[]{:S(2)}, u32[]{:S(2)}) collective-permute-start(bf16[2,128,128]{2,1,0:T(8,128)(2,1)} %own.1), channel_id=1, source_target_pairs={{0,2},{1,3},{2,0},{3,1},{4,6},{5,7},{6,4},{7,5},{8,10},{9,11},{10,... | collective-permute-start | bytes 196616 | tf_op jit(solution)/shard_map/ppermute | solution.py:51
  3.7 2.6 %collective-permute-start.4 = (bf16[2,128,128]{2,1,0:T(8,128)(2,1)}, bf16[2,128,128]{2,1,0:T(8,128)(2,1)S(1)}, u32[]{:S(2)}, u32[]{:S(2)}) collective-permute-start(bf16[2,128,128]{2,1,0:T(8,128)(2,1)} %own.1), channel_id=1, source_target_pairs={{0,8},{1,9},{2,10},{3,11},{4,12},{5,13},{6,14},{7,15},{8,0},{9,1},... | collective-permute-start | bytes 196616 | tf_op jit(solution)/shard_map/ppermute | solution.py:51
  6.3 2.4 %pack.1 = (bf16[3,64,1024]{2,1,0:T(8,128)(2,1)}, bf16[2,64,1024]{2,1,0:T(8,128)(2,1)}, bf16[3,64,1024]{2,1,0:T(8,128)(2,1)}, bf16[2,64,1024]{2,1,0:T(8,128)(2,1)}) custom-call(bf16[2,64,2048]{2,1,0:T(8,128)(2,1)} %same.1, bf16[1,64,2048]{2,1,0:T(8,128)(2,1)} %nxt.1, bf16[1,2,64,2048]{3,2,1,0:T(8,128)(2,1)} %cross.1), custom_call_target="tpu_custom_call" | custom-call | tf_op jit(solution)/shard_map/pack/pallas_call | solution.py:246
  9.9 1.5 %collective-permute-start.3 = (bf16[2,64,1024]{2,1,0:T(8,128)(2,1)S(1)}, bf16[2,64,1024]{2,1,0:T(8,128)(2,1)S(1)}, u32[]{:S(2)}, u32[]{:S(2)}) collective-permute-start(bf16[2,64,1024]{2,1,0:T(8,128)(2,1)S(1)} %copy-done.1), channel_id=1, source_target_pairs={{0,16},{1,17},{2,18},{3,19},{4,20},{5,21},{6,22},{7,23},{8,24},{9,... | collective-permute-start | bytes 786440 | tf_op jit(solution)/shard_map/ppermute | solution.py:57
  11.4 1.5 %collective-permute-start.5 = (bf16[2,128,128]{2,1,0:T(8,128)(2,1)S(1)}, bf16[2,128,128]{2,1,0:T(8,128)(2,1)S(1)}, u32[]{:S(2)}, u32[]{:S(2)}) collective-permute-start(bf16[2,128,128]{2,1,0:T(8,128)(2,1)S(1)} %collective-permute-done.4.refs_3_), channel_id=1, source_target_pairs={{0,2},{1,3},{2,0},{3,1},{4,6},{5,7},{6,4},{7,5},{8,10},{9,11},{10,... | collective-permute-start | bytes 196616 | tf_op jit(solution)/shard_map/ppermute | solution.py:51
  12.9 1.3 %collective-permute-start.1 = (bf16[2,2,128,128]{3,2,1,0:T(8,128)(2,1)S(1)}, bf16[2,2,128,128]{3,2,1,0:T(8,128)(2,1)S(1)}, u32[]{:S(2)}, u32[]{:S(2)}) collective-permute-start(bf16[2,2,128,128]{3,2,1,0:T(8,128)(2,1)S(1)} %pair.1.refs_0_), channel_id=1, source_target_pairs={{0,4},{1,5},{2,6},{3,7},{4,0},{5,1},{6,2},{7,3},{8,12},{9,13},{10,... | collective-permute-start | bytes 393224 | tf_op jit(solution)/shard_map/ppermute | solution.py:51
  14.2 2.6 %collective-permute-start.2 = (bf16[2,2,128,128]{3,2,1,0:T(8,128)(2,1)S(1)}, bf16[2,2,128,128]{3,2,1,0:T(8,128)(2,1)S(1)}, u32[]{:S(2)}, u32[]{:S(2)}) collective-permute-start(bf16[2,2,128,128]{3,2,1,0:T(8,128)(2,1)S(1)} %pair.1.refs_0_), channel_id=1, source_target_pairs={{0,12},{1,13},{2,14},{3,15},{4,8},{5,9},{6,10},{7,11},{8,4},{9,5},... | collective-permute-start | bytes 393224 | tf_op jit(solution)/shard_map/ppermute | solution.py:51
  19.3 1.9 %collective-permute-done.2.refs_2_ = bf16[2,2,128,128]{3,2,1,0:T(8,128)(2,1)S(1)} collective-permute-done((bf16[2,2,128,128]{3,2,1,0:T(8,128)(2,1)S(1)}, bf16[2,2,128,128]{3,2,1,0:T(8,128)(2,1)S(1)}, u32[]{:S(2)}, u32[]{:S(2)}) %collective-permute-start.2) | collective-permute-done | bytes 131104 | tf_op jit(solution)/shard_map/ppermute | solution.py:51
  25.6 1.3 %collective-permute-start.12 = (bf16[2,64,128]{2,1,0:T(8,128)(2,1)S(1)}, bf16[2,64,128]{2,1,0:T(8,128)(2,1)S(1)}, u32[]{:S(2)}, u32[]{:S(2)}) collective-permute-start(bf16[2,64,128]{2,1,0:T(8,128)(2,1)S(1)} %get-tuple-element.48.act), channel_id=1, source_target_pairs={{0,16},{1,17},{2,18},{3,19},{4,20},{5,21},{6,22},{7,23},{8,24},{9,... | collective-permute-start | bytes 98312 | tf_op jit(solution)/shard_map/ppermute | solution.py:57
  26.9 1.5 %collective-permute-start.13 = (bf16[2,64,128]{2,1,0:T(8,128)(2,1)S(1)}, bf16[2,64,128]{2,1,0:T(8,128)(2,1)S(1)}, u32[]{:S(2)}, u32[]{:S(2)}) collective-permute-start(bf16[2,64,128]{2,1,0:T(8,128)(2,1)S(1)} %get-tuple-element.48.act), channel_id=1, source_target_pairs={{0,18},{1,19},{2,16},{3,17},{4,22},{5,23},{6,20},{7,21},{8,26},{9,... | collective-permute-start | bytes 98312 | tf_op jit(solution)/shard_map/ppermute | solution.py:57
  28.8 2.2 %collective-permute-done.12.act_x = bf16[2,64,128]{2,1,0:T(8,128)(2,1)S(1)} collective-permute-done((bf16[2,64,128]{2,1,0:T(8,128)(2,1)S(1)}, bf16[2,64,128]{2,1,0:T(8,128)(2,1)S(1)}, u32[]{:S(2)}, u32[]{:S(2)}) %collective-permute-start.12) | collective-permute-done | bytes 32800 | tf_op jit(solution)/shard_map/ppermute | solution.py:57
  32.5 1.5 %collective-permute-done.17.got = bf16[4,2,128,128]{3,2,1,0:T(8,128)(2,1)S(1)} collective-permute-done((bf16[4,2,128,128]{3,2,1,0:T(8,128)(2,1)S(1)}, bf16[4,2,128,128]{3,2,1,0:T(8,128)(2,1)S(1)}, u32[]{:S(2)}, u32[]{:S(2)}) %collective-permute-start.17) | collective-permute-done | bytes 262176 | tf_op jit(solution)/shard_map/ppermute | solution.py:51
  34.9 2.0 %collective-permute-start.19 = (bf16[2,128,128]{2,1,0:T(8,128)(2,1)S(1)}, bf16[2,128,128]{2,1,0:T(8,128)(2,1)S(1)}, u32[]{:S(2)}, u32[]{:S(2)}) collective-permute-start(bf16[2,128,128]{2,1,0:T(8,128)(2,1)S(1)} %get-tuple-element.58), channel_id=1, source_target_pairs={{0,8},{1,9},{2,10},{3,11},{4,12},{5,13},{6,14},{7,15},{8,0},{9,1},... | collective-permute-start | bytes 196616 | tf_op jit(solution)/shard_map/ppermute | solution.py:51
  36.9 1.6 %collective-permute-start.20 = (bf16[2,128,128]{2,1,0:T(8,128)(2,1)S(1)}, bf16[2,128,128]{2,1,0:T(8,128)(2,1)S(1)}, u32[]{:S(2)}, u32[]{:S(2)}) collective-permute-start(bf16[2,128,128]{2,1,0:T(8,128)(2,1)S(1)} %get-tuple-element.59), channel_id=1, source_target_pairs={{0,12},{1,13},{2,14},{3,15},{4,8},{5,9},{6,10},{7,11},{8,4},{9,5},... | collective-permute-start | bytes 196616 | tf_op jit(solution)/shard_map/ppermute | solution.py:51
  38.5 4.7 %collective-permute-done.19.g2 = bf16[2,128,128]{2,1,0:T(8,128)(2,1)S(1)} collective-permute-done((bf16[2,128,128]{2,1,0:T(8,128)(2,1)S(1)}, bf16[2,128,128]{2,1,0:T(8,128)(2,1)S(1)}, u32[]{:S(2)}, u32[]{:S(2)}) %collective-permute-start.19) | collective-permute-done | bytes 65568 | tf_op jit(solution)/shard_map/ppermute | solution.py:51
  43.2 1.7 %collective-permute-start.21 = (bf16[2,128,128]{2,1,0:T(8,128)(2,1)S(1)}, bf16[2,128,128]{2,1,0:T(8,128)(2,1)S(1)}, u32[]{:S(2)}, u32[]{:S(2)}) collective-permute-start(bf16[2,128,128]{2,1,0:T(8,128)(2,1)S(1)} %misfit.1.own), channel_id=1, source_target_pairs={{0,4},{1,5},{2,6},{3,7},{4,0},{5,1},{6,2},{7,3},{8,12},{9,13},{10,... | collective-permute-start | bytes 196616 | tf_op jit(solution)/shard_map/ppermute | solution.py:51
  44.9 1.6 %collective-permute-start.22 = (bf16[2,128,128]{2,1,0:T(8,128)(2,1)S(1)}, bf16[2,128,128]{2,1,0:T(8,128)(2,1)S(1)}, u32[]{:S(2)}, u32[]{:S(2)}) collective-permute-start(bf16[2,128,128]{2,1,0:T(8,128)(2,1)S(1)} %misfit.1.own), channel_id=1, source_target_pairs={{0,8},{1,9},{2,10},{3,11},{4,12},{5,13},{6,14},{7,15},{8,0},{9,1},... | collective-permute-start | bytes 196616 | tf_op jit(solution)/shard_map/ppermute | solution.py:51
  47.7 5.1 %collective-permute-done.22.refs_1_ = bf16[2,128,128]{2,1,0:T(8,128)(2,1)S(1)} collective-permute-done((bf16[2,128,128]{2,1,0:T(8,128)(2,1)S(1)}, bf16[2,128,128]{2,1,0:T(8,128)(2,1)S(1)}, u32[]{:S(2)}, u32[]{:S(2)}) %collective-permute-start.22) | collective-permute-done | bytes 65568 | tf_op jit(solution)/shard_map/ppermute | solution.py:51
  52.9 1.6 %collective-permute-start.28 = (bf16[4,2,128,128]{3,2,1,0:T(8,128)(2,1)S(1)}, bf16[4,2,128,128]{3,2,1,0:T(8,128)(2,1)S(1)}, u32[]{:S(2)}, u32[]{:S(2)}) collective-permute-start(bf16[4,2,128,128]{3,2,1,0:T(8,128)(2,1)S(1)} %get-tuple-element.60.mine), channel_id=1, source_target_pairs={{0,2},{1,3},{2,0},{3,1},{4,6},{5,7},{6,4},{7,5},{8,10},{9,11},{10,... | collective-permute-start | bytes 786440 | tf_op jit(solution)/shard_map/ppermute | solution.py:51
  55.2 1.2 %collective-permute-start.30 = (bf16[4,128,128]{2,1,0:T(8,128)(2,1)S(1)}, bf16[4,128,128]{2,1,0:T(8,128)(2,1)S(1)}, u32[]{:S(2)}, u32[]{:S(2)}) collective-permute-start(bf16[4,128,128]{2,1,0:T(8,128)(2,1)S(1)} %get-tuple-element.71), channel_id=1, source_target_pairs={{0,18},{1,19},{2,16},{3,17},{4,22},{5,23},{6,20},{7,21},{8,26},{9,... | collective-permute-start | bytes 393224 | tf_op jit(solution)/shard_map/ppermute | solution.py:57
  57.3 1.6 %collective-permute-start.25 = (bf16[144,128]{1,0:T(8,128)(2,1)S(1)}, bf16[144,128]{1,0:T(8,128)(2,1)S(1)}, u32[]{:S(2)}, u32[]{:S(2)}) collective-permute-start(bf16[144,128]{1,0:T(8,128)(2,1)S(1)} %get-tuple-element.62), channel_id=1, source_target_pairs={{0,2},{1,3},{2,0},{3,1},{4,6},{5,7},{6,4},{7,5},{8,10},{9,11},{10,... | collective-permute-start | bytes 110600 | tf_op jit(solution)/shard_map/ppermute | solution.py:51
  61.7 1.9 %collective-permute-done.30.d_own = bf16[4,128,128]{2,1,0:T(8,128)(2,1)S(1)} collective-permute-done((bf16[4,128,128]{2,1,0:T(8,128)(2,1)S(1)}, bf16[4,128,128]{2,1,0:T(8,128)(2,1)S(1)}, u32[]{:S(2)}, u32[]{:S(2)}) %collective-permute-start.30) | collective-permute-done | bytes 131104 | tf_op jit(solution)/shard_map/ppermute | solution.py:57
  63.5 1.6 %collective-permute-done.28.far = bf16[4,2,128,128]{3,2,1,0:T(8,128)(2,1)S(1)} collective-permute-done((bf16[4,2,128,128]{3,2,1,0:T(8,128)(2,1)S(1)}, bf16[4,2,128,128]{3,2,1,0:T(8,128)(2,1)S(1)}, u32[]{:S(2)}, u32[]{:S(2)}) %collective-permute-start.28) | collective-permute-done | bytes 262176 | tf_op jit(solution)/shard_map/ppermute | solution.py:51
  67.9 2.0 %decoder_grad.1 = (bf16[2,64,2048]{2,1,0:T(8,128)(2,1)}, bf16[1,64,2048]{2,1,0:T(8,128)(2,1)}, bf16[1,2,64,2048]{3,2,1,0:T(8,128)(2,1)}) custom-call(bf16[2,64,128]{2,1,0:T(8,128)(2,1)S(1)} %get-tuple-element.48.act, bf16[2,64,128]{2,1,0:T(8,128)(2,1)S(1)} %collective-permute-done.12.act_x, bf16[2,128,1024]{2,1,0:T(8,128)(2,1)S(1)} %get-tuple-element.70.half, ...), custom_call_target="tpu_custom_call" | custom-call | tf_op jit(solution)/shard_map/decoder_grad/pallas_call | solution.py:321
  (71 shorter events, 19.3 us)
Async XLA Ops:
  0.6 8.1 %collective-permute-start = (bf16[2,128,128]{2,1,0:T(8,128)(2,1)}, bf16[2,128,128]{2,1,0:T(8,128)(2,1)S(1)}, u32[]{:S(2)}, u32[]{:S(2)}) collective-permute-start(bf16[2,128,128]{2,1,0:T(8,128)(2,1)} %own.1), channel_id=1, source_target_pairs={{0,2},{1,3},{2,0},{3,1},{4,6},{5,7},{6,4},{7,5},{8,10},{9,11},{10,... | collective-permute-start | bytes 196616 | tf_op jit(solution)/shard_map/ppermute | solution.py:51
  3.7 5.7 %collective-permute-start.4 = (bf16[2,128,128]{2,1,0:T(8,128)(2,1)}, bf16[2,128,128]{2,1,0:T(8,128)(2,1)S(1)}, u32[]{:S(2)}, u32[]{:S(2)}) collective-permute-start(bf16[2,128,128]{2,1,0:T(8,128)(2,1)} %own.1), channel_id=1, source_target_pairs={{0,8},{1,9},{2,10},{3,11},{4,12},{5,13},{6,14},{7,15},{8,0},{9,1},... | collective-permute-start | bytes 196616 | tf_op jit(solution)/shard_map/ppermute | solution.py:51
  9.4 11.8 %collective-permute-start.15 = (bf16[2,64,1024]{2,1,0:T(8,128)(2,1)}, bf16[2,64,1024]{2,1,0:T(8,128)(2,1)S(1)}, u32[]{:S(2)}, u32[]{:S(2)}) collective-permute-start(bf16[2,64,1024]{2,1,0:T(8,128)(2,1)} %get-tuple-element.52), channel_id=1, source_target_pairs={{0,2},{1,3},{2,0},{3,1},{4,6},{5,7},{6,4},{7,5},{8,10},{9,11},{10,... | collective-permute-start | bytes 786440 | tf_op jit(solution)/shard_map/ppermute | solution.py:51
  9.9 11.9 %collective-permute-start.3 = (bf16[2,64,1024]{2,1,0:T(8,128)(2,1)S(1)}, bf16[2,64,1024]{2,1,0:T(8,128)(2,1)S(1)}, u32[]{:S(2)}, u32[]{:S(2)}) collective-permute-start(bf16[2,64,1024]{2,1,0:T(8,128)(2,1)S(1)} %copy-done.1), channel_id=1, source_target_pairs={{0,16},{1,17},{2,18},{3,19},{4,20},{5,21},{6,22},{7,23},{8,24},{9,... | collective-permute-start | bytes 786440 | tf_op jit(solution)/shard_map/ppermute | solution.py:57
  11.4 6.6 %collective-permute-start.5 = (bf16[2,128,128]{2,1,0:T(8,128)(2,1)S(1)}, bf16[2,128,128]{2,1,0:T(8,128)(2,1)S(1)}, u32[]{:S(2)}, u32[]{:S(2)}) collective-permute-start(bf16[2,128,128]{2,1,0:T(8,128)(2,1)S(1)} %collective-permute-done.4.refs_3_), channel_id=1, source_target_pairs={{0,2},{1,3},{2,0},{3,1},{4,6},{5,7},{6,4},{7,5},{8,10},{9,11},{10,... | collective-permute-start | bytes 196616 | tf_op jit(solution)/shard_map/ppermute | solution.py:51
  12.9 6.4 %collective-permute-start.1 = (bf16[2,2,128,128]{3,2,1,0:T(8,128)(2,1)S(1)}, bf16[2,2,128,128]{3,2,1,0:T(8,128)(2,1)S(1)}, u32[]{:S(2)}, u32[]{:S(2)}) collective-permute-start(bf16[2,2,128,128]{3,2,1,0:T(8,128)(2,1)S(1)} %pair.1.refs_0_), channel_id=1, source_target_pairs={{0,4},{1,5},{2,6},{3,7},{4,0},{5,1},{6,2},{7,3},{8,12},{9,13},{10,... | collective-permute-start | bytes 393224 | tf_op jit(solution)/shard_map/ppermute | solution.py:51
  14.2 7.1 %collective-permute-start.2 = (bf16[2,2,128,128]{3,2,1,0:T(8,128)(2,1)S(1)}, bf16[2,2,128,128]{3,2,1,0:T(8,128)(2,1)S(1)}, u32[]{:S(2)}, u32[]{:S(2)}) collective-permute-start(bf16[2,2,128,128]{3,2,1,0:T(8,128)(2,1)S(1)} %pair.1.refs_0_), channel_id=1, source_target_pairs={{0,12},{1,13},{2,14},{3,15},{4,8},{5,9},{6,10},{7,11},{8,4},{9,5},... | collective-permute-start | bytes 393224 | tf_op jit(solution)/shard_map/ppermute | solution.py:51
  17.9 10.4 %collective-permute-start.14 = (bf16[3,64,1024]{2,1,0:T(8,128)(2,1)}, bf16[3,64,1024]{2,1,0:T(8,128)(2,1)S(1)}, u32[]{:S(2)}, u32[]{:S(2)}) collective-permute-start(bf16[3,64,1024]{2,1,0:T(8,128)(2,1)} %get-tuple-element.51), channel_id=1, source_target_pairs={{0,2},{1,3},{2,0},{3,1},{4,6},{5,7},{6,4},{7,5},{8,10},{9,11},{10,... | collective-permute-start | bytes 1179656 | tf_op jit(solution)/shard_map/ppermute | solution.py:51
  21.2 10.5 %collective-permute-start.16 = (bf16[2,64,1024]{2,1,0:T(8,128)(2,1)S(1)}, bf16[2,64,1024]{2,1,0:T(8,128)(2,1)S(1)}, u32[]{:S(2)}, u32[]{:S(2)}) collective-permute-start(bf16[2,64,1024]{2,1,0:T(8,128)(2,1)S(1)} %collective-permute-done.15.peer_x), channel_id=1, source_target_pairs={{0,16},{1,17},{2,18},{3,19},{4,20},{5,21},{6,22},{7,23},{8,24},{9,... | collective-permute-start | bytes 786440 | tf_op jit(solution)/shard_map/ppermute | solution.py:57
  24.8 4.0 %collective-permute-start.11 = (bf16[2,64,128]{2,1,0:T(8,128)(2,1)S(1)}, bf16[2,64,128]{2,1,0:T(8,128)(2,1)S(1)}, u32[]{:S(2)}, u32[]{:S(2)}) collective-permute-start(bf16[2,64,128]{2,1,0:T(8,128)(2,1)S(1)} %get-tuple-element.48.act), channel_id=1, source_target_pairs={{0,2},{1,3},{2,0},{3,1},{4,6},{5,7},{6,4},{7,5},{8,10},{9,11},{10,... | collective-permute-start | bytes 98312 | tf_op jit(solution)/shard_map/ppermute | solution.py:51
  25.6 5.4 %collective-permute-start.12 = (bf16[2,64,128]{2,1,0:T(8,128)(2,1)S(1)}, bf16[2,64,128]{2,1,0:T(8,128)(2,1)S(1)}, u32[]{:S(2)}, u32[]{:S(2)}) collective-permute-start(bf16[2,64,128]{2,1,0:T(8,128)(2,1)S(1)} %get-tuple-element.48.act), channel_id=1, source_target_pairs={{0,16},{1,17},{2,18},{3,19},{4,20},{5,21},{6,22},{7,23},{8,24},{9,... | collective-permute-start | bytes 98312 | tf_op jit(solution)/shard_map/ppermute | solution.py:57
  26.9 4.8 %collective-permute-start.13 = (bf16[2,64,128]{2,1,0:T(8,128)(2,1)S(1)}, bf16[2,64,128]{2,1,0:T(8,128)(2,1)S(1)}, u32[]{:S(2)}, u32[]{:S(2)}) collective-permute-start(bf16[2,64,128]{2,1,0:T(8,128)(2,1)S(1)} %get-tuple-element.48.act), channel_id=1, source_target_pairs={{0,18},{1,19},{2,16},{3,17},{4,22},{5,23},{6,20},{7,21},{8,26},{9,... | collective-permute-start | bytes 98312 | tf_op jit(solution)/shard_map/ppermute | solution.py:57
  34.0 4.5 %collective-permute-start.18 = (bf16[2,128,128]{2,1,0:T(8,128)(2,1)S(1)}, bf16[2,128,128]{2,1,0:T(8,128)(2,1)S(1)}, u32[]{:S(2)}, u32[]{:S(2)}) collective-permute-start(bf16[2,128,128]{2,1,0:T(8,128)(2,1)S(1)} %get-tuple-element.57), channel_id=1, source_target_pairs={{0,4},{1,5},{2,6},{3,7},{4,0},{5,1},{6,2},{7,3},{8,12},{9,13},{10,... | collective-permute-start | bytes 196616 | tf_op jit(solution)/shard_map/ppermute | solution.py:51
  34.9 8.2 %collective-permute-start.19 = (bf16[2,128,128]{2,1,0:T(8,128)(2,1)S(1)}, bf16[2,128,128]{2,1,0:T(8,128)(2,1)S(1)}, u32[]{:S(2)}, u32[]{:S(2)}) collective-permute-start(bf16[2,128,128]{2,1,0:T(8,128)(2,1)S(1)} %get-tuple-element.58), channel_id=1, source_target_pairs={{0,8},{1,9},{2,10},{3,11},{4,12},{5,13},{6,14},{7,15},{8,0},{9,1},... | collective-permute-start | bytes 196616 | tf_op jit(solution)/shard_map/ppermute | solution.py:51
  36.9 6.3 %collective-permute-start.20 = (bf16[2,128,128]{2,1,0:T(8,128)(2,1)S(1)}, bf16[2,128,128]{2,1,0:T(8,128)(2,1)S(1)}, u32[]{:S(2)}, u32[]{:S(2)}) collective-permute-start(bf16[2,128,128]{2,1,0:T(8,128)(2,1)S(1)} %get-tuple-element.59), channel_id=1, source_target_pairs={{0,12},{1,13},{2,14},{3,15},{4,8},{5,9},{6,10},{7,11},{8,4},{9,5},... | collective-permute-start | bytes 196616 | tf_op jit(solution)/shard_map/ppermute | solution.py:51
  43.2 4.5 %collective-permute-start.21 = (bf16[2,128,128]{2,1,0:T(8,128)(2,1)S(1)}, bf16[2,128,128]{2,1,0:T(8,128)(2,1)S(1)}, u32[]{:S(2)}, u32[]{:S(2)}) collective-permute-start(bf16[2,128,128]{2,1,0:T(8,128)(2,1)S(1)} %misfit.1.own), channel_id=1, source_target_pairs={{0,4},{1,5},{2,6},{3,7},{4,0},{5,1},{6,2},{7,3},{8,12},{9,13},{10,... | collective-permute-start | bytes 196616 | tf_op jit(solution)/shard_map/ppermute | solution.py:51
  44.9 7.9 %collective-permute-start.22 = (bf16[2,128,128]{2,1,0:T(8,128)(2,1)S(1)}, bf16[2,128,128]{2,1,0:T(8,128)(2,1)S(1)}, u32[]{:S(2)}, u32[]{:S(2)}) collective-permute-start(bf16[2,128,128]{2,1,0:T(8,128)(2,1)S(1)} %misfit.1.own), channel_id=1, source_target_pairs={{0,8},{1,9},{2,10},{3,11},{4,12},{5,13},{6,14},{7,15},{8,0},{9,1},... | collective-permute-start | bytes 196616 | tf_op jit(solution)/shard_map/ppermute | solution.py:51
  46.5 6.3 %collective-permute-start.23 = (bf16[2,128,128]{2,1,0:T(8,128)(2,1)S(1)}, bf16[2,128,128]{2,1,0:T(8,128)(2,1)S(1)}, u32[]{:S(2)}, u32[]{:S(2)}) collective-permute-start(bf16[2,128,128]{2,1,0:T(8,128)(2,1)S(1)} %misfit.1.own), channel_id=1, source_target_pairs={{0,12},{1,13},{2,14},{3,15},{4,8},{5,9},{6,10},{7,11},{8,4},{9,5},... | collective-permute-start | bytes 196616 | tf_op jit(solution)/shard_map/ppermute | solution.py:51
  52.9 12.3 %collective-permute-start.28 = (bf16[4,2,128,128]{3,2,1,0:T(8,128)(2,1)S(1)}, bf16[4,2,128,128]{3,2,1,0:T(8,128)(2,1)S(1)}, u32[]{:S(2)}, u32[]{:S(2)}) collective-permute-start(bf16[4,2,128,128]{3,2,1,0:T(8,128)(2,1)S(1)} %get-tuple-element.60.mine), channel_id=1, source_target_pairs={{0,2},{1,3},{2,0},{3,1},{4,6},{5,7},{6,4},{7,5},{8,10},{9,11},{10,... | collective-permute-start | bytes 786440 | tf_op jit(solution)/shard_map/ppermute | solution.py:51
  54.4 6.3 %collective-permute-start.29 = (bf16[4,128,128]{2,1,0:T(8,128)(2,1)S(1)}, bf16[4,128,128]{2,1,0:T(8,128)(2,1)S(1)}, u32[]{:S(2)}, u32[]{:S(2)}) collective-permute-start(bf16[4,128,128]{2,1,0:T(8,128)(2,1)S(1)} %get-tuple-element.71), channel_id=1, source_target_pairs={{0,16},{1,17},{2,18},{3,19},{4,20},{5,21},{6,22},{7,23},{8,24},{9,... | collective-permute-start | bytes 393224 | tf_op jit(solution)/shard_map/ppermute | solution.py:57
  55.2 8.4 %collective-permute-start.30 = (bf16[4,128,128]{2,1,0:T(8,128)(2,1)S(1)}, bf16[4,128,128]{2,1,0:T(8,128)(2,1)S(1)}, u32[]{:S(2)}, u32[]{:S(2)}) collective-permute-start(bf16[4,128,128]{2,1,0:T(8,128)(2,1)S(1)} %get-tuple-element.71), channel_id=1, source_target_pairs={{0,18},{1,19},{2,16},{3,17},{4,22},{5,23},{6,20},{7,21},{8,26},{9,... | collective-permute-start | bytes 393224 | tf_op jit(solution)/shard_map/ppermute | solution.py:57
  57.3 8.7 %collective-permute-start.25 = (bf16[144,128]{1,0:T(8,128)(2,1)S(1)}, bf16[144,128]{1,0:T(8,128)(2,1)S(1)}, u32[]{:S(2)}, u32[]{:S(2)}) collective-permute-start(bf16[144,128]{1,0:T(8,128)(2,1)S(1)} %get-tuple-element.62), channel_id=1, source_target_pairs={{0,2},{1,3},{2,0},{3,1},{4,6},{5,7},{6,4},{7,5},{8,10},{9,11},{10,... | collective-permute-start | bytes 110600 | tf_op jit(solution)/shard_map/ppermute | solution.py:51
  58.9 7.1 %collective-permute-start.26 = (bf16[144,128]{1,0:T(8,128)(2,1)S(1)}, bf16[144,128]{1,0:T(8,128)(2,1)S(1)}, u32[]{:S(2)}, u32[]{:S(2)}) collective-permute-start(bf16[144,128]{1,0:T(8,128)(2,1)S(1)} %get-tuple-element.63), channel_id=1, source_target_pairs={{0,16},{1,17},{2,18},{3,19},{4,20},{5,21},{6,22},{7,23},{8,24},{9,... | collective-permute-start | bytes 110600 | tf_op jit(solution)/shard_map/ppermute | solution.py:57
  60.8 5.2 %collective-permute-start.27 = (bf16[144,128]{1,0:T(8,128)(2,1)S(1)}, bf16[144,128]{1,0:T(8,128)(2,1)S(1)}, u32[]{:S(2)}, u32[]{:S(2)}) collective-permute-start(bf16[144,128]{1,0:T(8,128)(2,1)S(1)} %get-tuple-element.64), channel_id=1, source_target_pairs={{0,18},{1,19},{2,16},{3,17},{4,22},{5,23},{6,20},{7,21},{8,26},{9,... | collective-permute-start | bytes 110600 | tf_op jit(solution)/shard_map/ppermute | solution.py:57
  (17 other events, 76.2 us)

commit v4 on v3

--- a/solution.py
+++ b/solution.py
@@ -95,15 +95,25 @@
     pair[1] = other[...]
 
 
-def row_kernel(own, *refs):
-    others, (row, lead) = refs[:3], refs[3:]
-    for k, part in enumerate((own, *others)):
-        row[k] = part[...]
+def relay_kernel(line1, line3, lines):
+    lines[0] = line1[...]
+    lines[1] = line3[...]
+
+
+def row_kernel(one, two, row):
+    row[0] = one[...]
+    row[1] = two[...]
+
+
+def last_kernel(own, line1, line2, line3, row, lead):
+    row[0] = line2[...]
+    row[1] = line3[...]
+    for k, part in enumerate((own, line1, line2, line3)):
         lead[k] = part[0]
 
 
 def encode_kernel(*refs):
-    pieces, (weight, bias, cut, full, slope, act) = refs[:10], refs[10:]
+    pieces, (weight, bias, cut, full, slope, act) = refs[:8], refs[8:]
     z, y, c = place()
     block = pieces[0].shape[-1]
 
@@ -112,11 +122,12 @@
         full[layer, :, lanes(home * block, block)] = value
 
     for core in range(2):
-        mine, line1, line3, line2, line2_y = pieces[core * 5 : core * 5 + 5]
+        mine, lines, line2, line2_y = pieces[core * 4 : core * 4 + 4]
         for layer in range(2):
             for j in range(2):
-                for k, pair in ((0, mine), (1, line1), (3, line3)):
-                    put(k, j, core, layer, pair[j, layer])
+                put(0, j, core, layer, mine[j, layer])
+                put(1, j, core, layer, lines[0, j, layer])
+                put(3, j, core, layer, lines[1, j, layer])
             put(2, 0, core, layer, line2[layer])
             put(2, 1, core, layer, line2_y[layer])
     for layer in range(2):
@@ -160,13 +171,14 @@
     dy[...] = (total - target[...].astype(jnp.float32)).astype(jnp.bfloat16)
 
 
-def act_grad_kernel(mine, core, own_s, own_x, peer_s, peer_x, near_x, diag_x, half, grad_own, to_y, to_x, to_d):
+def act_grad_kernel(near, near_core, last, last_core, own_s, own_x, peer_s, peer_x, near_x, diag_x, half, grad_own, to_y, to_x, to_d):
     z, _, c = place()
-    block = mine.shape[-1]
+    block = near.shape[-1]
     for k in range(4):
+        mine, core = ((near, near_core), (last, last_core))[k // 2]
         for layer in range(2):
-            half[layer, :, lanes(((z ^ k) * 2 + c) * block, block)] = mine[k, layer]
-            half[layer, :, lanes(((z ^ k) * 2 + 1 - c) * block, block)] = core[k, layer]
+            half[layer, :, lanes(((z ^ k) * 2 + c) * block, block)] = mine[k % 2, layer]
+            half[layer, :, lanes(((z ^ k) * 2 + 1 - c) * block, block)] = core[k % 2, layer]
     first, second = half[0], half[1]
     a = dot_nt(stacked(own_s, 1, 3), second)
     grad_own[0] = a[64:128] + dot_nt(own_s[0], first)
@@ -200,7 +212,7 @@
         grad_enc[layer] = dot_nn(pre_grad.astype(jnp.bfloat16), full[layer]).astype(jnp.bfloat16)
 
 
-def decoder_grad_kernel(act, act_x, half, far, far_core, x_own, x_core, d_own, d_core, grad_same, grad_next, grad_cross, dy, dx):
+def decoder_grad_kernel(act, act_x, half, far, last, far_core, last_core, x_own, x_core, d_own, d_core, grad_same, grad_next, grad_cross, dy, dx):
     z, y, c = place()
     leading = lax.axis_index("sec") == 0
     block = far.shape[-1]
@@ -209,8 +221,9 @@
             dy[layer, :, lanes((n * 2 + y) * 2 * block, 2 * block)] = half[layer, :, n * 2 * block : (n + 1) * 2 * block]
         for k in range(4):
             home = (z ^ k) * Z_STEP + (1 - y) * Y_STEP
-            dy[layer, :, lanes((home + c) * block, block)] = far[k, layer]
-            dy[layer, :, lanes((home + 1 - c) * block, block)] = far_core[k, layer]
+            mine, core = ((far, far_core), (last, last_core))[k // 2]
+            dy[layer, :, lanes((home + c) * block, block)] = mine[k % 2, layer]
+            dy[layer, :, lanes((home + 1 - c) * block, block)] = core[k % 2, layer]
     both = jnp.concatenate([act[0], act[1]])
     grad_same[0] = dot_nn(act[0], dy[0]).astype(jnp.bfloat16)
     second = dot_nn(both, dy[1]).astype(jnp.bfloat16)
@@ -263,11 +276,12 @@
     peer_x = to_lat(far_x, Y_STEP)
     lead_x, _ = lax.optimization_barrier((own_x, other))
     near_x = to_both(lead_x, SWAP, 0)
-    far_s, _, _ = lax.optimization_barrier((far_s, other, line2))
+    far_s, line2_y = lax.optimization_barrier((far_s, line2_y))
     peer_s = to_lat(far_s, Y_STEP)
     diag_x = to_both(peer_x, SWAP, 0)
-    line1, line3, near_x = lax.optimization_barrier((line1, line3, near_x))
-    pieces = [near, line1, line3, line2, line2_y]
+    (lines,) = run(relay_kernel, "relay", [((2, 2, 2, 128, block), bf16)], line1, line3, cost=(1_000_000_000, 0))
+    lines, near_x = lax.optimization_barrier((lines, near_x))
+    pieces = [near, lines, line2, line2_y]
     pieces += [to_lat(piece, C_STEP) for piece in pieces]
     full, slope, act = run(
         encode_kernel, "encode",
@@ -290,19 +304,22 @@
     )
     parts = [to_lat(part, k * Z_STEP) for k, part in zip((1, 2, 3), parts)]
     (dy,) = run(misfit_kernel, "misfit", [((2, 128, block), bf16)], mine, *parts, mlp_out)
-    row, lead = run(
-        row_kernel, "row",
-        [((4, 2, 128, block), bf16), ((4, 128, block), bf16)],
-        dy, *[to_lat(dy, k * Z_STEP) for k in (1, 2, 3)],
-    )
+    pair = ((2, 2, 128, block), bf16)
+    line1, line2, line3 = (to_lat(dy, k * Z_STEP) for k in (1, 2, 3))
+    (row,) = run(row_kernel, "row", [pair], dy, line1)
+    far = to_lat(row, Y_STEP)
     row_core = to_lat(row, C_STEP)
-    far = to_lat(row, Y_STEP)
+    last, lead = run(last_kernel, "last", [pair, ((4, 128, block), bf16)], dy, line1, line2, line3, cost=(2_000_000_000, 0))
+    last, lead, far = lax.optimization_barrier((last, lead, far))
+    far_core = to_lat(far, C_STEP)
+    last_core = to_lat(last, C_STEP)
+    far_last = to_lat(last, Y_STEP)
     x_own = to_both(lead, SWAP, 0)
     d_own = to_both(lead, SWAP, Y_STEP)
     half, grad_own, to_y, to_x, to_d = run(
         act_grad_kernel, "act_grad",
         [((2, 128, depth // 2), bf16), ((3, 64, 128), f32)] + [((144, 128), bf16)] * 3,
-        row, row_core, own_s, own_x, peer_s, peer_x, near_x, diag_x,
+        row, row_core, last, last_core, own_s, own_x, peer_s, peer_x, near_x, diag_x,
     )
     from_y = to_lat(to_y, Y_STEP)
     from_x = to_both(to_x, SWAP, 0)
@@ -312,11 +329,11 @@
         [((1, 1), f32), ((2, 64, depth), bf16), ((2, 64), f32)],
         grad_own, from_y, from_x, from_d, slope, full,
     )
-    far, x_own, d_own, _, _, _ = lax.optimization_barrier((far, x_own, d_own, from_y, from_x, from_d))
-    far_core = to_lat(far, C_STEP)
+    far_last, x_own, d_own, _ = lax.optimization_barrier((far_last, x_own, d_own, (from_y, from_x, from_d)))
+    last_far_core = to_lat(far_last, C_STEP)
     x_core = to_lat(x_own, C_STEP)
     d_core = to_lat(d_own, C_STEP)
-    operands = (act, act_x, half, far, far_core, x_own, x_core, d_own, d_core)
+    operands = (act, act_x, half, far, far_last, far_core, last_far_core, x_own, x_core, d_own, d_core)
     outs = [((2, 64, depth), bf16), ((1, 64, depth), bf16), ((1, 2, 64, depth), bf16)]
     grad_same, grad_next, grad_cross = pl.pallas_call(
         decoder_grad_kernel,

time: 70.1 us -> 67.9 us (0.969)
  waiting for transfers between devices: 26.2 us -> 22.6 us
  starting transfers between devices: 34.7 us -> 36.1 us
    ppermute x26 -> x28, waiting for transfers between devices: 20.3 us -> 16.7 us  [to_lat(): lax.ppermute(value, 'lat', [(source, source ^ step) for source in range(l...]
    ppermute x8, starting transfers between devices: 8.41 us -> 10.9 us  [to_both(): return lax.ppermute(value, ('sec', 'lat'), pairs)]
    ppermute x26 -> x28, starting transfers between devices: 26.2 us -> 25.2 us  [to_lat(): lax.ppermute(value, 'lat', [(source, source ^ step) for source in range(l...]
    pallas_call x8 -> x10, Pallas kernels: 3.61 us -> 3.62 us  [run(): pl.pallas_call(kernel, name=name, out_shape=[jax.ShapeDtypeStruct(shape,...]
  transfers between devices with their start and end apart: 34 -> 36, of which waited for: 19 -> 13; matrix products, arithmetic and copies ran while one was open for 0% -> 0% of each run, Pallas kernels for 7% -> 8%
where the time goes in v4:
time: 67.9 us; the launch traced here: 67.7 us
  starting transfers between devices  36.1 us (53%)
  waiting for transfers between devices  22.6 us (33%)
  Pallas kernels  8.01 us (12%)
  between operations  0.82 us (1%)
    ppermute x28, starting transfers between devices, to_lat(): lax.ppermute(value, 'lat', [(source, source ^ step) for source in range(l...  25.2 us
    ppermute x28, waiting for transfers between devices, to_lat(): lax.ppermute(value, 'lat', [(source, source ^ step) for source in range(l...  16.7 us
    ppermute x8, starting transfers between devices, to_both(): return lax.ppermute(value, ('sec', 'lat'), pairs)  10.9 us
    ppermute x8, waiting for transfers between devices, to_both(): return lax.ppermute(value, ('sec', 'lat'), pairs)  5.87 us
    pallas_call x10, Pallas kernels, run(): pl.pallas_call(kernel, name=name, out_shape=[jax.ShapeDtypeStruct(shape,...  3.62 us
    pallas_call x1, Pallas kernels, staged(): pl.pallas_call(pack_kernel, name='pack', out_shape=[jax.ShapeDtypeStruct(...  2.38 us
    pallas_call x1, Pallas kernels, staged(): pl.pallas_call(decoder_grad_kernel, name='decoder_grad', out_shape=[jax.S...  2.01 us
  transfers between devices with their start and end apart: 36, of which 13 were waited for; matrix products, arithmetic and copies ran while one was open for 0% of the time, Pallas kernels for 8%

profile of v4, /device:TPU:0, one launch (start us, length us, event | category | flops | bytes accessed | tf_op | source)
XLA Modules:
  0.0 67.7 jit_solution(8072204787040876950)
XLA Ops:
  0.6 3.0 %collective-permute-start = (bf16[2,128,128]{2,1,0:T(8,128)(2,1)}, bf16[2,128,128]{2,1,0:T(8,128)(2,1)S(1)}, u32[]{:S(2)}, u32[]{:S(2)}) collective-permute-start(bf16[2,128,128]{2,1,0:T(8,128)(2,1)} %own.1), channel_id=1, source_target_pairs={{0,2},{1,3},{2,0},{3,1},{4,6},{5,7},{6,4},{7,5},{8,10},{9,11},{10,... | collective-permute-start | bytes 196616 | tf_op jit(solution)/shard_map/ppermute | solution.py:51
  3.7 2.6 %collective-permute-start.4 = (bf16[2,128,128]{2,1,0:T(8,128)(2,1)}, bf16[2,128,128]{2,1,0:T(8,128)(2,1)S(1)}, u32[]{:S(2)}, u32[]{:S(2)}) collective-permute-start(bf16[2,128,128]{2,1,0:T(8,128)(2,1)} %own.1), channel_id=1, source_target_pairs={{0,8},{1,9},{2,10},{3,11},{4,12},{5,13},{6,14},{7,15},{8,0},{9,1},... | collective-permute-start | bytes 196616 | tf_op jit(solution)/shard_map/ppermute | solution.py:51
  6.3 2.4 %pack.1 = (bf16[3,64,1024]{2,1,0:T(8,128)(2,1)}, bf16[2,64,1024]{2,1,0:T(8,128)(2,1)}, bf16[3,64,1024]{2,1,0:T(8,128)(2,1)}, bf16[2,64,1024]{2,1,0:T(8,128)(2,1)}) custom-call(bf16[2,64,2048]{2,1,0:T(8,128)(2,1)} %same.1, bf16[1,64,2048]{2,1,0:T(8,128)(2,1)} %nxt.1, bf16[1,2,64,2048]{3,2,1,0:T(8,128)(2,1)} %cross.1), custom_call_target="tpu_custom_call" | custom-call | tf_op jit(solution)/shard_map/pack/pallas_call | solution.py:259
  8.7 1.6 %collective-permute-start.3 = (bf16[2,64,1024]{2,1,0:T(8,128)(2,1)}, bf16[2,64,1024]{2,1,0:T(8,128)(2,1)S(1)}, u32[]{:S(2)}, u32[]{:S(2)}) collective-permute-start(bf16[2,64,1024]{2,1,0:T(8,128)(2,1)} %get-tuple-element.46.own_x), channel_id=1, source_target_pairs={{0,16},{1,17},{2,18},{3,19},{4,20},{5,21},{6,22},{7,23},{8,24},{9,... | collective-permute-start | bytes 786440 | tf_op jit(solution)/shard_map/ppermute | solution.py:57
  10.8 1.6 %collective-permute-start.1 = (bf16[2,2,128,128]{3,2,1,0:T(8,128)(2,1)S(1)}, bf16[2,2,128,128]{3,2,1,0:T(8,128)(2,1)S(1)}, u32[]{:S(2)}, u32[]{:S(2)}) collective-permute-start(bf16[2,2,128,128]{3,2,1,0:T(8,128)(2,1)S(1)} %pair.1.refs_0_), channel_id=1, source_target_pairs={{0,4},{1,5},{2,6},{3,7},{4,0},{5,1},{6,2},{7,3},{8,12},{9,13},{10,... | collective-permute-start | bytes 393224 | tf_op jit(solution)/shard_map/ppermute | solution.py:51
  12.4 1.4 %collective-permute-start.2 = (bf16[2,2,128,128]{3,2,1,0:T(8,128)(2,1)S(1)}, bf16[2,2,128,128]{3,2,1,0:T(8,128)(2,1)S(1)}, u32[]{:S(2)}, u32[]{:S(2)}) collective-permute-start(bf16[2,2,128,128]{3,2,1,0:T(8,128)(2,1)S(1)} %pair.1.refs_0_), channel_id=1, source_target_pairs={{0,12},{1,13},{2,14},{3,15},{4,8},{5,9},{6,10},{7,11},{8,4},{9,5},... | collective-permute-start | bytes 393224 | tf_op jit(solution)/shard_map/ppermute | solution.py:51
  13.8 1.5 %collective-permute-start.5 = (bf16[2,128,128]{2,1,0:T(8,128)(2,1)S(1)}, bf16[2,128,128]{2,1,0:T(8,128)(2,1)S(1)}, u32[]{:S(2)}, u32[]{:S(2)}) collective-permute-start(bf16[2,128,128]{2,1,0:T(8,128)(2,1)S(1)} %collective-permute-done.4.refs_2_), channel_id=1, source_target_pairs={{0,2},{1,3},{2,0},{3,1},{4,6},{5,7},{6,4},{7,5},{8,10},{9,11},{10,... | collective-permute-start | bytes 196616 | tf_op jit(solution)/shard_map/ppermute | solution.py:51
  15.3 3.7 %collective-permute-done.5.refs_3_ = bf16[2,128,128]{2,1,0:T(8,128)(2,1)S(1)} collective-permute-done((bf16[2,128,128]{2,1,0:T(8,128)(2,1)S(1)}, bf16[2,128,128]{2,1,0:T(8,128)(2,1)S(1)}, u32[]{:S(2)}, u32[]{:S(2)}) %collective-permute-start.5) | collective-permute-done | bytes 65568 | tf_op jit(solution)/shard_map/ppermute | solution.py:51
  20.2 1.5 %collective-permute-start.15 = (bf16[2,64,1024]{2,1,0:T(8,128)(2,1)S(1)}, bf16[2,64,1024]{2,1,0:T(8,128)(2,1)S(1)}, u32[]{:S(2)}, u32[]{:S(2)}) collective-permute-start(bf16[2,64,1024]{2,1,0:T(8,128)(2,1)S(1)} %collective-permute-done.14.peer_x), channel_id=1, source_target_pairs={{0,16},{1,17},{2,18},{3,19},{4,20},{5,21},{6,22},{7,23},{8,24},{9,... | collective-permute-start | bytes 786440 | tf_op jit(solution)/shard_map/ppermute | solution.py:57
  24.7 1.4 %collective-permute-start.10 = (bf16[2,64,128]{2,1,0:T(8,128)(2,1)S(1)}, bf16[2,64,128]{2,1,0:T(8,128)(2,1)S(1)}, u32[]{:S(2)}, u32[]{:S(2)}) collective-permute-start(bf16[2,64,128]{2,1,0:T(8,128)(2,1)S(1)} %get-tuple-element.52.act), channel_id=1, source_target_pairs={{0,2},{1,3},{2,0},{3,1},{4,6},{5,7},{6,4},{7,5},{8,10},{9,11},{10,... | collective-permute-start | bytes 98312 | tf_op jit(solution)/shard_map/ppermute | solution.py:51
  26.1 1.5 %collective-permute-start.12 = (bf16[2,64,128]{2,1,0:T(8,128)(2,1)S(1)}, bf16[2,64,128]{2,1,0:T(8,128)(2,1)S(1)}, u32[]{:S(2)}, u32[]{:S(2)}) collective-permute-start(bf16[2,64,128]{2,1,0:T(8,128)(2,1)S(1)} %get-tuple-element.52.act), channel_id=1, source_target_pairs={{0,18},{1,19},{2,16},{3,17},{4,22},{5,23},{6,20},{7,21},{8,26},{9,... | collective-permute-start | bytes 98312 | tf_op jit(solution)/shard_map/ppermute | solution.py:57
  29.5 1.4 %collective-permute-done.12.act_d = bf16[2,64,128]{2,1,0:T(8,128)(2,1)S(1)} collective-permute-done((bf16[2,64,128]{2,1,0:T(8,128)(2,1)S(1)}, bf16[2,64,128]{2,1,0:T(8,128)(2,1)S(1)}, u32[]{:S(2)}, u32[]{:S(2)}) %collective-permute-start.12) | collective-permute-done | bytes 32800 | tf_op jit(solution)/shard_map/ppermute | solution.py:57
  31.7 1.5 %collective-permute-done.16.got = bf16[4,2,128,128]{3,2,1,0:T(8,128)(2,1)S(1)} collective-permute-done((bf16[4,2,128,128]{3,2,1,0:T(8,128)(2,1)S(1)}, bf16[4,2,128,128]{3,2,1,0:T(8,128)(2,1)S(1)}, u32[]{:S(2)}, u32[]{:S(2)}) %collective-permute-start.16) | collective-permute-done | bytes 262176 | tf_op jit(solution)/shard_map/ppermute | solution.py:51
  33.3 1.7 %collective-permute-start.17 = (bf16[2,128,128]{2,1,0:T(8,128)(2,1)S(1)}, bf16[2,128,128]{2,1,0:T(8,128)(2,1)S(1)}, u32[]{:S(2)}, u32[]{:S(2)}) collective-permute-start(bf16[2,128,128]{2,1,0:T(8,128)(2,1)S(1)} %get-tuple-element.60), channel_id=1, source_target_pairs={{0,4},{1,5},{2,6},{3,7},{4,0},{5,1},{6,2},{7,3},{8,12},{9,13},{10,... | collective-permute-start | bytes 196616 | tf_op jit(solution)/shard_map/ppermute | solution.py:51
  35.0 1.3 %collective-permute-start.18 = (bf16[2,128,128]{2,1,0:T(8,128)(2,1)S(1)}, bf16[2,128,128]{2,1,0:T(8,128)(2,1)S(1)}, u32[]{:S(2)}, u32[]{:S(2)}) collective-permute-start(bf16[2,128,128]{2,1,0:T(8,128)(2,1)S(1)} %get-tuple-element.61), channel_id=1, source_target_pairs={{0,8},{1,9},{2,10},{3,11},{4,12},{5,13},{6,14},{7,15},{8,0},{9,1},... | collective-permute-start | bytes 196616 | tf_op jit(solution)/shard_map/ppermute | solution.py:51
  36.2 1.5 %collective-permute-start.19 = (bf16[2,128,128]{2,1,0:T(8,128)(2,1)S(1)}, bf16[2,128,128]{2,1,0:T(8,128)(2,1)S(1)}, u32[]{:S(2)}, u32[]{:S(2)}) collective-permute-start(bf16[2,128,128]{2,1,0:T(8,128)(2,1)S(1)} %get-tuple-element.62), channel_id=1, source_target_pairs={{0,12},{1,13},{2,14},{3,15},{4,8},{5,9},{6,10},{7,11},{8,4},{9,5},... | collective-permute-start | bytes 196616 | tf_op jit(solution)/shard_map/ppermute | solution.py:51
  37.8 5.1 %collective-permute-done.18.g2 = bf16[2,128,128]{2,1,0:T(8,128)(2,1)S(1)} collective-permute-done((bf16[2,128,128]{2,1,0:T(8,128)(2,1)S(1)}, bf16[2,128,128]{2,1,0:T(8,128)(2,1)S(1)}, u32[]{:S(2)}, u32[]{:S(2)}) %collective-permute-start.18) | collective-permute-done | bytes 65568 | tf_op jit(solution)/shard_map/ppermute | solution.py:51
  42.9 1.6 %collective-permute-start.20 = (bf16[2,128,128]{2,1,0:T(8,128)(2,1)S(1)}, bf16[2,128,128]{2,1,0:T(8,128)(2,1)S(1)}, u32[]{:S(2)}, u32[]{:S(2)}) collective-permute-start(bf16[2,128,128]{2,1,0:T(8,128)(2,1)S(1)} %misfit.1.one.own), channel_id=1, source_target_pairs={{0,4},{1,5},{2,6},{3,7},{4,0},{5,1},{6,2},{7,3},{8,12},{9,13},{10,... | collective-permute-start | bytes 196616 | tf_op jit(solution)/shard_map/ppermute | solution.py:51
  44.7 2.6 %collective-permute-start.23 = (bf16[2,128,128]{2,1,0:T(8,128)(2,1)S(1)}, bf16[2,128,128]{2,1,0:T(8,128)(2,1)S(1)}, u32[]{:S(2)}, u32[]{:S(2)}) collective-permute-start(bf16[2,128,128]{2,1,0:T(8,128)(2,1)S(1)} %misfit.1.one.own), channel_id=1, source_target_pairs={{0,12},{1,13},{2,14},{3,15},{4,8},{5,9},{6,10},{7,11},{8,4},{9,5},... | collective-permute-start | bytes 196616 | tf_op jit(solution)/shard_map/ppermute | solution.py:51
  48.0 4.1 %collective-permute-done.22.line2 = bf16[2,128,128]{2,1,0:T(8,128)(2,1)S(1)} collective-permute-done((bf16[2,128,128]{2,1,0:T(8,128)(2,1)S(1)}, bf16[2,128,128]{2,1,0:T(8,128)(2,1)S(1)}, u32[]{:S(2)}, u32[]{:S(2)}) %collective-permute-start.22) | collective-permute-done | bytes 65568 | tf_op jit(solution)/shard_map/ppermute | solution.py:51
  54.1 1.7 %collective-permute-start.31 = (bf16[4,128,128]{2,1,0:T(8,128)(2,1)S(1)}, bf16[4,128,128]{2,1,0:T(8,128)(2,1)S(1)}, u32[]{:S(2)}, u32[]{:S(2)}) collective-permute-start(bf16[4,128,128]{2,1,0:T(8,128)(2,1)S(1)} %get-tuple-element.77), channel_id=1, source_target_pairs={{0,18},{1,19},{2,16},{3,17},{4,22},{5,23},{6,20},{7,21},{8,26},{9,... | collective-permute-start | bytes 393224 | tf_op jit(solution)/shard_map/ppermute | solution.py:57
  58.6 1.7 %collective-permute-start.28 = (bf16[144,128]{1,0:T(8,128)(2,1)S(1)}, bf16[144,128]{1,0:T(8,128)(2,1)S(1)}, u32[]{:S(2)}, u32[]{:S(2)}) collective-permute-start(bf16[144,128]{1,0:T(8,128)(2,1)S(1)} %get-tuple-element.69), channel_id=1, source_target_pairs={{0,18},{1,19},{2,16},{3,17},{4,22},{5,23},{6,20},{7,21},{8,26},{9,... | collective-permute-start | bytes 110600 | tf_op jit(solution)/shard_map/ppermute | solution.py:57
  60.3 2.6 %collective-permute-done.31.d_own = bf16[4,128,128]{2,1,0:T(8,128)(2,1)S(1)} collective-permute-done((bf16[4,128,128]{2,1,0:T(8,128)(2,1)S(1)}, bf16[4,128,128]{2,1,0:T(8,128)(2,1)S(1)}, u32[]{:S(2)}, u32[]{:S(2)}) %collective-permute-start.31) | collective-permute-done | bytes 131104 | tf_op jit(solution)/shard_map/ppermute | solution.py:57
  65.7 2.0 %decoder_grad.1 = (bf16[2,64,2048]{2,1,0:T(8,128)(2,1)}, bf16[1,64,2048]{2,1,0:T(8,128)(2,1)}, bf16[1,2,64,2048]{3,2,1,0:T(8,128)(2,1)}) custom-call(bf16[2,64,128]{2,1,0:T(8,128)(2,1)S(1)} %get-tuple-element.52.act, bf16[2,64,128]{2,1,0:T(8,128)(2,1)S(1)} %collective-permute-done.11.act_x, bf16[2,128,1024]{2,1,0:T(8,128)(2,1)S(1)} %get-tuple-element.75.half, ...), custom_call_target="tpu_custom_call" | custom-call | tf_op jit(solution)/shard_map/decoder_grad/pallas_call | solution.py:338
  (79 shorter events, 16.0 us)
Async XLA Ops:
  0.6 8.0 %collective-permute-start = (bf16[2,128,128]{2,1,0:T(8,128)(2,1)}, bf16[2,128,128]{2,1,0:T(8,128)(2,1)S(1)}, u32[]{:S(2)}, u32[]{:S(2)}) collective-permute-start(bf16[2,128,128]{2,1,0:T(8,128)(2,1)} %own.1), channel_id=1, source_target_pairs={{0,2},{1,3},{2,0},{3,1},{4,6},{5,7},{6,4},{7,5},{8,10},{9,11},{10,... | collective-permute-start | bytes 196616 | tf_op jit(solution)/shard_map/ppermute | solution.py:51
  3.7 6.6 %collective-permute-start.4 = (bf16[2,128,128]{2,1,0:T(8,128)(2,1)}, bf16[2,128,128]{2,1,0:T(8,128)(2,1)S(1)}, u32[]{:S(2)}, u32[]{:S(2)}) collective-permute-start(bf16[2,128,128]{2,1,0:T(8,128)(2,1)} %own.1), channel_id=1, source_target_pairs={{0,8},{1,9},{2,10},{3,11},{4,12},{5,13},{6,14},{7,15},{8,0},{9,1},... | collective-permute-start | bytes 196616 | tf_op jit(solution)/shard_map/ppermute | solution.py:51
  8.7 10.9 %collective-permute-start.3 = (bf16[2,64,1024]{2,1,0:T(8,128)(2,1)}, bf16[2,64,1024]{2,1,0:T(8,128)(2,1)S(1)}, u32[]{:S(2)}, u32[]{:S(2)}) collective-permute-start(bf16[2,64,1024]{2,1,0:T(8,128)(2,1)} %get-tuple-element.46.own_x), channel_id=1, source_target_pairs={{0,16},{1,17},{2,18},{3,19},{4,20},{5,21},{6,22},{7,23},{8,24},{9,... | collective-permute-start | bytes 786440 | tf_op jit(solution)/shard_map/ppermute | solution.py:57
  10.3 9.9 %collective-permute-start.14 = (bf16[2,64,1024]{2,1,0:T(8,128)(2,1)S(1)}, bf16[2,64,1024]{2,1,0:T(8,128)(2,1)S(1)}, u32[]{:S(2)}, u32[]{:S(2)}) collective-permute-start(bf16[2,64,1024]{2,1,0:T(8,128)(2,1)S(1)} %copy-done.7), channel_id=1, source_target_pairs={{0,2},{1,3},{2,0},{3,1},{4,6},{5,7},{6,4},{7,5},{8,10},{9,11},{10,... | collective-permute-start | bytes 786440 | tf_op jit(solution)/shard_map/ppermute | solution.py:51
  10.8 8.7 %collective-permute-start.1 = (bf16[2,2,128,128]{3,2,1,0:T(8,128)(2,1)S(1)}, bf16[2,2,128,128]{3,2,1,0:T(8,128)(2,1)S(1)}, u32[]{:S(2)}, u32[]{:S(2)}) collective-permute-start(bf16[2,2,128,128]{3,2,1,0:T(8,128)(2,1)S(1)} %pair.1.refs_0_), channel_id=1, source_target_pairs={{0,4},{1,5},{2,6},{3,7},{4,0},{5,1},{6,2},{7,3},{8,12},{9,13},{10,... | collective-permute-start | bytes 393224 | tf_op jit(solution)/shard_map/ppermute | solution.py:51
  12.4 7.1 %collective-permute-start.2 = (bf16[2,2,128,128]{3,2,1,0:T(8,128)(2,1)S(1)}, bf16[2,2,128,128]{3,2,1,0:T(8,128)(2,1)S(1)}, u32[]{:S(2)}, u32[]{:S(2)}) collective-permute-start(bf16[2,2,128,128]{3,2,1,0:T(8,128)(2,1)S(1)} %pair.1.refs_0_), channel_id=1, source_target_pairs={{0,12},{1,13},{2,14},{3,15},{4,8},{5,9},{6,10},{7,11},{8,4},{9,5},... | collective-permute-start | bytes 393224 | tf_op jit(solution)/shard_map/ppermute | solution.py:51
  13.8 5.1 %collective-permute-start.5 = (bf16[2,128,128]{2,1,0:T(8,128)(2,1)S(1)}, bf16[2,128,128]{2,1,0:T(8,128)(2,1)S(1)}, u32[]{:S(2)}, u32[]{:S(2)}) collective-permute-start(bf16[2,128,128]{2,1,0:T(8,128)(2,1)S(1)} %collective-permute-done.4.refs_2_), channel_id=1, source_target_pairs={{0,2},{1,3},{2,0},{3,1},{4,6},{5,7},{6,4},{7,5},{8,10},{9,11},{10,... | collective-permute-start | bytes 196616 | tf_op jit(solution)/shard_map/ppermute | solution.py:51
  18.9 9.7 %collective-permute-start.13 = (bf16[3,64,1024]{2,1,0:T(8,128)(2,1)}, bf16[3,64,1024]{2,1,0:T(8,128)(2,1)S(1)}, u32[]{:S(2)}, u32[]{:S(2)}) collective-permute-start(bf16[3,64,1024]{2,1,0:T(8,128)(2,1)} %get-tuple-element.54), channel_id=1, source_target_pairs={{0,2},{1,3},{2,0},{3,1},{4,6},{5,7},{6,4},{7,5},{8,10},{9,11},{10,... | collective-permute-start | bytes 1179656 | tf_op jit(solution)/shard_map/ppermute | solution.py:51
  20.2 8.9 %collective-permute-start.15 = (bf16[2,64,1024]{2,1,0:T(8,128)(2,1)S(1)}, bf16[2,64,1024]{2,1,0:T(8,128)(2,1)S(1)}, u32[]{:S(2)}, u32[]{:S(2)}) collective-permute-start(bf16[2,64,1024]{2,1,0:T(8,128)(2,1)S(1)} %collective-permute-done.14.peer_x), channel_id=1, source_target_pairs={{0,16},{1,17},{2,18},{3,19},{4,20},{5,21},{6,22},{7,23},{8,24},{9,... | collective-permute-start | bytes 786440 | tf_op jit(solution)/shard_map/ppermute | solution.py:57
  24.1 5.4 %collective-permute-start.11 = (bf16[2,64,128]{2,1,0:T(8,128)(2,1)S(1)}, bf16[2,64,128]{2,1,0:T(8,128)(2,1)S(1)}, u32[]{:S(2)}, u32[]{:S(2)}) collective-permute-start(bf16[2,64,128]{2,1,0:T(8,128)(2,1)S(1)} %get-tuple-element.52.act), channel_id=1, source_target_pairs={{0,16},{1,17},{2,18},{3,19},{4,20},{5,21},{6,22},{7,23},{8,24},{9,... | collective-permute-start | bytes 98312 | tf_op jit(solution)/shard_map/ppermute | solution.py:57
  26.1 4.8 %collective-permute-start.12 = (bf16[2,64,128]{2,1,0:T(8,128)(2,1)S(1)}, bf16[2,64,128]{2,1,0:T(8,128)(2,1)S(1)}, u32[]{:S(2)}, u32[]{:S(2)}) collective-permute-start(bf16[2,64,128]{2,1,0:T(8,128)(2,1)S(1)} %get-tuple-element.52.act), channel_id=1, source_target_pairs={{0,18},{1,19},{2,16},{3,17},{4,22},{5,23},{6,20},{7,21},{8,26},{9,... | collective-permute-start | bytes 98312 | tf_op jit(solution)/shard_map/ppermute | solution.py:57
  35.0 7.9 %collective-permute-start.18 = (bf16[2,128,128]{2,1,0:T(8,128)(2,1)S(1)}, bf16[2,128,128]{2,1,0:T(8,128)(2,1)S(1)}, u32[]{:S(2)}, u32[]{:S(2)}) collective-permute-start(bf16[2,128,128]{2,1,0:T(8,128)(2,1)S(1)} %get-tuple-element.61), channel_id=1, source_target_pairs={{0,8},{1,9},{2,10},{3,11},{4,12},{5,13},{6,14},{7,15},{8,0},{9,1},... | collective-permute-start | bytes 196616 | tf_op jit(solution)/shard_map/ppermute | solution.py:51
  36.2 6.6 %collective-permute-start.19 = (bf16[2,128,128]{2,1,0:T(8,128)(2,1)S(1)}, bf16[2,128,128]{2,1,0:T(8,128)(2,1)S(1)}, u32[]{:S(2)}, u32[]{:S(2)}) collective-permute-start(bf16[2,128,128]{2,1,0:T(8,128)(2,1)S(1)} %get-tuple-element.62), channel_id=1, source_target_pairs={{0,12},{1,13},{2,14},{3,15},{4,8},{5,9},{6,10},{7,11},{8,4},{9,5},... | collective-permute-start | bytes 196616 | tf_op jit(solution)/shard_map/ppermute | solution.py:51
  44.5 7.6 %collective-permute-start.22 = (bf16[2,128,128]{2,1,0:T(8,128)(2,1)S(1)}, bf16[2,128,128]{2,1,0:T(8,128)(2,1)S(1)}, u32[]{:S(2)}, u32[]{:S(2)}) collective-permute-start(bf16[2,128,128]{2,1,0:T(8,128)(2,1)S(1)} %misfit.1.one.own), channel_id=1, source_target_pairs={{0,8},{1,9},{2,10},{3,11},{4,12},{5,13},{6,14},{7,15},{8,0},{9,1},... | collective-permute-start | bytes 196616 | tf_op jit(solution)/shard_map/ppermute | solution.py:51
  44.7 7.4 %collective-permute-start.23 = (bf16[2,128,128]{2,1,0:T(8,128)(2,1)S(1)}, bf16[2,128,128]{2,1,0:T(8,128)(2,1)S(1)}, u32[]{:S(2)}, u32[]{:S(2)}) collective-permute-start(bf16[2,128,128]{2,1,0:T(8,128)(2,1)S(1)} %misfit.1.one.own), channel_id=1, source_target_pairs={{0,12},{1,13},{2,14},{3,15},{4,8},{5,9},{6,10},{7,11},{8,4},{9,5},... | collective-permute-start | bytes 196616 | tf_op jit(solution)/shard_map/ppermute | solution.py:51
  47.3 5.0 %collective-permute-start.24 = (bf16[2,2,128,128]{3,2,1,0:T(8,128)(2,1)S(1)}, bf16[2,2,128,128]{3,2,1,0:T(8,128)(2,1)S(1)}, u32[]{:S(2)}, u32[]{:S(2)}) collective-permute-start(bf16[2,2,128,128]{3,2,1,0:T(8,128)(2,1)S(1)} %row.1.near), channel_id=1, source_target_pairs={{0,2},{1,3},{2,0},{3,1},{4,6},{5,7},{6,4},{7,5},{8,10},{9,11},{10,... | collective-permute-start | bytes 393224 | tf_op jit(solution)/shard_map/ppermute | solution.py:51
  48.0 7.9 %collective-permute-start.21 = (bf16[2,2,128,128]{3,2,1,0:T(8,128)(2,1)S(1)}, bf16[2,2,128,128]{3,2,1,0:T(8,128)(2,1)S(1)}, u32[]{:S(2)}, u32[]{:S(2)}) collective-permute-start(bf16[2,2,128,128]{3,2,1,0:T(8,128)(2,1)S(1)} %row.1.near), channel_id=1, source_target_pairs={{0,1},{1,0},{2,3},{3,2},{4,5},{5,4},{6,7},{7,6},{8,9},{9,8},{10,11... | collective-permute-start | bytes 393224 | tf_op jit(solution)/shard_map/ppermute | solution.py:51
  52.4 6.2 %collective-permute-start.29 = (bf16[2,2,128,128]{3,2,1,0:T(8,128)(2,1)S(1)}, bf16[2,2,128,128]{3,2,1,0:T(8,128)(2,1)S(1)}, u32[]{:S(2)}, u32[]{:S(2)}) collective-permute-start(bf16[2,2,128,128]{3,2,1,0:T(8,128)(2,1)S(1)} %get-tuple-element.65.last), channel_id=1, source_target_pairs={{0,2},{1,3},{2,0},{3,1},{4,6},{5,7},{6,4},{7,5},{8,10},{9,11},{10,... | collective-permute-start | bytes 393224 | tf_op jit(solution)/shard_map/ppermute | solution.py:51
  53.0 7.3 %collective-permute-start.30 = (bf16[4,128,128]{2,1,0:T(8,128)(2,1)S(1)}, bf16[4,128,128]{2,1,0:T(8,128)(2,1)S(1)}, u32[]{:S(2)}, u32[]{:S(2)}) collective-permute-start(bf16[4,128,128]{2,1,0:T(8,128)(2,1)S(1)} %get-tuple-element.77), channel_id=1, source_target_pairs={{0,16},{1,17},{2,18},{3,19},{4,20},{5,21},{6,22},{7,23},{8,24},{9,... | collective-permute-start | bytes 393224 | tf_op jit(solution)/shard_map/ppermute | solution.py:57
  54.1 8.8 %collective-permute-start.31 = (bf16[4,128,128]{2,1,0:T(8,128)(2,1)S(1)}, bf16[4,128,128]{2,1,0:T(8,128)(2,1)S(1)}, u32[]{:S(2)}, u32[]{:S(2)}) collective-permute-start(bf16[4,128,128]{2,1,0:T(8,128)(2,1)S(1)} %get-tuple-element.77), channel_id=1, source_target_pairs={{0,18},{1,19},{2,16},{3,17},{4,22},{5,23},{6,20},{7,21},{8,26},{9,... | collective-permute-start | bytes 393224 | tf_op jit(solution)/shard_map/ppermute | solution.py:57
  56.8 6.2 %collective-permute-start.26 = (bf16[144,128]{1,0:T(8,128)(2,1)S(1)}, bf16[144,128]{1,0:T(8,128)(2,1)S(1)}, u32[]{:S(2)}, u32[]{:S(2)}) collective-permute-start(bf16[144,128]{1,0:T(8,128)(2,1)S(1)} %get-tuple-element.67), channel_id=1, source_target_pairs={{0,2},{1,3},{2,0},{3,1},{4,6},{5,7},{6,4},{7,5},{8,10},{9,11},{10,... | collective-permute-start | bytes 110600 | tf_op jit(solution)/shard_map/ppermute | solution.py:51
  57.4 5.5 %collective-permute-start.27 = (bf16[144,128]{1,0:T(8,128)(2,1)S(1)}, bf16[144,128]{1,0:T(8,128)(2,1)S(1)}, u32[]{:S(2)}, u32[]{:S(2)}) collective-permute-start(bf16[144,128]{1,0:T(8,128)(2,1)S(1)} %get-tuple-element.68), channel_id=1, source_target_pairs={{0,16},{1,17},{2,18},{3,19},{4,20},{5,21},{6,22},{7,23},{8,24},{9,... | collective-permute-start | bytes 110600 | tf_op jit(solution)/shard_map/ppermute | solution.py:57
  58.6 5.2 %collective-permute-start.28 = (bf16[144,128]{1,0:T(8,128)(2,1)S(1)}, bf16[144,128]{1,0:T(8,128)(2,1)S(1)}, u32[]{:S(2)}, u32[]{:S(2)}) collective-permute-start(bf16[144,128]{1,0:T(8,128)(2,1)S(1)} %get-tuple-element.69), channel_id=1, source_target_pairs={{0,18},{1,19},{2,16},{3,17},{4,22},{5,23},{6,20},{7,21},{8,26},{9,... | collective-permute-start | bytes 110600 | tf_op jit(solution)/shard_map/ppermute | solution.py:57
  60.3 5.1 %collective-permute-start.32 = (bf16[2,2,128,128]{3,2,1,0:T(8,128)(2,1)S(1)}, bf16[2,2,128,128]{3,2,1,0:T(8,128)(2,1)S(1)}, u32[]{:S(2)}, u32[]{:S(2)}) collective-permute-start(bf16[2,2,128,128]{3,2,1,0:T(8,128)(2,1)S(1)} %collective-permute-done.24.far), channel_id=1, source_target_pairs={{0,1},{1,0},{2,3},{3,2},{4,5},{5,4},{6,7},{7,6},{8,9},{9,8},{10,11... | collective-permute-start | bytes 393224 | tf_op jit(solution)/shard_map/ppermute | solution.py:51
  (20 other events, 76.6 us)

commit v5 on v4

--- a/solution.py
+++ b/solution.py
@@ -212,7 +212,7 @@
         grad_enc[layer] = dot_nn(pre_grad.astype(jnp.bfloat16), full[layer]).astype(jnp.bfloat16)
 
 
-def decoder_grad_kernel(act, act_x, half, far, last, far_core, last_core, x_own, x_core, d_own, d_core, grad_same, grad_next, grad_cross, dy, dx):
+def decoder_grad_kernel(act, act_x, half, far, last, far_core, last_core, x_own, x_core, d_own, d_core, grad_same, grad_next, grad_cross, dy, dx, staged_out, sems):
     z, y, c = place()
     leading = lax.axis_index("sec") == 0
     block = far.shape[-1]
@@ -224,11 +224,18 @@
             mine, core = ((far, far_core), (last, last_core))[k // 2]
             dy[layer, :, lanes((home + c) * block, block)] = mine[k % 2, layer]
             dy[layer, :, lanes((home + 1 - c) * block, block)] = core[k % 2, layer]
+    copies = []
+
+    def out(value, stage, target):
+        stage[...] = value.astype(jnp.bfloat16)
+        copies.append(pltpu.make_async_copy(stage, target, sems.at[len(copies)]))
+        copies[-1].start()
+
     both = jnp.concatenate([act[0], act[1]])
-    grad_same[0] = dot_nn(act[0], dy[0]).astype(jnp.bfloat16)
-    second = dot_nn(both, dy[1]).astype(jnp.bfloat16)
-    grad_next[0] = second[0:64]
-    grad_same[1] = second[64:128]
+    second = dot_nn(both, dy[1])
+    out(second[0:64], staged_out.at[0], grad_next.at[0])
+    out(second[64:128], staged_out.at[1], grad_same.at[1])
+    out(dot_nn(act[0], dy[0]), staged_out.at[2], grad_same.at[0])
 
     @pl.when(leading)
     def _():
@@ -237,11 +244,16 @@
                 home = (z ^ k) * Z_STEP + row * Y_STEP
                 dx[:, lanes((home + c) * block, block)] = own[k]
                 dx[:, lanes((home + 1 - c) * block, block)] = core[k]
-        grad_cross[0] = dot_nn(both, dx[...]).astype(jnp.bfloat16).reshape(2, 64, -1)
 
     @pl.when(jnp.logical_not(leading))
     def _():
-        grad_cross[0] = dot_nn(act_x[...].reshape(128, 128), dy[1]).astype(jnp.bfloat16).reshape(2, 64, -1)
+        dx[...] = dy[1]
+
+    source = jnp.where(leading, both, stacked(act_x, 0, 2))
+    for j in range(2):
+        out(dot_nn(source[j * 64 : j * 64 + 64], dx[...]), staged_out.at[3 + j], grad_cross.at[0, j])
+    for copy in copies:
+        copy.wait()
 
 
 def staged(resid_in, mlp_out, enc_weight, enc_bias, thresholds, same_dec, next_dec, cross_dec):
@@ -340,8 +352,13 @@
         name="decoder_grad",
         out_shape=[jax.ShapeDtypeStruct(shape, dtype) for shape, dtype in outs],
         in_specs=[VMEM] * len(operands),
-        out_specs=[VMEM] * len(outs),
-        scratch_shapes=[pltpu.VMEM((2, 128, depth), bf16), pltpu.VMEM((128, depth), bf16)],
+        out_specs=[pl.BlockSpec(memory_space=pl.ANY)] * len(outs),
+        scratch_shapes=[
+            pltpu.VMEM((2, 128, depth), bf16),
+            pltpu.VMEM((128, depth), bf16),
+            pltpu.VMEM((5, 64, depth), bf16),
+            pltpu.SemaphoreType.DMA((5,)),
+        ],
         compiler_params=pltpu.CompilerParams(vmem_limit_bytes=48 * 1024 * 1024),
     )(*operands)
     return (mean_square[0, 0], jnp.swapaxes(grad_enc, 1, 2), grad_bias, grad_same, grad_next, grad_cross)

time: 67.9 us -> 67.6 us (level)
  no operation moved by 1% of the time
where the time goes in v5:
time: 67.6 us; the launch traced here: 67.4 us
  starting transfers between devices  36.1 us (53%)
  waiting for transfers between devices  22.6 us (33%)
  Pallas kernels  7.73 us (11%)
  between operations  0.82 us (1%)
    ppermute x28, starting transfers between devices, to_lat(): lax.ppermute(value, 'lat', [(source, source ^ step) for source in range(l...  25.2 us
    ppermute x28, waiting for transfers between devices, to_lat(): lax.ppermute(value, 'lat', [(source, source ^ step) for source in range(l...  16.7 us
    ppermute x8, starting transfers between devices, to_both(): return lax.ppermute(value, ('sec', 'lat'), pairs)  10.9 us
    ppermute x8, waiting for transfers between devices, to_both(): return lax.ppermute(value, ('sec', 'lat'), pairs)  5.87 us
    pallas_call x10, Pallas kernels, run(): pl.pallas_call(kernel, name=name, out_shape=[jax.ShapeDtypeStruct(shape,...  3.62 us
    pallas_call x1, Pallas kernels, staged(): pl.pallas_call(pack_kernel, name='pack', out_shape=[jax.ShapeDtypeStruct(...  2.38 us
    pallas_call x1, Pallas kernels, staged(): pl.pallas_call(decoder_grad_kernel, name='decoder_grad', out_shape=[jax.S...  1.73 us
  transfers between devices with their start and end apart: 36, of which 13 were waited for; matrix products, arithmetic and copies ran while one was open for 0% of the time, Pallas kernels for 8%

profile of v5, /device:TPU:0, one launch (start us, length us, event | category | flops | bytes accessed | tf_op | source)
XLA Modules:
  0.0 67.4 jit_solution(5754010899096858918)
XLA Ops:
  0.6 3.0 %collective-permute-start = (bf16[2,128,128]{2,1,0:T(8,128)(2,1)}, bf16[2,128,128]{2,1,0:T(8,128)(2,1)S(1)}, u32[]{:S(2)}, u32[]{:S(2)}) collective-permute-start(bf16[2,128,128]{2,1,0:T(8,128)(2,1)} %own.1), channel_id=1, source_target_pairs={{0,2},{1,3},{2,0},{3,1},{4,6},{5,7},{6,4},{7,5},{8,10},{9,11},{10,... | collective-permute-start | bytes 196616 | tf_op jit(solution)/shard_map/ppermute | solution.py:51
  3.7 2.6 %collective-permute-start.4 = (bf16[2,128,128]{2,1,0:T(8,128)(2,1)}, bf16[2,128,128]{2,1,0:T(8,128)(2,1)S(1)}, u32[]{:S(2)}, u32[]{:S(2)}) collective-permute-start(bf16[2,128,128]{2,1,0:T(8,128)(2,1)} %own.1), channel_id=1, source_target_pairs={{0,8},{1,9},{2,10},{3,11},{4,12},{5,13},{6,14},{7,15},{8,0},{9,1},... | collective-permute-start | bytes 196616 | tf_op jit(solution)/shard_map/ppermute | solution.py:51
  6.3 2.4 %pack.1 = (bf16[3,64,1024]{2,1,0:T(8,128)(2,1)}, bf16[2,64,1024]{2,1,0:T(8,128)(2,1)}, bf16[3,64,1024]{2,1,0:T(8,128)(2,1)}, bf16[2,64,1024]{2,1,0:T(8,128)(2,1)}) custom-call(bf16[2,64,2048]{2,1,0:T(8,128)(2,1)} %same.1, bf16[1,64,2048]{2,1,0:T(8,128)(2,1)} %nxt.1, bf16[1,2,64,2048]{3,2,1,0:T(8,128)(2,1)} %cross.1), custom_call_target="tpu_custom_call" | custom-call | tf_op jit(solution)/shard_map/pack/pallas_call | solution.py:271
  8.7 1.6 %collective-permute-start.3 = (bf16[2,64,1024]{2,1,0:T(8,128)(2,1)}, bf16[2,64,1024]{2,1,0:T(8,128)(2,1)S(1)}, u32[]{:S(2)}, u32[]{:S(2)}) collective-permute-start(bf16[2,64,1024]{2,1,0:T(8,128)(2,1)} %get-tuple-element.46.own_x), channel_id=1, source_target_pairs={{0,16},{1,17},{2,18},{3,19},{4,20},{5,21},{6,22},{7,23},{8,24},{9,... | collective-permute-start | bytes 786440 | tf_op jit(solution)/shard_map/ppermute | solution.py:57
  10.8 1.6 %collective-permute-start.1 = (bf16[2,2,128,128]{3,2,1,0:T(8,128)(2,1)S(1)}, bf16[2,2,128,128]{3,2,1,0:T(8,128)(2,1)S(1)}, u32[]{:S(2)}, u32[]{:S(2)}) collective-permute-start(bf16[2,2,128,128]{3,2,1,0:T(8,128)(2,1)S(1)} %pair.1.refs_0_), channel_id=1, source_target_pairs={{0,4},{1,5},{2,6},{3,7},{4,0},{5,1},{6,2},{7,3},{8,12},{9,13},{10,... | collective-permute-start | bytes 393224 | tf_op jit(solution)/shard_map/ppermute | solution.py:51
  12.4 1.4 %collective-permute-start.2 = (bf16[2,2,128,128]{3,2,1,0:T(8,128)(2,1)S(1)}, bf16[2,2,128,128]{3,2,1,0:T(8,128)(2,1)S(1)}, u32[]{:S(2)}, u32[]{:S(2)}) collective-permute-start(bf16[2,2,128,128]{3,2,1,0:T(8,128)(2,1)S(1)} %pair.1.refs_0_), channel_id=1, source_target_pairs={{0,12},{1,13},{2,14},{3,15},{4,8},{5,9},{6,10},{7,11},{8,4},{9,5},... | collective-permute-start | bytes 393224 | tf_op jit(solution)/shard_map/ppermute | solution.py:51
  13.8 1.5 %collective-permute-start.5 = (bf16[2,128,128]{2,1,0:T(8,128)(2,1)S(1)}, bf16[2,128,128]{2,1,0:T(8,128)(2,1)S(1)}, u32[]{:S(2)}, u32[]{:S(2)}) collective-permute-start(bf16[2,128,128]{2,1,0:T(8,128)(2,1)S(1)} %collective-permute-done.4.refs_2_), channel_id=1, source_target_pairs={{0,2},{1,3},{2,0},{3,1},{4,6},{5,7},{6,4},{7,5},{8,10},{9,11},{10,... | collective-permute-start | bytes 196616 | tf_op jit(solution)/shard_map/ppermute | solution.py:51
  15.3 3.7 %collective-permute-done.5.refs_3_ = bf16[2,128,128]{2,1,0:T(8,128)(2,1)S(1)} collective-permute-done((bf16[2,128,128]{2,1,0:T(8,128)(2,1)S(1)}, bf16[2,128,128]{2,1,0:T(8,128)(2,1)S(1)}, u32[]{:S(2)}, u32[]{:S(2)}) %collective-permute-start.5) | collective-permute-done | bytes 65568 | tf_op jit(solution)/shard_map/ppermute | solution.py:51
  20.2 1.5 %collective-permute-start.15 = (bf16[2,64,1024]{2,1,0:T(8,128)(2,1)S(1)}, bf16[2,64,1024]{2,1,0:T(8,128)(2,1)S(1)}, u32[]{:S(2)}, u32[]{:S(2)}) collective-permute-start(bf16[2,64,1024]{2,1,0:T(8,128)(2,1)S(1)} %collective-permute-done.14.peer_x), channel_id=1, source_target_pairs={{0,16},{1,17},{2,18},{3,19},{4,20},{5,21},{6,22},{7,23},{8,24},{9,... | collective-permute-start | bytes 786440 | tf_op jit(solution)/shard_map/ppermute | solution.py:57
  24.7 1.4 %collective-permute-start.10 = (bf16[2,64,128]{2,1,0:T(8,128)(2,1)S(1)}, bf16[2,64,128]{2,1,0:T(8,128)(2,1)S(1)}, u32[]{:S(2)}, u32[]{:S(2)}) collective-permute-start(bf16[2,64,128]{2,1,0:T(8,128)(2,1)S(1)} %get-tuple-element.52.act), channel_id=1, source_target_pairs={{0,2},{1,3},{2,0},{3,1},{4,6},{5,7},{6,4},{7,5},{8,10},{9,11},{10,... | collective-permute-start | bytes 98312 | tf_op jit(solution)/shard_map/ppermute | solution.py:51
  26.1 1.5 %collective-permute-start.12 = (bf16[2,64,128]{2,1,0:T(8,128)(2,1)S(1)}, bf16[2,64,128]{2,1,0:T(8,128)(2,1)S(1)}, u32[]{:S(2)}, u32[]{:S(2)}) collective-permute-start(bf16[2,64,128]{2,1,0:T(8,128)(2,1)S(1)} %get-tuple-element.52.act), channel_id=1, source_target_pairs={{0,18},{1,19},{2,16},{3,17},{4,22},{5,23},{6,20},{7,21},{8,26},{9,... | collective-permute-start | bytes 98312 | tf_op jit(solution)/shard_map/ppermute | solution.py:57
  29.5 1.4 %collective-permute-done.12.act_d = bf16[2,64,128]{2,1,0:T(8,128)(2,1)S(1)} collective-permute-done((bf16[2,64,128]{2,1,0:T(8,128)(2,1)S(1)}, bf16[2,64,128]{2,1,0:T(8,128)(2,1)S(1)}, u32[]{:S(2)}, u32[]{:S(2)}) %collective-permute-start.12) | collective-permute-done | bytes 32800 | tf_op jit(solution)/shard_map/ppermute | solution.py:57
  31.7 1.5 %collective-permute-done.16.got = bf16[4,2,128,128]{3,2,1,0:T(8,128)(2,1)S(1)} collective-permute-done((bf16[4,2,128,128]{3,2,1,0:T(8,128)(2,1)S(1)}, bf16[4,2,128,128]{3,2,1,0:T(8,128)(2,1)S(1)}, u32[]{:S(2)}, u32[]{:S(2)}) %collective-permute-start.16) | collective-permute-done | bytes 262176 | tf_op jit(solution)/shard_map/ppermute | solution.py:51
  33.3 1.7 %collective-permute-start.17 = (bf16[2,128,128]{2,1,0:T(8,128)(2,1)S(1)}, bf16[2,128,128]{2,1,0:T(8,128)(2,1)S(1)}, u32[]{:S(2)}, u32[]{:S(2)}) collective-permute-start(bf16[2,128,128]{2,1,0:T(8,128)(2,1)S(1)} %get-tuple-element.60), channel_id=1, source_target_pairs={{0,4},{1,5},{2,6},{3,7},{4,0},{5,1},{6,2},{7,3},{8,12},{9,13},{10,... | collective-permute-start | bytes 196616 | tf_op jit(solution)/shard_map/ppermute | solution.py:51
  35.0 1.3 %collective-permute-start.18 = (bf16[2,128,128]{2,1,0:T(8,128)(2,1)S(1)}, bf16[2,128,128]{2,1,0:T(8,128)(2,1)S(1)}, u32[]{:S(2)}, u32[]{:S(2)}) collective-permute-start(bf16[2,128,128]{2,1,0:T(8,128)(2,1)S(1)} %get-tuple-element.61), channel_id=1, source_target_pairs={{0,8},{1,9},{2,10},{3,11},{4,12},{5,13},{6,14},{7,15},{8,0},{9,1},... | collective-permute-start | bytes 196616 | tf_op jit(solution)/shard_map/ppermute | solution.py:51
  36.2 1.5 %collective-permute-start.19 = (bf16[2,128,128]{2,1,0:T(8,128)(2,1)S(1)}, bf16[2,128,128]{2,1,0:T(8,128)(2,1)S(1)}, u32[]{:S(2)}, u32[]{:S(2)}) collective-permute-start(bf16[2,128,128]{2,1,0:T(8,128)(2,1)S(1)} %get-tuple-element.62), channel_id=1, source_target_pairs={{0,12},{1,13},{2,14},{3,15},{4,8},{5,9},{6,10},{7,11},{8,4},{9,5},... | collective-permute-start | bytes 196616 | tf_op jit(solution)/shard_map/ppermute | solution.py:51
  37.8 5.1 %collective-permute-done.18.g2 = bf16[2,128,128]{2,1,0:T(8,128)(2,1)S(1)} collective-permute-done((bf16[2,128,128]{2,1,0:T(8,128)(2,1)S(1)}, bf16[2,128,128]{2,1,0:T(8,128)(2,1)S(1)}, u32[]{:S(2)}, u32[]{:S(2)}) %collective-permute-start.18) | collective-permute-done | bytes 65568 | tf_op jit(solution)/shard_map/ppermute | solution.py:51
  42.9 1.6 %collective-permute-start.20 = (bf16[2,128,128]{2,1,0:T(8,128)(2,1)S(1)}, bf16[2,128,128]{2,1,0:T(8,128)(2,1)S(1)}, u32[]{:S(2)}, u32[]{:S(2)}) collective-permute-start(bf16[2,128,128]{2,1,0:T(8,128)(2,1)S(1)} %misfit.1.one.own), channel_id=1, source_target_pairs={{0,4},{1,5},{2,6},{3,7},{4,0},{5,1},{6,2},{7,3},{8,12},{9,13},{10,... | collective-permute-start | bytes 196616 | tf_op jit(solution)/shard_map/ppermute | solution.py:51
  44.7 2.6 %collective-permute-start.23 = (bf16[2,128,128]{2,1,0:T(8,128)(2,1)S(1)}, bf16[2,128,128]{2,1,0:T(8,128)(2,1)S(1)}, u32[]{:S(2)}, u32[]{:S(2)}) collective-permute-start(bf16[2,128,128]{2,1,0:T(8,128)(2,1)S(1)} %misfit.1.one.own), channel_id=1, source_target_pairs={{0,12},{1,13},{2,14},{3,15},{4,8},{5,9},{6,10},{7,11},{8,4},{9,5},... | collective-permute-start | bytes 196616 | tf_op jit(solution)/shard_map/ppermute | solution.py:51
  48.0 4.1 %collective-permute-done.22.line2 = bf16[2,128,128]{2,1,0:T(8,128)(2,1)S(1)} collective-permute-done((bf16[2,128,128]{2,1,0:T(8,128)(2,1)S(1)}, bf16[2,128,128]{2,1,0:T(8,128)(2,1)S(1)}, u32[]{:S(2)}, u32[]{:S(2)}) %collective-permute-start.22) | collective-permute-done | bytes 65568 | tf_op jit(solution)/shard_map/ppermute | solution.py:51
  54.1 1.7 %collective-permute-start.31 = (bf16[4,128,128]{2,1,0:T(8,128)(2,1)S(1)}, bf16[4,128,128]{2,1,0:T(8,128)(2,1)S(1)}, u32[]{:S(2)}, u32[]{:S(2)}) collective-permute-start(bf16[4,128,128]{2,1,0:T(8,128)(2,1)S(1)} %get-tuple-element.77), channel_id=1, source_target_pairs={{0,18},{1,19},{2,16},{3,17},{4,22},{5,23},{6,20},{7,21},{8,26},{9,... | collective-permute-start | bytes 393224 | tf_op jit(solution)/shard_map/ppermute | solution.py:57
  58.6 1.7 %collective-permute-start.28 = (bf16[144,128]{1,0:T(8,128)(2,1)S(1)}, bf16[144,128]{1,0:T(8,128)(2,1)S(1)}, u32[]{:S(2)}, u32[]{:S(2)}) collective-permute-start(bf16[144,128]{1,0:T(8,128)(2,1)S(1)} %get-tuple-element.69), channel_id=1, source_target_pairs={{0,18},{1,19},{2,16},{3,17},{4,22},{5,23},{6,20},{7,21},{8,26},{9,... | collective-permute-start | bytes 110600 | tf_op jit(solution)/shard_map/ppermute | solution.py:57
  60.3 2.6 %collective-permute-done.31.d_own = bf16[4,128,128]{2,1,0:T(8,128)(2,1)S(1)} collective-permute-done((bf16[4,128,128]{2,1,0:T(8,128)(2,1)S(1)}, bf16[4,128,128]{2,1,0:T(8,128)(2,1)S(1)}, u32[]{:S(2)}, u32[]{:S(2)}) %collective-permute-start.31) | collective-permute-done | bytes 131104 | tf_op jit(solution)/shard_map/ppermute | solution.py:57
  65.7 1.7 %decoder_grad.1 = (bf16[2,64,2048]{2,1,0:T(8,128)(2,1)}, bf16[1,64,2048]{2,1,0:T(8,128)(2,1)}, bf16[1,2,64,2048]{3,2,1,0:T(8,128)(2,1)}) custom-call(bf16[2,64,128]{2,1,0:T(8,128)(2,1)S(1)} %get-tuple-element.52.act, bf16[2,64,128]{2,1,0:T(8,128)(2,1)S(1)} %collective-permute-done.11.act_x, bf16[2,128,1024]{2,1,0:T(8,128)(2,1)S(1)} %get-tuple-element.75.half, ...), custom_call_target="tpu_custom_call" | custom-call | tf_op jit(solution)/shard_map/decoder_grad/pallas_call | solution.py:350
  (79 shorter events, 16.0 us)
Async XLA Ops:
  0.6 8.0 %collective-permute-start = (bf16[2,128,128]{2,1,0:T(8,128)(2,1)}, bf16[2,128,128]{2,1,0:T(8,128)(2,1)S(1)}, u32[]{:S(2)}, u32[]{:S(2)}) collective-permute-start(bf16[2,128,128]{2,1,0:T(8,128)(2,1)} %own.1), channel_id=1, source_target_pairs={{0,2},{1,3},{2,0},{3,1},{4,6},{5,7},{6,4},{7,5},{8,10},{9,11},{10,... | collective-permute-start | bytes 196616 | tf_op jit(solution)/shard_map/ppermute | solution.py:51
  3.7 6.6 %collective-permute-start.4 = (bf16[2,128,128]{2,1,0:T(8,128)(2,1)}, bf16[2,128,128]{2,1,0:T(8,128)(2,1)S(1)}, u32[]{:S(2)}, u32[]{:S(2)}) collective-permute-start(bf16[2,128,128]{2,1,0:T(8,128)(2,1)} %own.1), channel_id=1, source_target_pairs={{0,8},{1,9},{2,10},{3,11},{4,12},{5,13},{6,14},{7,15},{8,0},{9,1},... | collective-permute-start | bytes 196616 | tf_op jit(solution)/shard_map/ppermute | solution.py:51
  8.7 10.9 %collective-permute-start.3 = (bf16[2,64,1024]{2,1,0:T(8,128)(2,1)}, bf16[2,64,1024]{2,1,0:T(8,128)(2,1)S(1)}, u32[]{:S(2)}, u32[]{:S(2)}) collective-permute-start(bf16[2,64,1024]{2,1,0:T(8,128)(2,1)} %get-tuple-element.46.own_x), channel_id=1, source_target_pairs={{0,16},{1,17},{2,18},{3,19},{4,20},{5,21},{6,22},{7,23},{8,24},{9,... | collective-permute-start | bytes 786440 | tf_op jit(solution)/shard_map/ppermute | solution.py:57
  10.3 9.9 %collective-permute-start.14 = (bf16[2,64,1024]{2,1,0:T(8,128)(2,1)S(1)}, bf16[2,64,1024]{2,1,0:T(8,128)(2,1)S(1)}, u32[]{:S(2)}, u32[]{:S(2)}) collective-permute-start(bf16[2,64,1024]{2,1,0:T(8,128)(2,1)S(1)} %copy-done.7), channel_id=1, source_target_pairs={{0,2},{1,3},{2,0},{3,1},{4,6},{5,7},{6,4},{7,5},{8,10},{9,11},{10,... | collective-permute-start | bytes 786440 | tf_op jit(solution)/shard_map/ppermute | solution.py:51
  10.8 8.7 %collective-permute-start.1 = (bf16[2,2,128,128]{3,2,1,0:T(8,128)(2,1)S(1)}, bf16[2,2,128,128]{3,2,1,0:T(8,128)(2,1)S(1)}, u32[]{:S(2)}, u32[]{:S(2)}) collective-permute-start(bf16[2,2,128,128]{3,2,1,0:T(8,128)(2,1)S(1)} %pair.1.refs_0_), channel_id=1, source_target_pairs={{0,4},{1,5},{2,6},{3,7},{4,0},{5,1},{6,2},{7,3},{8,12},{9,13},{10,... | collective-permute-start | bytes 393224 | tf_op jit(solution)/shard_map/ppermute | solution.py:51
  12.4 7.1 %collective-permute-start.2 = (bf16[2,2,128,128]{3,2,1,0:T(8,128)(2,1)S(1)}, bf16[2,2,128,128]{3,2,1,0:T(8,128)(2,1)S(1)}, u32[]{:S(2)}, u32[]{:S(2)}) collective-permute-start(bf16[2,2,128,128]{3,2,1,0:T(8,128)(2,1)S(1)} %pair.1.refs_0_), channel_id=1, source_target_pairs={{0,12},{1,13},{2,14},{3,15},{4,8},{5,9},{6,10},{7,11},{8,4},{9,5},... | collective-permute-start | bytes 393224 | tf_op jit(solution)/shard_map/ppermute | solution.py:51
  13.8 5.1 %collective-permute-start.5 = (bf16[2,128,128]{2,1,0:T(8,128)(2,1)S(1)}, bf16[2,128,128]{2,1,0:T(8,128)(2,1)S(1)}, u32[]{:S(2)}, u32[]{:S(2)}) collective-permute-start(bf16[2,128,128]{2,1,0:T(8,128)(2,1)S(1)} %collective-permute-done.4.refs_2_), channel_id=1, source_target_pairs={{0,2},{1,3},{2,0},{3,1},{4,6},{5,7},{6,4},{7,5},{8,10},{9,11},{10,... | collective-permute-start | bytes 196616 | tf_op jit(solution)/shard_map/ppermute | solution.py:51
  18.9 9.7 %collective-permute-start.13 = (bf16[3,64,1024]{2,1,0:T(8,128)(2,1)}, bf16[3,64,1024]{2,1,0:T(8,128)(2,1)S(1)}, u32[]{:S(2)}, u32[]{:S(2)}) collective-permute-start(bf16[3,64,1024]{2,1,0:T(8,128)(2,1)} %get-tuple-element.54), channel_id=1, source_target_pairs={{0,2},{1,3},{2,0},{3,1},{4,6},{5,7},{6,4},{7,5},{8,10},{9,11},{10,... | collective-permute-start | bytes 1179656 | tf_op jit(solution)/shard_map/ppermute | solution.py:51
  20.2 8.9 %collective-permute-start.15 = (bf16[2,64,1024]{2,1,0:T(8,128)(2,1)S(1)}, bf16[2,64,1024]{2,1,0:T(8,128)(2,1)S(1)}, u32[]{:S(2)}, u32[]{:S(2)}) collective-permute-start(bf16[2,64,1024]{2,1,0:T(8,128)(2,1)S(1)} %collective-permute-done.14.peer_x), channel_id=1, source_target_pairs={{0,16},{1,17},{2,18},{3,19},{4,20},{5,21},{6,22},{7,23},{8,24},{9,... | collective-permute-start | bytes 786440 | tf_op jit(solution)/shard_map/ppermute | solution.py:57
  24.1 5.4 %collective-permute-start.11 = (bf16[2,64,128]{2,1,0:T(8,128)(2,1)S(1)}, bf16[2,64,128]{2,1,0:T(8,128)(2,1)S(1)}, u32[]{:S(2)}, u32[]{:S(2)}) collective-permute-start(bf16[2,64,128]{2,1,0:T(8,128)(2,1)S(1)} %get-tuple-element.52.act), channel_id=1, source_target_pairs={{0,16},{1,17},{2,18},{3,19},{4,20},{5,21},{6,22},{7,23},{8,24},{9,... | collective-permute-start | bytes 98312 | tf_op jit(solution)/shard_map/ppermute | solution.py:57
  26.1 4.8 %collective-permute-start.12 = (bf16[2,64,128]{2,1,0:T(8,128)(2,1)S(1)}, bf16[2,64,128]{2,1,0:T(8,128)(2,1)S(1)}, u32[]{:S(2)}, u32[]{:S(2)}) collective-permute-start(bf16[2,64,128]{2,1,0:T(8,128)(2,1)S(1)} %get-tuple-element.52.act), channel_id=1, source_target_pairs={{0,18},{1,19},{2,16},{3,17},{4,22},{5,23},{6,20},{7,21},{8,26},{9,... | collective-permute-start | bytes 98312 | tf_op jit(solution)/shard_map/ppermute | solution.py:57
  35.0 7.9 %collective-permute-start.18 = (bf16[2,128,128]{2,1,0:T(8,128)(2,1)S(1)}, bf16[2,128,128]{2,1,0:T(8,128)(2,1)S(1)}, u32[]{:S(2)}, u32[]{:S(2)}) collective-permute-start(bf16[2,128,128]{2,1,0:T(8,128)(2,1)S(1)} %get-tuple-element.61), channel_id=1, source_target_pairs={{0,8},{1,9},{2,10},{3,11},{4,12},{5,13},{6,14},{7,15},{8,0},{9,1},... | collective-permute-start | bytes 196616 | tf_op jit(solution)/shard_map/ppermute | solution.py:51
  36.2 6.6 %collective-permute-start.19 = (bf16[2,128,128]{2,1,0:T(8,128)(2,1)S(1)}, bf16[2,128,128]{2,1,0:T(8,128)(2,1)S(1)}, u32[]{:S(2)}, u32[]{:S(2)}) collective-permute-start(bf16[2,128,128]{2,1,0:T(8,128)(2,1)S(1)} %get-tuple-element.62), channel_id=1, source_target_pairs={{0,12},{1,13},{2,14},{3,15},{4,8},{5,9},{6,10},{7,11},{8,4},{9,5},... | collective-permute-start | bytes 196616 | tf_op jit(solution)/shard_map/ppermute | solution.py:51
  44.5 7.6 %collective-permute-start.22 = (bf16[2,128,128]{2,1,0:T(8,128)(2,1)S(1)}, bf16[2,128,128]{2,1,0:T(8,128)(2,1)S(1)}, u32[]{:S(2)}, u32[]{:S(2)}) collective-permute-start(bf16[2,128,128]{2,1,0:T(8,128)(2,1)S(1)} %misfit.1.one.own), channel_id=1, source_target_pairs={{0,8},{1,9},{2,10},{3,11},{4,12},{5,13},{6,14},{7,15},{8,0},{9,1},... | collective-permute-start | bytes 196616 | tf_op jit(solution)/shard_map/ppermute | solution.py:51
  44.7 7.4 %collective-permute-start.23 = (bf16[2,128,128]{2,1,0:T(8,128)(2,1)S(1)}, bf16[2,128,128]{2,1,0:T(8,128)(2,1)S(1)}, u32[]{:S(2)}, u32[]{:S(2)}) collective-permute-start(bf16[2,128,128]{2,1,0:T(8,128)(2,1)S(1)} %misfit.1.one.own), channel_id=1, source_target_pairs={{0,12},{1,13},{2,14},{3,15},{4,8},{5,9},{6,10},{7,11},{8,4},{9,5},... | collective-permute-start | bytes 196616 | tf_op jit(solution)/shard_map/ppermute | solution.py:51
  47.3 5.0 %collective-permute-start.24 = (bf16[2,2,128,128]{3,2,1,0:T(8,128)(2,1)S(1)}, bf16[2,2,128,128]{3,2,1,0:T(8,128)(2,1)S(1)}, u32[]{:S(2)}, u32[]{:S(2)}) collective-permute-start(bf16[2,2,128,128]{3,2,1,0:T(8,128)(2,1)S(1)} %row.1.near), channel_id=1, source_target_pairs={{0,2},{1,3},{2,0},{3,1},{4,6},{5,7},{6,4},{7,5},{8,10},{9,11},{10,... | collective-permute-start | bytes 393224 | tf_op jit(solution)/shard_map/ppermute | solution.py:51
  48.0 7.9 %collective-permute-start.21 = (bf16[2,2,128,128]{3,2,1,0:T(8,128)(2,1)S(1)}, bf16[2,2,128,128]{3,2,1,0:T(8,128)(2,1)S(1)}, u32[]{:S(2)}, u32[]{:S(2)}) collective-permute-start(bf16[2,2,128,128]{3,2,1,0:T(8,128)(2,1)S(1)} %row.1.near), channel_id=1, source_target_pairs={{0,1},{1,0},{2,3},{3,2},{4,5},{5,4},{6,7},{7,6},{8,9},{9,8},{10,11... | collective-permute-start | bytes 393224 | tf_op jit(solution)/shard_map/ppermute | solution.py:51
  52.4 6.2 %collective-permute-start.29 = (bf16[2,2,128,128]{3,2,1,0:T(8,128)(2,1)S(1)}, bf16[2,2,128,128]{3,2,1,0:T(8,128)(2,1)S(1)}, u32[]{:S(2)}, u32[]{:S(2)}) collective-permute-start(bf16[2,2,128,128]{3,2,1,0:T(8,128)(2,1)S(1)} %get-tuple-element.65.last), channel_id=1, source_target_pairs={{0,2},{1,3},{2,0},{3,1},{4,6},{5,7},{6,4},{7,5},{8,10},{9,11},{10,... | collective-permute-start | bytes 393224 | tf_op jit(solution)/shard_map/ppermute | solution.py:51
  53.0 7.3 %collective-permute-start.30 = (bf16[4,128,128]{2,1,0:T(8,128)(2,1)S(1)}, bf16[4,128,128]{2,1,0:T(8,128)(2,1)S(1)}, u32[]{:S(2)}, u32[]{:S(2)}) collective-permute-start(bf16[4,128,128]{2,1,0:T(8,128)(2,1)S(1)} %get-tuple-element.77), channel_id=1, source_target_pairs={{0,16},{1,17},{2,18},{3,19},{4,20},{5,21},{6,22},{7,23},{8,24},{9,... | collective-permute-start | bytes 393224 | tf_op jit(solution)/shard_map/ppermute | solution.py:57
  54.1 8.8 %collective-permute-start.31 = (bf16[4,128,128]{2,1,0:T(8,128)(2,1)S(1)}, bf16[4,128,128]{2,1,0:T(8,128)(2,1)S(1)}, u32[]{:S(2)}, u32[]{:S(2)}) collective-permute-start(bf16[4,128,128]{2,1,0:T(8,128)(2,1)S(1)} %get-tuple-element.77), channel_id=1, source_target_pairs={{0,18},{1,19},{2,16},{3,17},{4,22},{5,23},{6,20},{7,21},{8,26},{9,... | collective-permute-start | bytes 393224 | tf_op jit(solution)/shard_map/ppermute | solution.py:57
  56.8 6.2 %collective-permute-start.26 = (bf16[144,128]{1,0:T(8,128)(2,1)S(1)}, bf16[144,128]{1,0:T(8,128)(2,1)S(1)}, u32[]{:S(2)}, u32[]{:S(2)}) collective-permute-start(bf16[144,128]{1,0:T(8,128)(2,1)S(1)} %get-tuple-element.67), channel_id=1, source_target_pairs={{0,2},{1,3},{2,0},{3,1},{4,6},{5,7},{6,4},{7,5},{8,10},{9,11},{10,... | collective-permute-start | bytes 110600 | tf_op jit(solution)/shard_map/ppermute | solution.py:51
  57.4 5.5 %collective-permute-start.27 = (bf16[144,128]{1,0:T(8,128)(2,1)S(1)}, bf16[144,128]{1,0:T(8,128)(2,1)S(1)}, u32[]{:S(2)}, u32[]{:S(2)}) collective-permute-start(bf16[144,128]{1,0:T(8,128)(2,1)S(1)} %get-tuple-element.68), channel_id=1, source_target_pairs={{0,16},{1,17},{2,18},{3,19},{4,20},{5,21},{6,22},{7,23},{8,24},{9,... | collective-permute-start | bytes 110600 | tf_op jit(solution)/shard_map/ppermute | solution.py:57
  58.6 5.2 %collective-permute-start.28 = (bf16[144,128]{1,0:T(8,128)(2,1)S(1)}, bf16[144,128]{1,0:T(8,128)(2,1)S(1)}, u32[]{:S(2)}, u32[]{:S(2)}) collective-permute-start(bf16[144,128]{1,0:T(8,128)(2,1)S(1)} %get-tuple-element.69), channel_id=1, source_target_pairs={{0,18},{1,19},{2,16},{3,17},{4,22},{5,23},{6,20},{7,21},{8,26},{9,... | collective-permute-start | bytes 110600 | tf_op jit(solution)/shard_map/ppermute | solution.py:57
  60.3 5.1 %collective-permute-start.32 = (bf16[2,2,128,128]{3,2,1,0:T(8,128)(2,1)S(1)}, bf16[2,2,128,128]{3,2,1,0:T(8,128)(2,1)S(1)}, u32[]{:S(2)}, u32[]{:S(2)}) collective-permute-start(bf16[2,2,128,128]{3,2,1,0:T(8,128)(2,1)S(1)} %collective-permute-done.24.far), channel_id=1, source_target_pairs={{0,1},{1,0},{2,3},{3,2},{4,5},{5,4},{6,7},{7,6},{8,9},{9,8},{10,11... | collective-permute-start | bytes 393224 | tf_op jit(solution)/shard_map/ppermute | solution.py:51
  (20 other events, 76.6 us)

commit v6 on v5

--- a/solution.py
+++ b/solution.py
@@ -292,7 +292,7 @@
     peer_s = to_lat(far_s, Y_STEP)
     diag_x = to_both(peer_x, SWAP, 0)
     (lines,) = run(relay_kernel, "relay", [((2, 2, 2, 128, block), bf16)], line1, line3, cost=(1_000_000_000, 0))
-    lines, near_x = lax.optimization_barrier((lines, near_x))
+    lines, near_x, bias, cut = lax.optimization_barrier((lines, near_x, bias, cut))
     pieces = [near, lines, line2, line2_y]
     pieces += [to_lat(piece, C_STEP) for piece in pieces]
     full, slope, act = run(

time: 67.6 us -> 72.8 us (1.077)
  waiting for transfers between devices: 22.6 us -> 28.9 us
  starting transfers between devices: 36.1 us -> 35 us
    ppermute x28, waiting for transfers between devices: 16.7 us -> 20.9 us  [to_lat(): lax.ppermute(value, 'lat', [(source, source ^ step) for source in range(l...]
    ppermute x8, waiting for transfers between devices: 5.87 us -> 7.96 us  [to_both(): return lax.ppermute(value, ('sec', 'lat'), pairs)]
    ppermute x8, starting transfers between devices: 10.9 us -> 9.62 us  [to_both(): return lax.ppermute(value, ('sec', 'lat'), pairs)]
  transfers between devices with their start and end apart: 36 -> 36, of which waited for: 13 -> 17; matrix products, arithmetic and copies ran while one was open for 0% -> 0% of each run, Pallas kernels for 8% -> 7%
where the time goes in v6:
time: 72.8 us; the launch traced here: 72.6 us
  starting transfers between devices  35 us (48%)
  waiting for transfers between devices  28.9 us (40%)
  Pallas kernels  7.72 us (11%)
  between operations  0.81 us (1%)
    ppermute x28, starting transfers between devices, to_lat(): lax.ppermute(value, 'lat', [(source, source ^ step) for source in range(l...  25.4 us
    ppermute x28, waiting for transfers between devices, to_lat(): lax.ppermute(value, 'lat', [(source, source ^ step) for source in range(l...  20.9 us
    ppermute x8, starting transfers between devices, to_both(): return lax.ppermute(value, ('sec', 'lat'), pairs)  9.62 us
    ppermute x8, waiting for transfers between devices, to_both(): return lax.ppermute(value, ('sec', 'lat'), pairs)  7.96 us
    pallas_call x10, Pallas kernels, run(): pl.pallas_call(kernel, name=name, out_shape=[jax.ShapeDtypeStruct(shape,...  3.62 us
    pallas_call x1, Pallas kernels, staged(): pl.pallas_call(pack_kernel, name='pack', out_shape=[jax.ShapeDtypeStruct(...  2.38 us
    pallas_call x1, Pallas kernels, staged(): pl.pallas_call(decoder_grad_kernel, name='decoder_grad', out_shape=[jax.S...  1.73 us
  transfers between devices with their start and end apart: 36, of which 17 were waited for; matrix products, arithmetic and copies ran while one was open for 0% of the time, Pallas kernels for 7%

profile of v6, /device:TPU:0, one launch (start us, length us, event | category | flops | bytes accessed | tf_op | source)
XLA Modules:
  0.0 72.6 jit_solution(1167615637502685739)
XLA Ops:
  0.6 3.0 %collective-permute-start = (bf16[2,128,128]{2,1,0:T(8,128)(2,1)}, bf16[2,128,128]{2,1,0:T(8,128)(2,1)S(1)}, u32[]{:S(2)}, u32[]{:S(2)}) collective-permute-start(bf16[2,128,128]{2,1,0:T(8,128)(2,1)} %own.1), channel_id=1, source_target_pairs={{0,2},{1,3},{2,0},{3,1},{4,6},{5,7},{6,4},{7,5},{8,10},{9,11},{10,... | collective-permute-start | bytes 196616 | tf_op jit(solution)/shard_map/ppermute | solution.py:51
  3.7 2.6 %collective-permute-start.4 = (bf16[2,128,128]{2,1,0:T(8,128)(2,1)}, bf16[2,128,128]{2,1,0:T(8,128)(2,1)S(1)}, u32[]{:S(2)}, u32[]{:S(2)}) collective-permute-start(bf16[2,128,128]{2,1,0:T(8,128)(2,1)} %own.1), channel_id=1, source_target_pairs={{0,8},{1,9},{2,10},{3,11},{4,12},{5,13},{6,14},{7,15},{8,0},{9,1},... | collective-permute-start | bytes 196616 | tf_op jit(solution)/shard_map/ppermute | solution.py:51
  6.3 2.4 %pack.1 = (bf16[3,64,1024]{2,1,0:T(8,128)(2,1)}, bf16[2,64,1024]{2,1,0:T(8,128)(2,1)}, bf16[3,64,1024]{2,1,0:T(8,128)(2,1)}, bf16[2,64,1024]{2,1,0:T(8,128)(2,1)}) custom-call(bf16[2,64,2048]{2,1,0:T(8,128)(2,1)} %same.1, bf16[1,64,2048]{2,1,0:T(8,128)(2,1)} %nxt.1, bf16[1,2,64,2048]{3,2,1,0:T(8,128)(2,1)} %cross.1), custom_call_target="tpu_custom_call" | custom-call | tf_op jit(solution)/shard_map/pack/pallas_call | solution.py:271
  9.9 1.3 %collective-permute-start.1 = (bf16[2,2,128,128]{3,2,1,0:T(8,128)(2,1)S(1)}, bf16[2,2,128,128]{3,2,1,0:T(8,128)(2,1)S(1)}, u32[]{:S(2)}, u32[]{:S(2)}) collective-permute-start(bf16[2,2,128,128]{3,2,1,0:T(8,128)(2,1)S(1)} %pair.1.refs_0_), channel_id=1, source_target_pairs={{0,4},{1,5},{2,6},{3,7},{4,0},{5,1},{6,2},{7,3},{8,12},{9,13},{10,... | collective-permute-start | bytes 393224 | tf_op jit(solution)/shard_map/ppermute | solution.py:51
  11.1 2.6 %collective-permute-start.2 = (bf16[2,2,128,128]{3,2,1,0:T(8,128)(2,1)S(1)}, bf16[2,2,128,128]{3,2,1,0:T(8,128)(2,1)S(1)}, u32[]{:S(2)}, u32[]{:S(2)}) collective-permute-start(bf16[2,2,128,128]{3,2,1,0:T(8,128)(2,1)S(1)} %pair.1.refs_0_), channel_id=1, source_target_pairs={{0,12},{1,13},{2,14},{3,15},{4,8},{5,9},{6,10},{7,11},{8,4},{9,5},... | collective-permute-start | bytes 393224 | tf_op jit(solution)/shard_map/ppermute | solution.py:51
  13.8 1.5 %collective-permute-start.3 = (bf16[2,64,1024]{2,1,0:T(8,128)(2,1)S(1)}, bf16[2,64,1024]{2,1,0:T(8,128)(2,1)S(1)}, u32[]{:S(2)}, u32[]{:S(2)}) collective-permute-start(bf16[2,64,1024]{2,1,0:T(8,128)(2,1)S(1)} %copy-done.1), channel_id=1, source_target_pairs={{0,16},{1,17},{2,18},{3,19},{4,20},{5,21},{6,22},{7,23},{8,24},{9,... | collective-permute-start | bytes 786440 | tf_op jit(solution)/shard_map/ppermute | solution.py:57
  15.2 1.5 %collective-permute-start.14 = (bf16[2,64,1024]{2,1,0:T(8,128)(2,1)}, bf16[2,64,1024]{2,1,0:T(8,128)(2,1)S(1)}, u32[]{:S(2)}, u32[]{:S(2)}) collective-permute-start(bf16[2,64,1024]{2,1,0:T(8,128)(2,1)} %get-tuple-element.59), channel_id=1, source_target_pairs={{0,2},{1,3},{2,0},{3,1},{4,6},{5,7},{6,4},{7,5},{8,10},{9,11},{10,... | collective-permute-start | bytes 786440 | tf_op jit(solution)/shard_map/ppermute | solution.py:51
  17.3 1.2 %collective-permute-done.2.line3 = bf16[2,2,128,128]{3,2,1,0:T(8,128)(2,1)S(1)} collective-permute-done((bf16[2,2,128,128]{3,2,1,0:T(8,128)(2,1)S(1)}, bf16[2,2,128,128]{3,2,1,0:T(8,128)(2,1)S(1)}, u32[]{:S(2)}, u32[]{:S(2)}) %collective-permute-start.2) | collective-permute-done | bytes 131104 | tf_op jit(solution)/shard_map/ppermute | solution.py:51
  18.5 1.6 %collective-permute-done.3.near_x = bf16[2,64,1024]{2,1,0:T(8,128)(2,1)S(1)} collective-permute-done((bf16[2,64,1024]{2,1,0:T(8,128)(2,1)S(1)}, bf16[2,64,1024]{2,1,0:T(8,128)(2,1)S(1)}, u32[]{:S(2)}, u32[]{:S(2)}) %collective-permute-start.3) | collective-permute-done | bytes 262176 | tf_op jit(solution)/shard_map/ppermute | solution.py:57
  20.3 4.4 %collective-permute-done.14.peer_x = bf16[2,64,1024]{2,1,0:T(8,128)(2,1)S(1)} collective-permute-done((bf16[2,64,1024]{2,1,0:T(8,128)(2,1)}, bf16[2,64,1024]{2,1,0:T(8,128)(2,1)S(1)}, u32[]{:S(2)}, u32[]{:S(2)}) %collective-permute-start.14) | collective-permute-done | bytes 262176 | tf_op jit(solution)/shard_map/ppermute | solution.py:51
  28.6 1.6 %collective-permute-start.11 = (bf16[2,64,128]{2,1,0:T(8,128)(2,1)S(1)}, bf16[2,64,128]{2,1,0:T(8,128)(2,1)S(1)}, u32[]{:S(2)}, u32[]{:S(2)}) collective-permute-start(bf16[2,64,128]{2,1,0:T(8,128)(2,1)S(1)} %get-tuple-element.56.act), channel_id=1, source_target_pairs={{0,16},{1,17},{2,18},{3,19},{4,20},{5,21},{6,22},{7,23},{8,24},{9,... | collective-permute-start | bytes 98312 | tf_op jit(solution)/shard_map/ppermute | solution.py:57
  30.1 1.5 %collective-permute-start.10 = (bf16[2,64,128]{2,1,0:T(8,128)(2,1)S(1)}, bf16[2,64,128]{2,1,0:T(8,128)(2,1)S(1)}, u32[]{:S(2)}, u32[]{:S(2)}) collective-permute-start(bf16[2,64,128]{2,1,0:T(8,128)(2,1)S(1)} %get-tuple-element.56.act), channel_id=1, source_target_pairs={{0,2},{1,3},{2,0},{3,1},{4,6},{5,7},{6,4},{7,5},{8,10},{9,11},{10,... | collective-permute-start | bytes 98312 | tf_op jit(solution)/shard_map/ppermute | solution.py:51
  32.6 1.5 %collective-permute-done.10.act_y = bf16[2,64,128]{2,1,0:T(8,128)(2,1)S(1)} collective-permute-done((bf16[2,64,128]{2,1,0:T(8,128)(2,1)S(1)}, bf16[2,64,128]{2,1,0:T(8,128)(2,1)S(1)}, u32[]{:S(2)}, u32[]{:S(2)}) %collective-permute-start.10) | collective-permute-done | bytes 32800 | tf_op jit(solution)/shard_map/ppermute | solution.py:51
  34.0 2.4 %collective-permute-done.12.act_d = bf16[2,64,128]{2,1,0:T(8,128)(2,1)S(1)} collective-permute-done((bf16[2,64,128]{2,1,0:T(8,128)(2,1)S(1)}, bf16[2,64,128]{2,1,0:T(8,128)(2,1)S(1)}, u32[]{:S(2)}, u32[]{:S(2)}) %collective-permute-start.12) | collective-permute-done | bytes 32800 | tf_op jit(solution)/shard_map/ppermute | solution.py:57
  37.2 1.5 %collective-permute-done.16.got = bf16[4,2,128,128]{3,2,1,0:T(8,128)(2,1)S(1)} collective-permute-done((bf16[4,2,128,128]{3,2,1,0:T(8,128)(2,1)S(1)}, bf16[4,2,128,128]{3,2,1,0:T(8,128)(2,1)S(1)}, u32[]{:S(2)}, u32[]{:S(2)}) %collective-permute-start.16) | collective-permute-done | bytes 262176 | tf_op jit(solution)/shard_map/ppermute | solution.py:51
  40.7 2.6 %collective-permute-start.19 = (bf16[2,128,128]{2,1,0:T(8,128)(2,1)S(1)}, bf16[2,128,128]{2,1,0:T(8,128)(2,1)S(1)}, u32[]{:S(2)}, u32[]{:S(2)}) collective-permute-start(bf16[2,128,128]{2,1,0:T(8,128)(2,1)S(1)} %get-tuple-element.66), channel_id=1, source_target_pairs={{0,12},{1,13},{2,14},{3,15},{4,8},{5,9},{6,10},{7,11},{8,4},{9,5},... | collective-permute-start | bytes 196616 | tf_op jit(solution)/shard_map/ppermute | solution.py:51
  43.3 4.7 %collective-permute-done.18.g2 = bf16[2,128,128]{2,1,0:T(8,128)(2,1)S(1)} collective-permute-done((bf16[2,128,128]{2,1,0:T(8,128)(2,1)S(1)}, bf16[2,128,128]{2,1,0:T(8,128)(2,1)S(1)}, u32[]{:S(2)}, u32[]{:S(2)}) %collective-permute-start.18) | collective-permute-done | bytes 65568 | tf_op jit(solution)/shard_map/ppermute | solution.py:51
  48.1 1.6 %collective-permute-start.20 = (bf16[2,128,128]{2,1,0:T(8,128)(2,1)S(1)}, bf16[2,128,128]{2,1,0:T(8,128)(2,1)S(1)}, u32[]{:S(2)}, u32[]{:S(2)}) collective-permute-start(bf16[2,128,128]{2,1,0:T(8,128)(2,1)S(1)} %misfit.1.one.own), channel_id=1, source_target_pairs={{0,4},{1,5},{2,6},{3,7},{4,0},{5,1},{6,2},{7,3},{8,12},{9,13},{10,... | collective-permute-start | bytes 196616 | tf_op jit(solution)/shard_map/ppermute | solution.py:51
  50.1 2.4 %collective-permute-start.23 = (bf16[2,128,128]{2,1,0:T(8,128)(2,1)S(1)}, bf16[2,128,128]{2,1,0:T(8,128)(2,1)S(1)}, u32[]{:S(2)}, u32[]{:S(2)}) collective-permute-start(bf16[2,128,128]{2,1,0:T(8,128)(2,1)S(1)} %misfit.1.one.own), channel_id=1, source_target_pairs={{0,12},{1,13},{2,14},{3,15},{4,8},{5,9},{6,10},{7,11},{8,4},{9,5},... | collective-permute-start | bytes 196616 | tf_op jit(solution)/shard_map/ppermute | solution.py:51
  53.1 4.2 %collective-permute-done.22.line2 = bf16[2,128,128]{2,1,0:T(8,128)(2,1)S(1)} collective-permute-done((bf16[2,128,128]{2,1,0:T(8,128)(2,1)S(1)}, bf16[2,128,128]{2,1,0:T(8,128)(2,1)S(1)}, u32[]{:S(2)}, u32[]{:S(2)}) %collective-permute-start.22) | collective-permute-done | bytes 65568 | tf_op jit(solution)/shard_map/ppermute | solution.py:51
  58.6 2.4 %collective-permute-start.31 = (bf16[4,128,128]{2,1,0:T(8,128)(2,1)S(1)}, bf16[4,128,128]{2,1,0:T(8,128)(2,1)S(1)}, u32[]{:S(2)}, u32[]{:S(2)}) collective-permute-start(bf16[4,128,128]{2,1,0:T(8,128)(2,1)S(1)} %get-tuple-element.81), channel_id=1, source_target_pairs={{0,18},{1,19},{2,16},{3,17},{4,22},{5,23},{6,20},{7,21},{8,26},{9,... | collective-permute-start | bytes 393224 | tf_op jit(solution)/shard_map/ppermute | solution.py:57
  63.5 2.0 %collective-permute-start.28 = (bf16[144,128]{1,0:T(8,128)(2,1)S(1)}, bf16[144,128]{1,0:T(8,128)(2,1)S(1)}, u32[]{:S(2)}, u32[]{:S(2)}) collective-permute-start(bf16[144,128]{1,0:T(8,128)(2,1)S(1)} %get-tuple-element.73), channel_id=1, source_target_pairs={{0,18},{1,19},{2,16},{3,17},{4,22},{5,23},{6,20},{7,21},{8,26},{9,... | collective-permute-start | bytes 110600 | tf_op jit(solution)/shard_map/ppermute | solution.py:57
  65.5 2.6 %collective-permute-done.31.d_own = bf16[4,128,128]{2,1,0:T(8,128)(2,1)S(1)} collective-permute-done((bf16[4,128,128]{2,1,0:T(8,128)(2,1)S(1)}, bf16[4,128,128]{2,1,0:T(8,128)(2,1)S(1)}, u32[]{:S(2)}, u32[]{:S(2)}) %collective-permute-start.31) | collective-permute-done | bytes 131104 | tf_op jit(solution)/shard_map/ppermute | solution.py:57
  70.9 1.7 %decoder_grad.1 = (bf16[2,64,2048]{2,1,0:T(8,128)(2,1)}, bf16[1,64,2048]{2,1,0:T(8,128)(2,1)}, bf16[1,2,64,2048]{3,2,1,0:T(8,128)(2,1)}) custom-call(bf16[2,64,128]{2,1,0:T(8,128)(2,1)S(1)} %get-tuple-element.56.act, bf16[2,64,128]{2,1,0:T(8,128)(2,1)S(1)} %collective-permute-done.11.act_x, bf16[2,128,1024]{2,1,0:T(8,128)(2,1)S(1)} %get-tuple-element.79.half, ...), custom_call_target="tpu_custom_call" | custom-call | tf_op jit(solution)/shard_map/decoder_grad/pallas_call | solution.py:350
  (77 shorter events, 16.9 us)
Async XLA Ops:
  0.6 8.0 %collective-permute-start = (bf16[2,128,128]{2,1,0:T(8,128)(2,1)}, bf16[2,128,128]{2,1,0:T(8,128)(2,1)S(1)}, u32[]{:S(2)}, u32[]{:S(2)}) collective-permute-start(bf16[2,128,128]{2,1,0:T(8,128)(2,1)} %own.1), channel_id=1, source_target_pairs={{0,2},{1,3},{2,0},{3,1},{4,6},{5,7},{6,4},{7,5},{8,10},{9,11},{10,... | collective-permute-start | bytes 196616 | tf_op jit(solution)/shard_map/ppermute | solution.py:51
  3.7 5.7 %collective-permute-start.4 = (bf16[2,128,128]{2,1,0:T(8,128)(2,1)}, bf16[2,128,128]{2,1,0:T(8,128)(2,1)S(1)}, u32[]{:S(2)}, u32[]{:S(2)}) collective-permute-start(bf16[2,128,128]{2,1,0:T(8,128)(2,1)} %own.1), channel_id=1, source_target_pairs={{0,8},{1,9},{2,10},{3,11},{4,12},{5,13},{6,14},{7,15},{8,0},{9,1},... | collective-permute-start | bytes 196616 | tf_op jit(solution)/shard_map/ppermute | solution.py:51
  9.4 7.4 %collective-permute-start.5 = (bf16[2,128,128]{2,1,0:T(8,128)(2,1)S(1)}, bf16[2,128,128]{2,1,0:T(8,128)(2,1)S(1)}, u32[]{:S(2)}, u32[]{:S(2)}) collective-permute-start(bf16[2,128,128]{2,1,0:T(8,128)(2,1)S(1)} %collective-permute-done.4.refs_2_), channel_id=1, source_target_pairs={{0,2},{1,3},{2,0},{3,1},{4,6},{5,7},{6,4},{7,5},{8,10},{9,11},{10,... | collective-permute-start | bytes 196616 | tf_op jit(solution)/shard_map/ppermute | solution.py:51
  9.9 7.4 %collective-permute-start.1 = (bf16[2,2,128,128]{3,2,1,0:T(8,128)(2,1)S(1)}, bf16[2,2,128,128]{3,2,1,0:T(8,128)(2,1)S(1)}, u32[]{:S(2)}, u32[]{:S(2)}) collective-permute-start(bf16[2,2,128,128]{3,2,1,0:T(8,128)(2,1)S(1)} %pair.1.refs_0_), channel_id=1, source_target_pairs={{0,4},{1,5},{2,6},{3,7},{4,0},{5,1},{6,2},{7,3},{8,12},{9,13},{10,... | collective-permute-start | bytes 393224 | tf_op jit(solution)/shard_map/ppermute | solution.py:51
  11.1 7.4 %collective-permute-start.2 = (bf16[2,2,128,128]{3,2,1,0:T(8,128)(2,1)S(1)}, bf16[2,2,128,128]{3,2,1,0:T(8,128)(2,1)S(1)}, u32[]{:S(2)}, u32[]{:S(2)}) collective-permute-start(bf16[2,2,128,128]{3,2,1,0:T(8,128)(2,1)S(1)} %pair.1.refs_0_), channel_id=1, source_target_pairs={{0,12},{1,13},{2,14},{3,15},{4,8},{5,9},{6,10},{7,11},{8,4},{9,5},... | collective-permute-start | bytes 393224 | tf_op jit(solution)/shard_map/ppermute | solution.py:51
  13.8 6.4 %collective-permute-start.3 = (bf16[2,64,1024]{2,1,0:T(8,128)(2,1)S(1)}, bf16[2,64,1024]{2,1,0:T(8,128)(2,1)S(1)}, u32[]{:S(2)}, u32[]{:S(2)}) collective-permute-start(bf16[2,64,1024]{2,1,0:T(8,128)(2,1)S(1)} %copy-done.1), channel_id=1, source_target_pairs={{0,16},{1,17},{2,18},{3,19},{4,20},{5,21},{6,22},{7,23},{8,24},{9,... | collective-permute-start | bytes 786440 | tf_op jit(solution)/shard_map/ppermute | solution.py:57
  15.2 9.5 %collective-permute-start.14 = (bf16[2,64,1024]{2,1,0:T(8,128)(2,1)}, bf16[2,64,1024]{2,1,0:T(8,128)(2,1)S(1)}, u32[]{:S(2)}, u32[]{:S(2)}) collective-permute-start(bf16[2,64,1024]{2,1,0:T(8,128)(2,1)} %get-tuple-element.59), channel_id=1, source_target_pairs={{0,2},{1,3},{2,0},{3,1},{4,6},{5,7},{6,4},{7,5},{8,10},{9,11},{10,... | collective-permute-start | bytes 786440 | tf_op jit(solution)/shard_map/ppermute | solution.py:51
  16.8 15.4 %collective-permute-start.13 = (bf16[3,64,1024]{2,1,0:T(8,128)(2,1)}, bf16[3,64,1024]{2,1,0:T(8,128)(2,1)S(1)}, u32[]{:S(2)}, u32[]{:S(2)}) collective-permute-start(bf16[3,64,1024]{2,1,0:T(8,128)(2,1)} %get-tuple-element.58), channel_id=1, source_target_pairs={{0,2},{1,3},{2,0},{3,1},{4,6},{5,7},{6,4},{7,5},{8,10},{9,11},{10,... | collective-permute-start | bytes 1179656 | tf_op jit(solution)/shard_map/ppermute | solution.py:51
  20.3 7.5 %collective-permute-start.7 = (bf16[2,2,2,128,128]{4,3,2,1,0:T(8,128)(2,1)S(1)}, bf16[2,2,2,128,128]{4,3,2,1,0:T(8,128)(2,1)S(1)}, u32[]{:S(2)}, u32[]{:S(2)}) collective-permute-start(bf16[2,2,2,128,128]{4,3,2,1,0:T(8,128)(2,1)S(1)} %relay.1.refs_1_), channel_id=1, source_target_pairs={{0,1},{1,0},{2,3},{3,2},{4,5},{5,4},{6,7},{7,6},{8,9},{9,8},{10,11... | collective-permute-start | bytes 786440 | tf_op jit(solution)/shard_map/ppermute | solution.py:51
  24.7 7.4 %collective-permute-start.15 = (bf16[2,64,1024]{2,1,0:T(8,128)(2,1)S(1)}, bf16[2,64,1024]{2,1,0:T(8,128)(2,1)S(1)}, u32[]{:S(2)}, u32[]{:S(2)}) collective-permute-start(bf16[2,64,1024]{2,1,0:T(8,128)(2,1)S(1)} %collective-permute-done.14.peer_x), channel_id=1, source_target_pairs={{0,16},{1,17},{2,18},{3,19},{4,20},{5,21},{6,22},{7,23},{8,24},{9,... | collective-permute-start | bytes 786440 | tf_op jit(solution)/shard_map/ppermute | solution.py:57
  31.7 4.8 %collective-permute-start.12 = (bf16[2,64,128]{2,1,0:T(8,128)(2,1)S(1)}, bf16[2,64,128]{2,1,0:T(8,128)(2,1)S(1)}, u32[]{:S(2)}, u32[]{:S(2)}) collective-permute-start(bf16[2,64,128]{2,1,0:T(8,128)(2,1)S(1)} %get-tuple-element.56.act), channel_id=1, source_target_pairs={{0,18},{1,19},{2,16},{3,17},{4,22},{5,23},{6,20},{7,21},{8,26},{9,... | collective-permute-start | bytes 98312 | tf_op jit(solution)/shard_map/ppermute | solution.py:57
  40.0 8.0 %collective-permute-start.18 = (bf16[2,128,128]{2,1,0:T(8,128)(2,1)S(1)}, bf16[2,128,128]{2,1,0:T(8,128)(2,1)S(1)}, u32[]{:S(2)}, u32[]{:S(2)}) collective-permute-start(bf16[2,128,128]{2,1,0:T(8,128)(2,1)S(1)} %get-tuple-element.65), channel_id=1, source_target_pairs={{0,8},{1,9},{2,10},{3,11},{4,12},{5,13},{6,14},{7,15},{8,0},{9,1},... | collective-permute-start | bytes 196616 | tf_op jit(solution)/shard_map/ppermute | solution.py:51
  40.7 7.4 %collective-permute-start.19 = (bf16[2,128,128]{2,1,0:T(8,128)(2,1)S(1)}, bf16[2,128,128]{2,1,0:T(8,128)(2,1)S(1)}, u32[]{:S(2)}, u32[]{:S(2)}) collective-permute-start(bf16[2,128,128]{2,1,0:T(8,128)(2,1)S(1)} %get-tuple-element.66), channel_id=1, source_target_pairs={{0,12},{1,13},{2,14},{3,15},{4,8},{5,9},{6,10},{7,11},{8,4},{9,5},... | collective-permute-start | bytes 196616 | tf_op jit(solution)/shard_map/ppermute | solution.py:51
  49.6 7.7 %collective-permute-start.22 = (bf16[2,128,128]{2,1,0:T(8,128)(2,1)S(1)}, bf16[2,128,128]{2,1,0:T(8,128)(2,1)S(1)}, u32[]{:S(2)}, u32[]{:S(2)}) collective-permute-start(bf16[2,128,128]{2,1,0:T(8,128)(2,1)S(1)} %misfit.1.one.own), channel_id=1, source_target_pairs={{0,8},{1,9},{2,10},{3,11},{4,12},{5,13},{6,14},{7,15},{8,0},{9,1},... | collective-permute-start | bytes 196616 | tf_op jit(solution)/shard_map/ppermute | solution.py:51
  50.1 7.2 %collective-permute-start.23 = (bf16[2,128,128]{2,1,0:T(8,128)(2,1)S(1)}, bf16[2,128,128]{2,1,0:T(8,128)(2,1)S(1)}, u32[]{:S(2)}, u32[]{:S(2)}) collective-permute-start(bf16[2,128,128]{2,1,0:T(8,128)(2,1)S(1)} %misfit.1.one.own), channel_id=1, source_target_pairs={{0,12},{1,13},{2,14},{3,15},{4,8},{5,9},{6,10},{7,11},{8,4},{9,5},... | collective-permute-start | bytes 196616 | tf_op jit(solution)/shard_map/ppermute | solution.py:51
  52.5 5.0 %collective-permute-start.24 = (bf16[2,2,128,128]{3,2,1,0:T(8,128)(2,1)S(1)}, bf16[2,2,128,128]{3,2,1,0:T(8,128)(2,1)S(1)}, u32[]{:S(2)}, u32[]{:S(2)}) collective-permute-start(bf16[2,2,128,128]{3,2,1,0:T(8,128)(2,1)S(1)} %row.1.near), channel_id=1, source_target_pairs={{0,2},{1,3},{2,0},{3,1},{4,6},{5,7},{6,4},{7,5},{8,10},{9,11},{10,... | collective-permute-start | bytes 393224 | tf_op jit(solution)/shard_map/ppermute | solution.py:51
  53.1 8.0 %collective-permute-start.21 = (bf16[2,2,128,128]{3,2,1,0:T(8,128)(2,1)S(1)}, bf16[2,2,128,128]{3,2,1,0:T(8,128)(2,1)S(1)}, u32[]{:S(2)}, u32[]{:S(2)}) collective-permute-start(bf16[2,2,128,128]{3,2,1,0:T(8,128)(2,1)S(1)} %row.1.near), channel_id=1, source_target_pairs={{0,1},{1,0},{2,3},{3,2},{4,5},{5,4},{6,7},{7,6},{8,9},{9,8},{10,11... | collective-permute-start | bytes 393224 | tf_op jit(solution)/shard_map/ppermute | solution.py:51
  57.6 5.9 %collective-permute-start.29 = (bf16[2,2,128,128]{3,2,1,0:T(8,128)(2,1)S(1)}, bf16[2,2,128,128]{3,2,1,0:T(8,128)(2,1)S(1)}, u32[]{:S(2)}, u32[]{:S(2)}) collective-permute-start(bf16[2,2,128,128]{3,2,1,0:T(8,128)(2,1)S(1)} %get-tuple-element.69.last), channel_id=1, source_target_pairs={{0,2},{1,3},{2,0},{3,1},{4,6},{5,7},{6,4},{7,5},{8,10},{9,11},{10,... | collective-permute-start | bytes 393224 | tf_op jit(solution)/shard_map/ppermute | solution.py:51
  58.1 7.5 %collective-permute-start.30 = (bf16[4,128,128]{2,1,0:T(8,128)(2,1)S(1)}, bf16[4,128,128]{2,1,0:T(8,128)(2,1)S(1)}, u32[]{:S(2)}, u32[]{:S(2)}) collective-permute-start(bf16[4,128,128]{2,1,0:T(8,128)(2,1)S(1)} %get-tuple-element.81), channel_id=1, source_target_pairs={{0,16},{1,17},{2,18},{3,19},{4,20},{5,21},{6,22},{7,23},{8,24},{9,... | collective-permute-start | bytes 393224 | tf_op jit(solution)/shard_map/ppermute | solution.py:57
  58.6 9.6 %collective-permute-start.31 = (bf16[4,128,128]{2,1,0:T(8,128)(2,1)S(1)}, bf16[4,128,128]{2,1,0:T(8,128)(2,1)S(1)}, u32[]{:S(2)}, u32[]{:S(2)}) collective-permute-start(bf16[4,128,128]{2,1,0:T(8,128)(2,1)S(1)} %get-tuple-element.81), channel_id=1, source_target_pairs={{0,18},{1,19},{2,16},{3,17},{4,22},{5,23},{6,20},{7,21},{8,26},{9,... | collective-permute-start | bytes 393224 | tf_op jit(solution)/shard_map/ppermute | solution.py:57
  62.0 6.2 %collective-permute-start.26 = (bf16[144,128]{1,0:T(8,128)(2,1)S(1)}, bf16[144,128]{1,0:T(8,128)(2,1)S(1)}, u32[]{:S(2)}, u32[]{:S(2)}) collective-permute-start(bf16[144,128]{1,0:T(8,128)(2,1)S(1)} %get-tuple-element.71), channel_id=1, source_target_pairs={{0,2},{1,3},{2,0},{3,1},{4,6},{5,7},{6,4},{7,5},{8,10},{9,11},{10,... | collective-permute-start | bytes 110600 | tf_op jit(solution)/shard_map/ppermute | solution.py:51
  62.5 5.6 %collective-permute-start.27 = (bf16[144,128]{1,0:T(8,128)(2,1)S(1)}, bf16[144,128]{1,0:T(8,128)(2,1)S(1)}, u32[]{:S(2)}, u32[]{:S(2)}) collective-permute-start(bf16[144,128]{1,0:T(8,128)(2,1)S(1)} %get-tuple-element.72), channel_id=1, source_target_pairs={{0,16},{1,17},{2,18},{3,19},{4,20},{5,21},{6,22},{7,23},{8,24},{9,... | collective-permute-start | bytes 110600 | tf_op jit(solution)/shard_map/ppermute | solution.py:57
  63.5 5.6 %collective-permute-start.28 = (bf16[144,128]{1,0:T(8,128)(2,1)S(1)}, bf16[144,128]{1,0:T(8,128)(2,1)S(1)}, u32[]{:S(2)}, u32[]{:S(2)}) collective-permute-start(bf16[144,128]{1,0:T(8,128)(2,1)S(1)} %get-tuple-element.73), channel_id=1, source_target_pairs={{0,18},{1,19},{2,16},{3,17},{4,22},{5,23},{6,20},{7,21},{8,26},{9,... | collective-permute-start | bytes 110600 | tf_op jit(solution)/shard_map/ppermute | solution.py:57
  65.5 5.1 %collective-permute-start.32 = (bf16[2,2,128,128]{3,2,1,0:T(8,128)(2,1)S(1)}, bf16[2,2,128,128]{3,2,1,0:T(8,128)(2,1)S(1)}, u32[]{:S(2)}, u32[]{:S(2)}) collective-permute-start(bf16[2,2,128,128]{3,2,1,0:T(8,128)(2,1)S(1)} %collective-permute-done.24.far), channel_id=1, source_target_pairs={{0,1},{1,0},{2,3},{3,2},{4,5},{5,4},{6,7},{7,6},{8,9},{9,8},{10,11... | collective-permute-start | bytes 393224 | tf_op jit(solution)/shard_map/ppermute | solution.py:51
  (19 other events, 78.3 us)
